TPU v7x, 256 devices: a whole 4x4x8 slice. The times are simulated.
256 devices in a mesh: row: 16 (over z_hi, x, core), grp: 16 (over y, z_lo).
Axes of the slice: x: 4, y: 4, z: 8 (z_hi: 2, z_lo: 4; z = z_hi * 4 + z_lo), core: 2. Of those that a mesh axis runs over, the one named last changes fastest.
Arguments:
- view_x: bfloat16 [65536, 1024], P(('row', 'grp')), may hold values from -64 to 64
- view_y: bfloat16 [65536, 1024], P(('row', 'grp')), may hold values from -64 to 64
Outputs:
- coherence: float32 [1024, 1024], P(('row', 'grp'))
All inputs are finite; a program needn't handle non-finite values.
Results may differ from a plain program's by a relative error of at most 0.0003.
Values sent between devices are 32-bit elements; how exact they have to be, the bound alone decides.
No kernel may reach another device: no remote copies, remote signals or barrier semaphores. Data moves between devices by JAX's collectives and lax.ppermute only.
A program may use at most 128 MiB of HBM per device.

v0:
```python
import jax
import jax.numpy as jnp
from jax import lax
from jax.sharding import PartitionSpec as P


def gram_of(left, right):
    return lax.dot_general(
        left, right, (((0,), (0,)), ((), ())), preferred_element_type=jnp.float32
    )


def on_device(view_x, view_y):
    width = view_x.shape[1]
    owned = width // (lax.axis_size("row") * lax.axis_size("grp"))
    own_start = lax.axis_index(("row", "grp")) * owned
    local_x = gram_of(view_x, view_x)
    local_y = gram_of(view_y, view_y)
    summed_first, summed_second = lax.psum((local_x, local_y), ("row", "grp"))
    cross = lax.psum_scatter(
        gram_of(view_x, view_y), ("row", "grp"), scatter_dimension=0, tiled=True
    )
    lower_x = jnp.linalg.cholesky(summed_first)
    lower_y = jnp.linalg.cholesky(summed_second)
    whiten = jax.scipy.linalg.solve_triangular(lower_y, cross.T, lower=True).T
    picker = (
        jnp.arange(width, dtype=jnp.int32)[:, None]
        == own_start + jnp.arange(owned, dtype=jnp.int32)[None, :]
    ).astype(jnp.float32)
    inverse_rows = jax.scipy.linalg.solve_triangular(lower_x, picker, lower=True, trans="T").T
    return jnp.dot(
        inverse_rows,
        lax.all_gather(whiten, ("row", "grp"), axis=0, tiled=True),
        precision=lax.Precision.HIGHEST,
        preferred_element_type=jnp.float32,
    )


def solution(mesh):
    in_specs = (P(("row", "grp"), None), P(("row", "grp"), None))
    out_specs = P(("row", "grp"), None)
    return jax.shard_map(
        on_device, mesh=mesh, in_specs=in_specs, out_specs=out_specs, check_vma=False
    )
```

profile of v0, /device:TPU:1, one launch (start us, length us, event | category | flops | bytes accessed | tf_op | source)
XLA Modules:
  0.0 1381.5 jit_solution(10510566932308907382)
XLA Ops:
  15.9 290.3 %all-reduce.5.cloned.1.call-done = (f32[1024,1024]{0,1:T(8,128)}, f32[1024,1024]{0,1:T(8,128)}, f32[1024,1024]{1,0:T(8,128)}) async-done(((f32[1024,1024]{0,1:T(8,128)}, f32[1024,1024]{0,1:T(8,128)}, f32[1024,1024]{1,0:T(8,128)}), (f32[1024,1024]{0,1:T(8,128)}, f32[1024,1024]{0,1:T(8,128)}, f32[1024,1024]{1,0:T(8,128)})) %all-reduce.5.cloned.1.call-update) | async-done | bytes 12582928 | tf_op jit(solution)/shard_map/psum | solution.py:19
  317.4 10.3 fusion
  329.7 11.7 cholesky.767
  341.5 9.8 custom-call.68
  357.7 11.9 cholesky.786
  370.2 9.8 custom-call.69
  383.4 11.7 cholesky.807
  411.4 11.7 cholesky.826
  424.4 9.8 custom-call.71
  437.7 11.7 cholesky.845
  450.8 10.2 custom-call.72
  464.3 11.7 cholesky.864
  490.1 11.9 cholesky.883
  515.7 11.7 cholesky.900
  538.7 22.9 %while.3 = (s32[]{:T(128)}, f32[1024,1024]{1,0:T(8,128)}, s32[8,2]{0,1:T(2,128)S(1)}, f32[8,128,128]{2,1,0:T(8,128)S(1)}, s32[]{:T(128)}) while((s32[]{:T(128)}, f32[1024,1024]{1,0:T(8,128)}, s32[8,2]{0,1:T(2,128)S(1)}, f32[8,128,128]{2,1,0:T(8,128)S(1)}, s32[]{:T(128)}) %tuple.94), condition=%wide.while_cond.1, body=%wide.while_body.1.sunk | while | flops 2 | bytes 131181 | solution.py:25
  561.6 78.8 %custom-call.53 = f32[8,128,128]{1,2,0:T(8,128)S(1)} custom-call(f32[8,128,128]{2,1,0:T(8,128)S(1)} %get-tuple-element.21), custom_call_target="InvertDiagBlocksLowerTriangular" | custom-call | tf_op jit(solution)/shard_map/jit(_solve_triangular)/triangular_solve | solution.py:25
  653.2 11.7 cholesky.619
  664.9 9.8 custom-call.61
  681.1 12.1 cholesky.638
  693.9 9.8 custom-call.62
  707.1 11.7 cholesky.659
  734.8 11.9 cholesky.678
  761.2 11.7 cholesky.697
  774.2 10.0 custom-call.65
  787.5 11.7 cholesky.716
  800.6 9.8 custom-call.66
  813.4 12.1 cholesky.735
  826.8 9.8 custom-call.67
  839.3 11.7 cholesky.752
  862.1 22.5 %while.2 = (s32[]{:T(128)}, f32[1024,1024]{1,0:T(8,128)}, s32[8,2]{0,1:T(2,128)S(1)}, f32[8,128,128]{2,1,0:T(8,128)S(1)}, s32[]{:T(128)}) while((s32[]{:T(128)}, f32[1024,1024]{1,0:T(8,128)}, s32[8,2]{0,1:T(2,128)S(1)}, f32[8,128,128]{2,1,0:T(8,128)S(1)}, s32[]{:T(128)}) %tuple.102), condition=%wide.while_cond, body=%wide.while_body.sunk | while | flops 2 | bytes 131181 | solution.py:30
  884.6 78.8 %custom-call.52 = f32[8,128,128]{1,2,0:T(8,128)S(1)} custom-call(f32[8,128,128]{2,1,0:T(8,128)S(1)} %get-tuple-element.13), custom_call_target="InvertDiagBlocksLowerTriangular" | custom-call | tf_op jit(solution)/shard_map/jit(_solve_triangular)/triangular_solve | solution.py:30
  976.3 387.9 %all-gather.3.cloned.1.call-done = f32[256,4,1024]{2,1,0:T(4,128)} async-done(((f32[1,4,1024]{2,1,0:T(4,128)}), f32[256,4,1024]{2,1,0:T(4,128)}) %all-gather.3.cloned.1.call-update) | async-done | bytes 4194320 | tf_op jit(solution)/shard_map/all_gather | solution.py:33
  (211 shorter events, 233.5 us)
Async XLA Ops:
  6.5 1.0 copy-start
  6.5 3.8 copy-start.3
  6.5 299.7 %all-reduce.5.cloned.1.call-start = ((), (), s32[]{:S(2)}) async-start(), calls=%async_computation.1 | async-start | bytes 25165824 | tf_op jit(solution)/shard_map/psum | solution.py:19
  15.7 1348.5 %all-gather.3.cloned.1.call-start = ((), (), s32[]{:S(2)}) async-start(), calls=%async_computation | async-start | bytes 4210688 | tf_op jit(solution)/shard_map/all_gather | solution.py:33
  327.7 2.0 copy-start.2
  651.7 0.6 copy-start.4
  1364.2 10.2 copy-start.1
Sparse Core Ops, SparseCore 0:
  15.8 290.3 all-reduce.4
  652.4 711.7 all-gather.2
where the time goes:
time: 1390 us; the launch traced here: 1380 us
  waiting for transfers between devices  678 us (49%)
  other arithmetic  524 us (38%)
  matrix products  82.5 us (6%)
  local copies, waits for them, and re-layouts  72.2 us (5%)
  between operations  24.1 us (2%)
    all_gather x1, waiting for transfers between devices, on_device(): lax.all_gather(whiten, ('row', 'grp'), axis=0, tiled=True)  388 us
    psum x1, waiting for transfers between devices, on_device(): summed_first, summed_second = lax.psum((local_x, local_y), ('row', 'grp'))  290 us
    another operation x31, other arithmetic, on_device(): lower_x = jnp.linalg.cholesky(summed_first)  173 us
    another operation x31, other arithmetic, on_device(): lower_y = jnp.linalg.cholesky(summed_second)  173 us
    another operation x2, other arithmetic, on_device(): whiten = jax.scipy.linalg.solve_triangular(lower_y, cross.T, lower=True).T  83.6 us
    another operation x3, other arithmetic, on_device(): jax.scipy.linalg.solve_triangular(lower_x, picker, lower=True, trans='T')  83.6 us
    another operation x48, local copies, waits for them, and re-layouts  45.1 us
  transfers between devices with their start and end apart: 2, of which 2 were waited for; matrix products, arithmetic and copies ran while one was open for 23% of the time, Pallas kernels for 0%

commit v1 on v0

v1 whole, which is shorter than its diff:
```python
import functools

import jax
import jax.numpy as jnp
from jax import lax
from jax.experimental import pallas as pl
from jax.experimental.pallas import tpu as pltpu
from jax.sharding import Mesh
from jax.sharding import PartitionSpec as P

AXES = ("z_hi", "x", "core", "y", "z_lo")
SIZES = (2, 4, 2, 4, 4)
PLANE = ("x", "y")
LINE = ("z_hi", "z_lo")
N, NB, SB, G = 1024, 128, 32, 8
KB = N // NB
OWNED = 4
UPPER = [(i, j) for i in range(KB) for j in range(i, KB)]
EARLY, LATE = UPPER[:16], UPPER[16:]
LATE_SLOTS = 24
VMEM = pl.BlockSpec(memory_space=pltpu.VMEM)
SMEM = pl.BlockSpec(memory_space=pltpu.SMEM)


def mm(a, b, dims):
    return lax.dot_general(
        a, b, (dims, ((), ())), precision=lax.Precision.HIGHEST, preferred_element_type=jnp.float32
    )


def call(kernel, outs, n_smem, n_vmem, scratch=(), flops=0, bytes_accessed=0):
    return pl.pallas_call(
        kernel,
        out_shape=[jax.ShapeDtypeStruct(s, jnp.float32) for s in outs],
        in_specs=[SMEM] * n_smem + [VMEM] * n_vmem,
        out_specs=[VMEM] * len(outs),
        scratch_shapes=list(scratch),
        compiler_params=pltpu.CompilerParams(vmem_limit_bytes=40 << 20),
        cost_estimate=pl.CostEstimate(flops=flops, bytes_accessed=bytes_accessed, transcendentals=0),
    )


def gram_kernel(blocks, slots, core, x, y, mine, other, pick):
    for out, which in ((mine, 0), (other, 1)):
        @pl.when(core[0] == which)
        def _():
            pick[...] = x[...]

        @pl.when(core[0] != which)
        def _():
            pick[...] = y[...]

        for i in sorted({i for i, _ in blocks}):
            cols = [j for a, j in blocks if a == i]
            lo, hi = min(cols), max(cols) + 1
            prod = lax.dot_general(
                pick[:, i * NB:(i + 1) * NB], pick[:, lo * NB:hi * NB], (((0,), (0,)), ((), ())),
                preferred_element_type=jnp.float32,
            )
            for j in cols:
                at = blocks.index((i, j))
                out[at * NB:(at + 1) * NB, :] = prod[:, (j - lo) * NB:(j - lo + 1) * NB]
        if slots > len(blocks):
            out[len(blocks) * NB:, :] = jnp.zeros(((slots - len(blocks)) * NB, NB), jnp.float32)


def cross_kernel(core, x, y, mine, other):
    half = N // 2
    for out, which in ((mine, core[0]), (other, 1 - core[0])):
        left = x[:, pl.ds(pl.multiple_of(which * half, half), half)]
        for j in range(KB // 2):
            prod = lax.dot_general(
                left, y[:, 2 * j * NB:2 * (j + 1) * NB], (((0,), (0,)), ((), ())), preferred_element_type=jnp.float32
            )
            for i in range(half // NB):
                for d in range(2):
                    at = i * KB + 2 * j + d
                    out[at * NB:(at + 1) * NB, :] = prod[i * NB:(i + 1) * NB, d * NB:(d + 1) * NB]


def exchange(pieces, axes):
    return lax.all_to_all(pieces, axes, 0, 0, tiled=True)


def spread(piece, n):
    return jnp.broadcast_to(piece[None], (n, *piece.shape))


def sum_of_chips(mine, other, name):
    with jax.named_scope(name):
        rows = mine.shape[0]
        total = mine + lax.ppermute(other, "core", [(0, 1), (1, 0)])
        piece = jnp.sum(exchange(total.reshape(16, rows // 16, NB), PLANE), axis=0)
        part = jnp.sum(exchange(piece.reshape(8, rows // 128, NB), LINE), axis=0)
        piece = exchange(spread(part, 8), LINE).reshape(rows // 16, NB)
        return exchange(spread(piece, 16), PLANE).reshape(rows, NB)


def tile(v):
    return jnp.broadcast_to(v, (G, NB))


def pivots(s):
    l = [[None] * G for _ in range(G)]
    r = [None] * G
    for k in range(G):
        r[k] = lax.rsqrt(s[k][k])
        for j in range(k + 1, G):
            l[j][k] = s[k][j] * r[k]
        for i in range(k + 1, G):
            for j in range(i, G):
                s[i][j] = s[i][j] - l[i][k] * l[j][k]
    return l, r


def forward(l, r, rows):
    out = []
    for k in range(G):
        v = rows[k]
        for j in range(k):
            v = v - l[k][j] * out[j]
        out.append(v * r[k])
    return out


def factor_block(work):
    groups = SB // G
    for top in range(0, NB, SB):
        left = [work[top + G * g:top + G * (g + 1), :NB] for g in range(groups)]
        right = [work[top + G * g:top + G * (g + 1), NB:] for g in range(groups)]
        for p in range(groups):
            c0 = top + G * p
            s = [[tile(left[p][i:i + 1, c0 + j:c0 + j + 1]) if j >= i else None for j in range(G)] for i in range(G)]
            cols = [
                [jnp.broadcast_to(left[q][:, c0 + k:c0 + k + 1], (G, NB)) for k in range(G)]
                for q in range(p + 1, groups)
            ]
            l, r = pivots(s)
            u = forward(l, r, [tile(left[p][i:i + 1, :]) for i in range(G)])
            b = forward(l, r, [tile(right[p][i:i + 1, :]) for i in range(G)])
            for i in range(G):
                work[c0 + i:c0 + i + 1, :NB] = u[i][0:1]
                work[c0 + i:c0 + i + 1, NB:] = b[i][0:1]
            for q in range(p + 1, groups):
                lc = forward(l, r, cols[q - p - 1])
                for k in range(G):
                    left[q] = left[q] - lc[k] * u[k]
                    right[q] = right[q] - lc[k] * b[k]
        rest = top + SB
        if rest < NB:
            rows = work[top:rest, :]
            work[rest:, :] -= mm(rows[:, rest:NB], rows, ((0,), (0,)))


def eliminate(first, last, upto, upper, inverse, work):
    eye = lax.broadcasted_iota(jnp.int32, (NB, NB), 0) == lax.broadcasted_iota(jnp.int32, (NB, NB), 1)

    def step(k, carry):
        at = pl.multiple_of(k * NB, NB)
        work[:, :NB] = upper[pl.ds(at, NB), pl.ds(at, NB)]
        work[:, NB:] = eye.astype(jnp.float32)
        factor_block(work)
        inverse[pl.ds(at, NB), :] = work[:, NB:]
        for kk in range(first, min(last, KB - 1)):
            @pl.when(k == kk)
            def _():
                lo, nxt = kk * NB, (kk + 1) * NB
                upper[lo:nxt, nxt:] = mm(work[:, NB:], upper[lo:nxt, nxt:], ((1,), (0,)))
                for i in range(kk + 1, upto):
                    rows = upper[lo:nxt, i * NB:]
                    upper[i * NB:(i + 1) * NB, i * NB:] -= mm(rows[:, :NB], rows, ((0,), (0,)))
        return carry

    lax.fori_loop(first, last, step, 0)


def early_kernel(blocks, upper, inverse, work):
    for at, (i, j) in enumerate(EARLY[:15]):
        upper[i * NB:(i + 1) * NB, j * NB:(j + 1) * NB] = blocks[at * NB:(at + 1) * NB, :]
    eliminate(0, 2, 2, upper, inverse, work)


def late_kernel(rows, early, late, top, top_inverse, upper, inverse, z, work):
    upper[:2 * NB, :] = top[...]
    inverse[:2 * NB, :] = top_inverse[...]
    upper[2 * NB:3 * NB, 2 * NB:3 * NB] = early[15 * NB:16 * NB, :]
    for at, (i, j) in enumerate(LATE):
        upper[i * NB:(i + 1) * NB, j * NB:(j + 1) * NB] = late[at * NB:(at + 1) * NB, :]
    for i in range(2, KB):
        both = upper[:2 * NB, i * NB:]
        upper[i * NB:(i + 1) * NB, i * NB:] -= mm(both[:, :NB], both, ((0,), (0,)))
    eliminate(2, KB, KB, upper, inverse, work)
    line = lax.broadcasted_iota(jnp.int32, (G, NB), 0)
    want = jnp.where(line < OWNED, rows[0] + line, rows[1] + line - OWNED)
    lane = lax.broadcasted_iota(jnp.int32, (G, NB), 1)
    for k in reversed(range(KB)):
        v = (want == lane + k * NB).astype(jnp.float32)
        if k < KB - 1:
            v = v - mm(z[:, (k + 1) * NB:], upper[k * NB:(k + 1) * NB, (k + 1) * NB:], ((1,), (1,)))
        z[:, k * NB:(k + 1) * NB] = mm(v, inverse[k * NB:(k + 1) * NB, :], ((1,), (0,)))


def apply_kernel(core, z_own, z_sent, cross, out):
    half = N // 2
    z = jnp.where(core[0] == 0, z_own[:, :half], z_sent[:, half:])
    acc = jnp.zeros((G, N), jnp.float32)
    for i in range(half // NB):
        row = jnp.concatenate([cross[(i * KB + j) * NB:(i * KB + j + 1) * NB, :] for j in range(KB)], axis=1)
        acc = acc + mm(z[:, i * NB:(i + 1) * NB], row, ((1,), (0,)))
    out[...] = acc


def solve_kernel(w_own, w_sent, upper, inverse, y):
    w = w_own[...] + w_sent[...]
    for k in range(KB):
        v = w[:, k * NB:(k + 1) * NB]
        if k:
            v = v - mm(y[:, :k * NB], upper[:k * NB, k * NB:(k + 1) * NB], ((1,), (0,)))
        y[:, k * NB:(k + 1) * NB] = mm(v, inverse[k * NB:(k + 1) * NB, :], ((1,), (1,)))


def on_device(view_x, view_y):
    core = lax.axis_index("core")
    core_ref = core.astype(jnp.int32).reshape(1)
    chip = ((lax.axis_index("z_hi") * 4 + lax.axis_index("x")) * 2) * 16 + lax.axis_index("y") * 4 + lax.axis_index("z_lo")
    rows = jnp.stack([chip * OWNED, (chip + 16) * OWNED]).astype(jnp.int32)
    work = pltpu.VMEM((NB, 2 * NB), jnp.float32)
    pick = pltpu.VMEM(view_x.shape, view_x.dtype)

    sums = []
    for blocks, slots, name in ((EARLY, 16, "early"), (LATE, LATE_SLOTS, "late")):
        mine, other = call(
            functools.partial(gram_kernel, blocks, slots), [(slots * NB, NB)] * 2, 1, 2, [pick], flops=10**9
        )(core_ref, view_x, view_y)
        sums.append(sum_of_chips(mine, other, name))
    early, late = sums
    mine, other = call(cross_kernel, [(32 * NB, NB)] * 2, 1, 2, flops=10**9)(core_ref, view_x, view_y)
    cross = sum_of_chips(mine, other, "cross")

    top, top_inverse = call(early_kernel, [(2 * NB, N), (2 * NB, NB)], 0, 1, [work], flops=10**10)(early)
    upper, inverse, z = call(late_kernel, [(N, N), (N, NB), (G, N)], 1, 4, [work], flops=3 * 10**10)(
        rows, early, late, top, top_inverse
    )
    z_sent = lax.ppermute(z, "core", [(0, 1), (1, 0)])
    (w,) = call(apply_kernel, [(G, N)], 1, 3)(core_ref, z, z_sent, cross)
    w_sent = lax.ppermute(w, "core", [(0, 1), (1, 0)])
    (y,) = call(solve_kernel, [(G, N)], 0, 4)(w, w_sent, upper, inverse)
    y_sent = lax.ppermute(y[:OWNED], "core", [(0, 1), (1, 0)])
    return jnp.where(core == 0, y_sent, y[OWNED:])


def solution(mesh):
    fine = Mesh(mesh.devices.reshape(SIZES), AXES)
    spec = P(AXES, None)
    return jax.shard_map(on_device, mesh=fine, in_specs=(spec, spec), out_specs=spec, check_vma=False)
```

time: 1390 us -> 268 us (0.19)
  waiting for transfers between devices: 678 us -> 78.4 us
  other arithmetic: 524 us -> 12.9 us
  matrix products: 82.5 us -> 0 us
  starting transfers between devices: 0.04 us -> 59.5 us
  Pallas kernels: 0 us -> 58 us
  local copies, waits for them, and re-layouts: 72.2 us -> 17.3 us
  blocking collectives: 0 us -> 40.5 us
  between operations: 24.1 us -> 0.18 us
    another operation x67 -> x1, other arithmetic: 514 us -> 0.08 us  [on_device(): rows = jnp.stack([chip * OWNED, (chip + 16) * OWNED]).astype(jnp.int32)]
    all_gather x1 -> x0, waiting for transfers between devices: 388 us -> none  [on_device(): lax.all_gather(whiten, ('row', 'grp'), axis=0, tiled=True)]
    psum x1 -> x0, waiting for transfers between devices: 290 us -> none  [on_device(): summed_first, summed_second = lax.psum((local_x, local_y), ('row', 'grp'))]
    all_to_all x0 -> x10, waiting for transfers between devices: none -> 75.9 us  [exchange(): return lax.all_to_all(pieces, axes, 0, 0, tiled=True)]
    another operation x58 -> x0, matrix products: 69.5 us -> none  [the longest x14 23.3 us: on_device(): lower_y = jnp.linalg.cholesky(summed_second)]
    pallas_call x0 -> x7, Pallas kernels: none -> 58 us  [the longest x1 38.3 us: on_device(): call(late_kernel, [(N, N), (N, NB), (G, N)], 1, 4, [work], flops=3 * 10 *...]
    another operation x69 -> x0, local copies, waits for them, and re-layouts: 51 us -> none
    all_to_all x0 -> x10, starting transfers between devices: none -> 42.8 us  [exchange(): return lax.all_to_all(pieces, axes, 0, 0, tiled=True)]
  transfers between devices with their start and end apart: 2 -> 16, of which waited for: 2 -> 12; matrix products, arithmetic and copies ran while one was open for 23% -> 5% of each run, Pallas kernels for 0% -> 20%
where the time goes in v1:
time: 268 us; the launch traced here: 267 us
  waiting for transfers between devices  78.4 us (29%)
  starting transfers between devices  59.5 us (22%)
  Pallas kernels  58 us (22%)
  blocking collectives  40.5 us (15%)
  local copies, waits for them, and re-layouts  17.3 us (6%)
  other arithmetic  12.9 us (5%)
    all_to_all x10, waiting for transfers between devices, exchange(): return lax.all_to_all(pieces, axes, 0, 0, tiled=True)  75.9 us
    all_to_all x10, starting transfers between devices, exchange(): return lax.all_to_all(pieces, axes, 0, 0, tiled=True)  42.8 us
    all_to_all x2, blocking collectives, exchange(): return lax.all_to_all(pieces, axes, 0, 0, tiled=True)  40.5 us
    pallas_call x1, Pallas kernels, on_device(): call(late_kernel, [(N, N), (N, NB), (G, N)], 1, 4, [work], flops=3 * 10 *...  38.3 us
    unnamed x26, local copies, waits for them, and re-layouts  11.9 us
    ppermute x1, starting transfers between devices, on_device(): z_sent = lax.ppermute(z, 'core', [(0, 1), (1, 0)])  11.6 us
    pallas_call x1, Pallas kernels, on_device(): call(early_kernel, [(2 * NB, N), (2 * NB, NB)], 0, 1, [work], flops=10 **...  10.2 us
    add x3, other arithmetic, sum_of_chips(): total = mine + lax.ppermute(other, 'core', [(0, 1), (1, 0)])  7.43 us
  transfers between devices with their start and end apart: 16, of which 12 were waited for; matrix products, arithmetic and copies ran while one was open for 5% of the time, Pallas kernels for 20%

profile of v1, /device:TPU:1, one launch (start us, length us, event | category | flops | bytes accessed | tf_op | source)
XLA Modules:
  0.0 266.9 jit_solution(8269602000662953487)
XLA Ops:
  2.9 3.4 %collective-permute-start = (f32[2048,128]{1,0:T(8,128)S(1)}, f32[2048,128]{1,0:T(8,128)S(1)}, u32[]{:S(2)}, u32[]{:S(2)}) collective-permute-start(f32[2048,128]{1,0:T(8,128)S(1)} %get-tuple-element.17), channel_id=1, source_target_pairs={{0,16},{16,0},{1,17},{17,1},{2,18},{18,2},{3,19},{19,3},{4,20},{20... | collective-permute-start | bytes 3145736 | tf_op jit(solution)/shard_map/early/ppermute | solution.py:92
  6.2 2.1 shard_map.29
  10.9 5.1 %all-to-all-start = ((f32[16,128,128]{2,1,0:T(8,128)}), f32[16,128,128]{2,1,0:T(8,128)}, u32[]{:S(2)}, u32[]{:S(2)}) async-start(f32[16,128,128]{2,1,0:T(8,128)} %bitcast.3), calls=%async_computation | async-start | bytes 2097152 | tf_op jit(solution)/shard_map/early/all_to_all | solution.py:82
  16.0 2.1 shard_map.32
  18.5 13.3 %all-to-all-done = f32[16,128,128]{2,1,0:T(8,128)} async-done(((f32[16,128,128]{2,1,0:T(8,128)}), f32[16,128,128]{2,1,0:T(8,128)}, u32[]{:S(2)}, u32[]{:S(2)}) %all-to-all-start) | async-done | bytes 1048608 | tf_op jit(solution)/shard_map/early/all_to_all | solution.py:82
  33.8 8.2 %all-to-all-start.1 = ((f32[8,16,128]{2,1,0:T(8,128)}), f32[8,16,128]{2,1,0:T(8,128)S(1)}, u32[]{:S(2)}, u32[]{:S(2)}) async-start(f32[8,16,128]{2,1,0:T(8,128)} %bitcast.4), calls=%async_computation.1 | async-start | bytes 131072 | tf_op jit(solution)/shard_map/early/all_to_all | solution.py:82
  42.0 3.2 %add.26 = f32[3072,128]{1,0:T(8,128)} add(f32[3072,128]{1,0:T(8,128)} %copy-done.4, f32[3072,128]{1,0:T(8,128)} %collective-permute-done.1) | non-fusion elementwise | flops 393216 | bytes 4718592 | tf_op jit(solution)/shard_map/late/add | solution.py:92
  45.2 4.0 %all-to-all-done.1 = f32[8,16,128]{2,1,0:T(8,128)S(1)} async-done(((f32[8,16,128]{2,1,0:T(8,128)}), f32[8,16,128]{2,1,0:T(8,128)S(1)}, u32[]{:S(2)}, u32[]{:S(2)}) %all-to-all-start.1) | async-done | bytes 65568 | tf_op jit(solution)/shard_map/early/all_to_all | solution.py:82
  49.2 4.6 %all-to-all-start.4 = ((f32[16,192,128]{2,1,0:T(8,128)}), f32[16,192,128]{2,1,0:T(8,128)}, u32[]{:S(2)}, u32[]{:S(2)}) async-start(f32[16,192,128]{2,1,0:T(8,128)} %bitcast.20), calls=%async_computation.4 | async-start | bytes 3145728 | tf_op jit(solution)/shard_map/late/all_to_all | solution.py:82
  53.8 19.1 %all-to-all-done.4 = f32[16,192,128]{2,1,0:T(8,128)} async-done(((f32[16,192,128]{2,1,0:T(8,128)}), f32[16,192,128]{2,1,0:T(8,128)}, u32[]{:S(2)}, u32[]{:S(2)}) %all-to-all-start.4) | async-done | bytes 1572896 | tf_op jit(solution)/shard_map/late/all_to_all | solution.py:82
  73.5 3.3 %all-to-all-start.2 = ((f32[8,16,128]{2,1,0:T(8,128)}), f32[8,16,128]{2,1,0:T(8,128)S(1)}, u32[]{:S(2)}, u32[]{:S(2)}) async-start(f32[8,16,128]{2,1,0:T(8,128)} %broadcast_in_dim.18), calls=%async_computation.2 | async-start | bytes 131072 | tf_op jit(solution)/shard_map/early/all_to_all | solution.py:82
  76.8 2.1 reduce_sum.56
  78.9 5.0 %all-to-all-done.2 = f32[8,16,128]{2,1,0:T(8,128)S(1)} async-done(((f32[8,16,128]{2,1,0:T(8,128)}), f32[8,16,128]{2,1,0:T(8,128)S(1)}, u32[]{:S(2)}, u32[]{:S(2)}) %all-to-all-start.2) | async-done | bytes 65568 | tf_op jit(solution)/shard_map/early/all_to_all | solution.py:82
  84.0 3.4 %all-to-all-start.5 = ((f32[8,24,128]{2,1,0:T(8,128)}), f32[8,24,128]{2,1,0:T(8,128)S(1)}, u32[]{:S(2)}, u32[]{:S(2)}) async-start(f32[8,24,128]{2,1,0:T(8,128)} %bitcast.8), calls=%async_computation.5 | async-start | bytes 196608 | tf_op jit(solution)/shard_map/late/all_to_all | solution.py:82
  87.3 3.1 %add.27 = f32[4096,128]{1,0:T(8,128)} add(f32[4096,128]{1,0:T(8,128)S(1)} %get-tuple-element.23, f32[4096,128]{1,0:T(8,128)} %collective-permute-done.3) | non-fusion elementwise | flops 524288 | bytes 6291456 | tf_op jit(solution)/shard_map/cross/add | solution.py:92
  90.4 4.4 %all-to-all-done.5 = f32[8,24,128]{2,1,0:T(8,128)S(1)} async-done(((f32[8,24,128]{2,1,0:T(8,128)}), f32[8,24,128]{2,1,0:T(8,128)S(1)}, u32[]{:S(2)}, u32[]{:S(2)}) %all-to-all-start.5) | async-done | bytes 98336 | tf_op jit(solution)/shard_map/late/all_to_all | solution.py:82
  94.8 30.2 %all_to_all.60 = f32[16,256,128]{2,1,0:T(8,128)S(1)} all-to-all(f32[16,256,128]{2,1,0:T(8,128)} %bitcast.19), channel_id=1, replica_groups=mesh['z_hi'=2,'x'=4,'core'=2,'y'=4,'z_lo'=4] {'x','y'}, dimensions={0} | all-to-all | bytes 4194304 | tf_op jit(solution)/shard_map/cross/all_to_all | solution.py:82
  126.1 4.0 %all-to-all-start.3 = ((f32[16,128,128]{2,1,0:T(8,128)}), f32[16,128,128]{2,1,0:T(8,128)S(1)}, u32[]{:S(2)}, u32[]{:S(2)}) async-start(f32[16,128,128]{2,1,0:T(8,128)} %broadcast_in_dim.20), calls=%async_computation.3 | async-start | bytes 2097152 | tf_op jit(solution)/shard_map/early/all_to_all | solution.py:82
  130.8 11.1 %all-to-all-done.3 = f32[16,128,128]{2,1,0:T(8,128)S(1)} async-done(((f32[16,128,128]{2,1,0:T(8,128)}), f32[16,128,128]{2,1,0:T(8,128)S(1)}, u32[]{:S(2)}, u32[]{:S(2)}) %all-to-all-start.3) | async-done | bytes 1048608 | tf_op jit(solution)/shard_map/early/all_to_all | solution.py:82
  141.9 3.4 %all-to-all-start.9 = ((f32[8,32,128]{2,1,0:T(8,128)}), f32[8,32,128]{2,1,0:T(8,128)S(1)}, u32[]{:S(2)}, u32[]{:S(2)}) async-start(f32[8,32,128]{2,1,0:T(8,128)} %bitcast.12), calls=%async_computation.9 | async-start | bytes 262144 | tf_op jit(solution)/shard_map/cross/all_to_all | solution.py:82
  145.3 7.8 %all-to-all-done.9 = f32[8,32,128]{2,1,0:T(8,128)S(1)} async-done(((f32[8,32,128]{2,1,0:T(8,128)}), f32[8,32,128]{2,1,0:T(8,128)S(1)}, u32[]{:S(2)}, u32[]{:S(2)}) %all-to-all-start.9) | async-done | bytes 131104 | tf_op jit(solution)/shard_map/cross/all_to_all | solution.py:82
  153.8 3.4 %all-to-all-start.6 = ((f32[8,24,128]{2,1,0:T(8,128)}), f32[8,24,128]{2,1,0:T(8,128)S(1)}, u32[]{:S(2)}, u32[]{:S(2)}) async-start(f32[8,24,128]{2,1,0:T(8,128)} %broadcast_in_dim.42), calls=%async_computation.6 | async-start | bytes 196608 | tf_op jit(solution)/shard_map/late/all_to_all | solution.py:82
  157.2 7.5 %all-to-all-done.6 = f32[8,24,128]{2,1,0:T(8,128)S(1)} async-done(((f32[8,24,128]{2,1,0:T(8,128)}), f32[8,24,128]{2,1,0:T(8,128)S(1)}, u32[]{:S(2)}, u32[]{:S(2)}) %all-to-all-start.6) | async-done | bytes 98336 | tf_op jit(solution)/shard_map/late/all_to_all | solution.py:82
  164.7 10.3 %all_to_all.61 = f32[8,32,128]{2,1,0:T(8,128)S(1)} all-to-all(f32[8,32,128]{2,1,0:T(8,128)S(1)} %broadcast_in_dim.45), channel_id=1, replica_groups=mesh['z_hi'=2,'x'=4,'core'=2,'y'=4,'z_lo'=4] {'z_hi','z_lo'}, dimensions={0} | all-to-all | bytes 262144 | tf_op jit(solution)/shard_map/cross/all_to_all | solution.py:82
  176.3 3.7 %all-to-all-start.7 = ((f32[16,192,128]{2,1,0:T(8,128)}), f32[16,192,128]{2,1,0:T(8,128)S(1)}, u32[]{:S(2)}, u32[]{:S(2)}) async-start(f32[16,192,128]{2,1,0:T(8,128)} %broadcast_in_dim.44), calls=%async_computation.7 | async-start | bytes 3145728 | tf_op jit(solution)/shard_map/late/all_to_all | solution.py:82
  180.1 10.2 %shard_map.30 = (f32[256,1024]{1,0:T(8,128)S(1)}, f32[256,128]{1,0:T(8,128)S(1)}) custom-call(f32[2048,128]{1,0:T(8,128)S(1)} %bitcast.17), custom_call_target="tpu_custom_call" | custom-call | flops 10000000000 | tf_op jit(solution)/shard_map/pallas_call | solution.py:240
  191.3 3.7 %all-to-all-done.7 = f32[16,192,128]{2,1,0:T(8,128)S(1)} async-done(((f32[16,192,128]{2,1,0:T(8,128)}), f32[16,192,128]{2,1,0:T(8,128)S(1)}, u32[]{:S(2)}, u32[]{:S(2)}) %all-to-all-start.7) | async-done | bytes 1572896 | tf_op jit(solution)/shard_map/late/all_to_all | solution.py:82
  196.8 3.9 %all-to-all-start.11 = ((f32[16,256,128]{2,1,0:T(8,128)}), f32[16,256,128]{2,1,0:T(8,128)S(1)}, u32[]{:S(2)}, u32[]{:S(2)}) async-start(f32[16,256,128]{2,1,0:T(8,128)} %broadcast_in_dim.47), calls=%async_computation.11 | async-start | bytes 4194304 | tf_op jit(solution)/shard_map/cross/all_to_all | solution.py:82
  203.4 38.3 %shard_map.31 = (f32[1024,1024]{1,0:T(8,128)S(1)}, f32[1024,128]{1,0:T(8,128)S(1)}, f32[8,1024]{1,0:T(8,128)S(1)}) custom-call(s32[2]{0:T(128)S(1)} %pad_add_fusion.rows, f32[2048,128]{1,0:T(8,128)S(1)} %bitcast.18, f32[3072,128]{1,0:T(8,128)S(1)} %bitcast.16, f32[256,1024]{1,0:T(8,128)S(1)} %copy-done.12, f32[256,128]{1,0:T(8,128)S(1)} %get-tuple-element.21.top_inverse), custom_call_target="tpu_custom_call" | custom-call | flops 30000001024 | tf_op jit(solution)/shard_map/pallas_call | solution.py:241
  244.4 11.6 %collective-permute-start.2 = (f32[8,1024]{1,0:T(8,128)S(1)}, f32[8,1024]{1,0:T(8,128)S(1)}, u32[]{:S(2)}, u32[]{:S(2)}) collective-permute-start(f32[8,1024]{1,0:T(8,128)S(1)} %get-tuple-element.22.z_own), channel_id=1, source_target_pairs={{0,16},{16,0},{1,17},{17,1},{2,18},{18,2},{3,19},{19,3},{4,20},{20... | collective-permute-start | bytes 98312 | tf_op jit(solution)/shard_map/ppermute | solution.py:244
  259.2 2.2 copy-done.1
  261.4 3.6 %shard_map.34 = f32[8,1024]{1,0:T(8,128)S(1)} custom-call(f32[8,1024]{1,0:T(8,128)S(1)} %shard_map.33.w_own, f32[8,1024]{1,0:T(8,128)S(1)} %collective-permute-done.4.w_sent, f32[1024,1024]{1,0:T(8,128)S(1)} %copy-done.1, f32[1024,128]{1,0:T(8,128)S(1)} %copy-done.6), custom_call_target="tpu_custom_call" | custom-call | tf_op jit(solution)/shard_map/pallas_call | solution.py:247
  (53 shorter events, 25.6 us)
Async XLA Ops:
  0.0 1.0 copy-start.7
  1.0 1.0 copy-start.9
  2.1 4.2 %copy-start.8 = (bf16[256,1024]{1,0:T(8,128)(2,1)S(1)}, bf16[256,1024]{1,0:T(8,128)(2,1)}, u32[]{:S(2)}) copy-start(bf16[256,1024]{1,0:T(8,128)(2,1)} %x.5) | copy-start | bytes 1572868
  2.1 4.2 %copy-start.10 = (bf16[256,1024]{1,0:T(8,128)(2,1)S(1)}, bf16[256,1024]{1,0:T(8,128)(2,1)}, u32[]{:S(2)}) copy-start(bf16[256,1024]{1,0:T(8,128)(2,1)} %y.5) | copy-start | bytes 1572868
  2.9 6.9 %collective-permute-start = (f32[2048,128]{1,0:T(8,128)S(1)}, f32[2048,128]{1,0:T(8,128)S(1)}, u32[]{:S(2)}, u32[]{:S(2)}) collective-permute-start(f32[2048,128]{1,0:T(8,128)S(1)} %get-tuple-element.17), channel_id=1, source_target_pairs={{0,16},{16,0},{1,17},{17,1},{2,18},{18,2},{3,19},{19,3},{4,20},{20... | collective-permute-start | bytes 3145736 | tf_op jit(solution)/shard_map/early/ppermute | solution.py:92
  8.3 1.2 copy-start.4
  9.5 32.5 %collective-permute-start.1 = (f32[3072,128]{1,0:T(8,128)}, f32[3072,128]{1,0:T(8,128)}, u32[]{:S(2)}, u32[]{:S(2)}) collective-permute-start(f32[3072,128]{1,0:T(8,128)} %get-tuple-element.19), channel_id=1, source_target_pairs={{0,16},{16,0},{1,17},{17,1},{2,18},{18,2},{3,19},{19,3},{4,20},{20... | collective-permute-start | bytes 4718600 | tf_op jit(solution)/shard_map/late/ppermute | solution.py:92
  10.9 21.0 %all-to-all-start = ((f32[16,128,128]{2,1,0:T(8,128)}), f32[16,128,128]{2,1,0:T(8,128)}, u32[]{:S(2)}, u32[]{:S(2)}) async-start(f32[16,128,128]{2,1,0:T(8,128)} %bitcast.3), calls=%async_computation | async-start | bytes 2097152 | tf_op jit(solution)/shard_map/early/all_to_all | solution.py:82
  18.0 69.3 %collective-permute-start.3 = (f32[4096,128]{1,0:T(8,128)}, f32[4096,128]{1,0:T(8,128)}, u32[]{:S(2)}, u32[]{:S(2)}) collective-permute-start(f32[4096,128]{1,0:T(8,128)} %get-tuple-element.24), channel_id=1, source_target_pairs={{0,16},{16,0},{1,17},{17,1},{2,18},{18,2},{3,19},{19,3},{4,20},{20... | collective-permute-start | bytes 6291464 | tf_op jit(solution)/shard_map/cross/ppermute | solution.py:92
  33.8 15.4 %all-to-all-start.1 = ((f32[8,16,128]{2,1,0:T(8,128)}), f32[8,16,128]{2,1,0:T(8,128)S(1)}, u32[]{:S(2)}, u32[]{:S(2)}) async-start(f32[8,16,128]{2,1,0:T(8,128)} %bitcast.4), calls=%async_computation.1 | async-start | bytes 131072 | tf_op jit(solution)/shard_map/early/all_to_all | solution.py:82
  49.2 23.6 %all-to-all-start.4 = ((f32[16,192,128]{2,1,0:T(8,128)}), f32[16,192,128]{2,1,0:T(8,128)}, u32[]{:S(2)}, u32[]{:S(2)}) async-start(f32[16,192,128]{2,1,0:T(8,128)} %bitcast.20), calls=%async_computation.4 | async-start | bytes 3145728 | tf_op jit(solution)/shard_map/late/all_to_all | solution.py:82
  73.5 10.5 %all-to-all-start.2 = ((f32[8,16,128]{2,1,0:T(8,128)}), f32[8,16,128]{2,1,0:T(8,128)S(1)}, u32[]{:S(2)}, u32[]{:S(2)}) async-start(f32[8,16,128]{2,1,0:T(8,128)} %broadcast_in_dim.18), calls=%async_computation.2 | async-start | bytes 131072 | tf_op jit(solution)/shard_map/early/all_to_all | solution.py:82
  84.0 10.9 %all-to-all-start.5 = ((f32[8,24,128]{2,1,0:T(8,128)}), f32[8,24,128]{2,1,0:T(8,128)S(1)}, u32[]{:S(2)}, u32[]{:S(2)}) async-start(f32[8,24,128]{2,1,0:T(8,128)} %bitcast.8), calls=%async_computation.5 | async-start | bytes 196608 | tf_op jit(solution)/shard_map/late/all_to_all | solution.py:82
  126.1 15.8 %all-to-all-start.3 = ((f32[16,128,128]{2,1,0:T(8,128)}), f32[16,128,128]{2,1,0:T(8,128)S(1)}, u32[]{:S(2)}, u32[]{:S(2)}) async-start(f32[16,128,128]{2,1,0:T(8,128)} %broadcast_in_dim.20), calls=%async_computation.3 | async-start | bytes 2097152 | tf_op jit(solution)/shard_map/early/all_to_all | solution.py:82
  141.9 11.2 %all-to-all-start.9 = ((f32[8,32,128]{2,1,0:T(8,128)}), f32[8,32,128]{2,1,0:T(8,128)S(1)}, u32[]{:S(2)}, u32[]{:S(2)}) async-start(f32[8,32,128]{2,1,0:T(8,128)} %bitcast.12), calls=%async_computation.9 | async-start | bytes 262144 | tf_op jit(solution)/shard_map/cross/all_to_all | solution.py:82
  153.8 10.9 %all-to-all-start.6 = ((f32[8,24,128]{2,1,0:T(8,128)}), f32[8,24,128]{2,1,0:T(8,128)S(1)}, u32[]{:S(2)}, u32[]{:S(2)}) async-start(f32[8,24,128]{2,1,0:T(8,128)} %broadcast_in_dim.42), calls=%async_computation.6 | async-start | bytes 196608 | tf_op jit(solution)/shard_map/late/all_to_all | solution.py:82
  176.3 18.8 %all-to-all-start.7 = ((f32[16,192,128]{2,1,0:T(8,128)}), f32[16,192,128]{2,1,0:T(8,128)S(1)}, u32[]{:S(2)}, u32[]{:S(2)}) async-start(f32[16,192,128]{2,1,0:T(8,128)} %broadcast_in_dim.44), calls=%async_computation.7 | async-start | bytes 3145728 | tf_op jit(solution)/shard_map/late/all_to_all | solution.py:82
  190.4 1.0 copy-start.11
  195.1 1.8 copy-start.2
  196.8 60.0 %all-to-all-start.11 = ((f32[16,256,128]{2,1,0:T(8,128)}), f32[16,256,128]{2,1,0:T(8,128)S(1)}, u32[]{:S(2)}, u32[]{:S(2)}) async-start(f32[16,256,128]{2,1,0:T(8,128)} %broadcast_in_dim.47), calls=%async_computation.11 | async-start | bytes 4194304 | tf_op jit(solution)/shard_map/cross/all_to_all | solution.py:82
  200.8 1.4 copy-start.3
  202.2 1.2 copy-start.12
  241.7 2.0 copy-start
  243.6 0.8 copy-start.5
  244.4 14.8 %copy-start.6 = (f32[1024,128]{1,0:T(8,128)S(1)}, f32[1024,128]{1,0:T(8,128)}, u32[]{:S(2)}) copy-start(f32[1024,128]{1,0:T(8,128)} %copy-done.5) | copy-start | bytes 1572868
  244.4 12.4 %collective-permute-start.2 = (f32[8,1024]{1,0:T(8,128)S(1)}, f32[8,1024]{1,0:T(8,128)S(1)}, u32[]{:S(2)}, u32[]{:S(2)}) collective-permute-start(f32[8,1024]{1,0:T(8,128)S(1)} %get-tuple-element.22.z_own), channel_id=1, source_target_pairs={{0,16},{16,0},{1,17},{17,1},{2,18},{18,2},{3,19},{19,3},{4,20},{20... | collective-permute-start | bytes 98312 | tf_op jit(solution)/shard_map/ppermute | solution.py:244
  257.8 1.4 collective-permute-start.4
  259.2 2.2 copy-start.1
  265.0 1.2 collective-permute-start.5

commit v2 on v1

--- a/solution.py
+++ b/solution.py
@@ -15,9 +15,11 @@
 N, NB, SB, G = 1024, 128, 32, 8
 KB = N // NB
 OWNED = 4
-UPPER = [(i, j) for i in range(KB) for j in range(i, KB)]
-EARLY, LATE = UPPER[:16], UPPER[16:]
-LATE_SLOTS = 24
+HEAD = 4
+EARLY = [(i, j) for i in range(HEAD) for j in range(i, HEAD)]
+LATE = [(i, j) for i in range(KB) for j in range(max(i, HEAD), KB)]
+LATE_SLOTS = 40 - len(EARLY)
+STEP = 16
 VMEM = pl.BlockSpec(memory_space=pltpu.VMEM)
 SMEM = pl.BlockSpec(memory_space=pltpu.SMEM)
 
@@ -35,12 +37,13 @@
         in_specs=[SMEM] * n_smem + [VMEM] * n_vmem,
         out_specs=[VMEM] * len(outs),
         scratch_shapes=list(scratch),
-        compiler_params=pltpu.CompilerParams(vmem_limit_bytes=40 << 20),
+        compiler_params=pltpu.CompilerParams(vmem_limit_bytes=16 << 20),
         cost_estimate=pl.CostEstimate(flops=flops, bytes_accessed=bytes_accessed, transcendentals=0),
     )
 
 
-def gram_kernel(blocks, slots, core, x, y, mine, other, pick):
+def gram_kernel(core, x, y, mine, other, pick):
+    early_rows, late_rows = len(EARLY) * NB // 16, LATE_SLOTS * NB // 16
     for out, which in ((mine, 0), (other, 1)):
         @pl.when(core[0] == which)
         def _():
@@ -50,18 +53,21 @@
         def _():
             pick[...] = y[...]
 
-        for i in sorted({i for i, _ in blocks}):
-            cols = [j for a, j in blocks if a == i]
-            lo, hi = min(cols), max(cols) + 1
+        for i in range(KB):
             prod = lax.dot_general(
-                pick[:, i * NB:(i + 1) * NB], pick[:, lo * NB:hi * NB], (((0,), (0,)), ((), ())),
+                pick[:, i * NB:(i + 1) * NB], pick[:, i * NB:], (((0,), (0,)), ((), ())),
                 preferred_element_type=jnp.float32,
             )
-            for j in cols:
-                at = blocks.index((i, j))
-                out[at * NB:(at + 1) * NB, :] = prod[:, (j - lo) * NB:(j - lo + 1) * NB]
-        if slots > len(blocks):
-            out[len(blocks) * NB:, :] = jnp.zeros(((slots - len(blocks)) * NB, NB), jnp.float32)
+            for j in range(i, KB):
+                early = (i, j) in EARLY
+                at = (EARLY if early else LATE).index((i, j)) * NB
+                rows, base = (early_rows, 0) if early else (late_rows, early_rows)
+                for t in range(0, NB, STEP):
+                    part, line = divmod(at + t, rows)
+                    out[part, base + line:base + line + STEP, :] = prod[t:t + STEP, (j - i) * NB:(j - i + 1) * NB]
+        for at in range(len(LATE) * NB, LATE_SLOTS * NB, STEP):
+            part, line = divmod(at, late_rows)
+            out[part, early_rows + line:early_rows + line + STEP, :] = jnp.zeros((STEP, NB), jnp.float32)
 
 
 def cross_kernel(core, x, y, mine, other):
@@ -86,14 +92,8 @@
     return jnp.broadcast_to(piece[None], (n, *piece.shape))
 
 
-def sum_of_chips(mine, other, name):
-    with jax.named_scope(name):
-        rows = mine.shape[0]
-        total = mine + lax.ppermute(other, "core", [(0, 1), (1, 0)])
-        piece = jnp.sum(exchange(total.reshape(16, rows // 16, NB), PLANE), axis=0)
-        part = jnp.sum(exchange(piece.reshape(8, rows // 128, NB), LINE), axis=0)
-        piece = exchange(spread(part, 8), LINE).reshape(rows // 16, NB)
-        return exchange(spread(piece, 16), PLANE).reshape(rows, NB)
+def swap(a):
+    return lax.ppermute(a, "core", [(0, 1), (1, 0)])
 
 
 def tile(v):
@@ -152,7 +152,7 @@
             work[rest:, :] -= mm(rows[:, rest:NB], rows, ((0,), (0,)))
 
 
-def eliminate(first, last, upto, upper, inverse, work):
+def eliminate(first, last, width, upper, inverse, work):
     eye = lax.broadcasted_iota(jnp.int32, (NB, NB), 0) == lax.broadcasted_iota(jnp.int32, (NB, NB), 1)
 
     def step(k, carry):
@@ -161,35 +161,45 @@
         work[:, NB:] = eye.astype(jnp.float32)
         factor_block(work)
         inverse[pl.ds(at, NB), :] = work[:, NB:]
-        for kk in range(first, min(last, KB - 1)):
+        for kk in range(first, min(last, width - 1)):
             @pl.when(k == kk)
             def _():
-                lo, nxt = kk * NB, (kk + 1) * NB
-                upper[lo:nxt, nxt:] = mm(work[:, NB:], upper[lo:nxt, nxt:], ((1,), (0,)))
-                for i in range(kk + 1, upto):
-                    rows = upper[lo:nxt, i * NB:]
-                    upper[i * NB:(i + 1) * NB, i * NB:] -= mm(rows[:, :NB], rows, ((0,), (0,)))
+                lo, nxt, end = kk * NB, (kk + 1) * NB, width * NB
+                upper[lo:nxt, nxt:end] = mm(work[:, NB:], upper[lo:nxt, nxt:end], ((1,), (0,)))
+                for i in range(kk + 1, width):
+                    rows = upper[lo:nxt, i * NB:end]
+                    upper[i * NB:(i + 1) * NB, i * NB:end] -= mm(rows[:, :NB], rows, ((0,), (0,)))
         return carry
 
     lax.fori_loop(first, last, step, 0)
 
 
-def early_kernel(blocks, upper, inverse, work):
-    for at, (i, j) in enumerate(EARLY[:15]):
+def head_kernel(blocks, upper, inverse, work):
+    for at, (i, j) in enumerate(EARLY):
         upper[i * NB:(i + 1) * NB, j * NB:(j + 1) * NB] = blocks[at * NB:(at + 1) * NB, :]
-    eliminate(0, 2, 2, upper, inverse, work)
-
-
-def late_kernel(rows, early, late, top, top_inverse, upper, inverse, z, work):
-    upper[:2 * NB, :] = top[...]
-    inverse[:2 * NB, :] = top_inverse[...]
-    upper[2 * NB:3 * NB, 2 * NB:3 * NB] = early[15 * NB:16 * NB, :]
+    eliminate(0, HEAD, HEAD, upper, inverse, work)
+
+
+def middle_kernel(last, blocks, head, head_inverse, upper, inverse, work):
+    h = HEAD * NB
+    upper[:h, :h] = head[...]
+    inverse[:h, :] = head_inverse[...]
     for at, (i, j) in enumerate(LATE):
-        upper[i * NB:(i + 1) * NB, j * NB:(j + 1) * NB] = late[at * NB:(at + 1) * NB, :]
-    for i in range(2, KB):
-        both = upper[:2 * NB, i * NB:]
-        upper[i * NB:(i + 1) * NB, i * NB:] -= mm(both[:, :NB], both, ((0,), (0,)))
-    eliminate(2, KB, KB, upper, inverse, work)
+        upper[i * NB:(i + 1) * NB, j * NB:(j + 1) * NB] = blocks[at * NB:(at + 1) * NB, :]
+    for k in range(HEAD):
+        lo, nxt = k * NB, (k + 1) * NB
+        v = upper[lo:nxt, h:]
+        if k:
+            v = v - mm(upper[:lo, lo:nxt], upper[:lo, h:], ((0,), (0,)))
+        upper[lo:nxt, h:] = mm(inverse[lo:nxt, :], v, ((1,), (0,)))
+    for i in range(HEAD, KB):
+        done = upper[:h, i * NB:]
+        upper[i * NB:(i + 1) * NB, i * NB:] -= mm(done[:, :NB], done, ((0,), (0,)))
+    eliminate(HEAD, last, KB, upper, inverse, work)
+
+
+def tail_kernel(first, rows, upper_in, inverse_in, upper, inverse, z, work):
+    eliminate(first, KB, KB, upper, inverse, work)
     line = lax.broadcasted_iota(jnp.int32, (G, NB), 0)
     want = jnp.where(line < OWNED, rows[0] + line, rows[1] + line - OWNED)
     lane = lax.broadcasted_iota(jnp.int32, (G, NB), 1)
@@ -219,33 +229,67 @@
         y[:, k * NB:(k + 1) * NB] = mm(v, inverse[k * NB:(k + 1) * NB, :], ((1,), (1,)))
 
 
+def after(value, *others):
+    return lax.optimization_barrier((value, *others))[0]
+
+
 def on_device(view_x, view_y):
     core = lax.axis_index("core")
     core_ref = core.astype(jnp.int32).reshape(1)
     chip = ((lax.axis_index("z_hi") * 4 + lax.axis_index("x")) * 2) * 16 + lax.axis_index("y") * 4 + lax.axis_index("z_lo")
     rows = jnp.stack([chip * OWNED, (chip + 16) * OWNED]).astype(jnp.int32)
     work = pltpu.VMEM((NB, 2 * NB), jnp.float32)
-    pick = pltpu.VMEM(view_x.shape, view_x.dtype)
-
-    sums = []
-    for blocks, slots, name in ((EARLY, 16, "early"), (LATE, LATE_SLOTS, "late")):
+    early_rows, late_rows = len(EARLY) * NB // 16, LATE_SLOTS * NB // 16
+    part = early_rows + late_rows
+
+    with jax.named_scope("gram"):
         mine, other = call(
-            functools.partial(gram_kernel, blocks, slots), [(slots * NB, NB)] * 2, 1, 2, [pick], flops=10**9
+            gram_kernel, [(16, part, NB)] * 2, 1, 2, [pltpu.VMEM(view_x.shape, view_x.dtype)], flops=2 * 10**9
         )(core_ref, view_x, view_y)
-        sums.append(sum_of_chips(mine, other, name))
-    early, late = sums
-    mine, other = call(cross_kernel, [(32 * NB, NB)] * 2, 1, 2, flops=10**9)(core_ref, view_x, view_y)
-    cross = sum_of_chips(mine, other, "cross")
-
-    top, top_inverse = call(early_kernel, [(2 * NB, N), (2 * NB, NB)], 0, 1, [work], flops=10**10)(early)
-    upper, inverse, z = call(late_kernel, [(N, N), (N, NB), (G, N)], 1, 4, [work], flops=3 * 10**10)(
-        rows, early, late, top, top_inverse
-    )
-    z_sent = lax.ppermute(z, "core", [(0, 1), (1, 0)])
-    (w,) = call(apply_kernel, [(G, N)], 1, 3)(core_ref, z, z_sent, cross)
-    w_sent = lax.ppermute(w, "core", [(0, 1), (1, 0)])
-    (y,) = call(solve_kernel, [(G, N)], 0, 4)(w, w_sent, upper, inverse)
-    y_sent = lax.ppermute(y[:OWNED], "core", [(0, 1), (1, 0)])
+        gram = mine + swap(other)
+    with jax.named_scope("cross"):
+        keep, give = call(cross_kernel, [(32 * NB, NB)] * 2, 1, 2, flops=10**9)(
+            core_ref, *after((view_x, view_y), mine)
+        )
+        cross = keep + swap(give)
+        for axis in PLANE:
+            cross = lax.psum_scatter(cross, axis, scatter_dimension=0, tiled=True)
+    with jax.named_scope("gram"):
+        piece = jnp.sum(exchange(gram, PLANE), axis=0)
+        share = jnp.sum(exchange(piece.reshape(8, part // 8, NB), LINE), axis=0)
+    with jax.named_scope("both"):
+        both = exchange(jnp.concatenate([spread(share, 8), cross.reshape(8, -1, NB)], axis=1), LINE)
+        piece = both[:, :part // 8].reshape(part, NB)
+        early = exchange(spread(piece[:early_rows], 16), PLANE).reshape(16 * early_rows, NB)
+        both = after(both, early)
+        piece = both[:, :part // 8].reshape(part, NB)
+        late = exchange(spread(piece[early_rows:], 16), PLANE).reshape(16 * late_rows, NB)
+        cross = jnp.sum(both[:, part // 8:], axis=0)
+
+    head, head_inverse = call(
+        head_kernel, [(HEAD * NB, HEAD * NB), (HEAD * NB, NB)], 0, 1, [work], flops=3 * 10**10
+    )(early)
+    with jax.named_scope("cross_back"):
+        cross = after(cross, head)
+        cross = exchange(spread(cross, 8), LINE).reshape(256, NB)
+    upper, inverse = call(
+        functools.partial(middle_kernel, 5), [(N, N), (N, NB)], 0, 3, [work], flops=10**10
+    )(late, head, head_inverse)
+    with jax.named_scope("cross_back"):
+        cross = exchange(spread(after(cross, upper), 16), PLANE).reshape(32 * NB, NB)
+    upper, inverse, z = pl.pallas_call(
+        functools.partial(tail_kernel, 5),
+        out_shape=[jax.ShapeDtypeStruct(s, jnp.float32) for s in ((N, N), (N, NB), (G, N))],
+        in_specs=[SMEM, VMEM, VMEM],
+        out_specs=[VMEM] * 3,
+        scratch_shapes=[work],
+        input_output_aliases={1: 0, 2: 1},
+        compiler_params=pltpu.CompilerParams(vmem_limit_bytes=16 << 20),
+        cost_estimate=pl.CostEstimate(flops=3 * 10**10, bytes_accessed=0, transcendentals=0),
+    )(rows, upper, inverse)
+    (w,) = call(apply_kernel, [(G, N)], 1, 3)(core_ref, z, swap(z), cross)
+    (y,) = call(solve_kernel, [(G, N)], 0, 4)(w, swap(w), upper, inverse)
+    y_sent = swap(y[:OWNED])
     return jnp.where(core == 0, y_sent, y[OWNED:])
 
 

time: 268 us -> 241 us (0.90)
  starting transfers between devices: 59.5 us -> 34.7 us
  between operations: 0.18 us -> 13.6 us
  blocking collectives: 40.5 us -> 32.3 us
  other arithmetic: 12.9 us -> 6.87 us
    all_to_all x10 -> x5, waiting for transfers between devices: 75.9 us -> 11.4 us  [exchange(): return lax.all_to_all(pieces, axes, 0, 0, tiled=True)]
    reduce_scatter x0 -> x2, waiting for transfers between devices: none -> 59.1 us  [on_device(): cross = lax.psum_scatter(cross, axis, scatter_dimension=0, tiled=True)]
    all_to_all x10 -> x5, starting transfers between devices: 42.8 us -> 25.2 us  [exchange(): return lax.all_to_all(pieces, axes, 0, 0, tiled=True)]
    all_to_all x2, blocking collectives: 40.5 us -> 32.3 us  [exchange(): return lax.all_to_all(pieces, axes, 0, 0, tiled=True)]
    ppermute x6 -> x5, starting transfers between devices: 16.6 us -> 9.48 us  [swap(): return lax.ppermute(a, 'core', [(0, 1), (1, 0)])]
    ppermute x6 -> x5, waiting for transfers between devices: 2.57 us -> 8.75 us  [swap(): return lax.ppermute(a, 'core', [(0, 1), (1, 0)])]
    reduce_sum x6 -> x3, other arithmetic: 4.83 us -> 0.16 us  [the longest x1 0.13 us: on_device(): piece = jnp.sum(exchange(gram, PLANE), axis=0)]
    add x3 -> x2, other arithmetic: 7.43 us -> 5.1 us  [the longest x1 3.54 us: on_device(): gram = mine + swap(other)]
  transfers between devices with their start and end apart: 16 -> 12, of which waited for: 12 -> 9; matrix products, arithmetic and copies ran while one was open for 5% -> 2% of each run, Pallas kernels for 20% -> 20%
where the time goes in v2:
time: 241 us; the launch traced here: 240 us
  waiting for transfers between devices  79.3 us (33%)
  Pallas kernels  56.3 us (23%)
  starting transfers between devices  34.7 us (14%)
  blocking collectives  32.3 us (13%)
  local copies, waits for them, and re-layouts  17.1 us (7%)
  between operations  13.6 us (6%)
  other arithmetic  6.87 us (3%)
    reduce_scatter x2, waiting for transfers between devices, on_device(): cross = lax.psum_scatter(cross, axis, scatter_dimension=0, tiled=True)  59.1 us
    all_to_all x2, blocking collectives, exchange(): return lax.all_to_all(pieces, axes, 0, 0, tiled=True)  32.3 us
    all_to_all x5, starting transfers between devices, exchange(): return lax.all_to_all(pieces, axes, 0, 0, tiled=True)  25.2 us
    pallas_call x1, Pallas kernels, on_device(): pl.pallas_call(functools.partial(tail_kernel, 5), out_shape=[jax.ShapeDty...  20.2 us
    pallas_call x1, Pallas kernels, on_device(): call(head_kernel, [(HEAD * NB, HEAD * NB), (HEAD * NB, NB)], 0, 1, [work]...  19.5 us
    unnamed x16, local copies, waits for them, and re-layouts  12.6 us
    all_to_all x5, waiting for transfers between devices, exchange(): return lax.all_to_all(pieces, axes, 0, 0, tiled=True)  11.4 us
    ppermute x5, starting transfers between devices, swap(): return lax.ppermute(a, 'core', [(0, 1), (1, 0)])  9.48 us
  transfers between devices with their start and end apart: 12, of which 9 were waited for; matrix products, arithmetic and copies ran while one was open for 2% of the time, Pallas kernels for 20%

profile of v2, /device:TPU:1, one launch (start us, length us, event | category | flops | bytes accessed | tf_op | source)
XLA Modules:
  0.0 240.1 jit_solution(17157834766996374105)
XLA Ops:
  6.5 1.0 copy-done.4
  7.6 1.0 copy-done.5
  8.6 2.7 %gram.1 = (f32[16,320,128]{2,1,0:T(8,128)S(1)}, f32[16,320,128]{2,1,0:T(8,128)}) custom-call(s32[1]{0:T(128)} %bitcast.core, bf16[256,1024]{1,0:T(8,128)(2,1)S(1)} %copy-done.4, bf16[256,1024]{1,0:T(8,128)(2,1)S(1)} %copy-done.5), custom_call_target="tpu_custom_call" | custom-call | flops 2000000000 | tf_op jit(solution)/shard_map/gram/pallas_call | solution.py:246
  12.0 3.3 %collective-permute-start.1 = (f32[4096,128]{1,0:T(8,128)S(1)}, f32[4096,128]{1,0:T(8,128)S(1)}, u32[]{:S(2)}, u32[]{:S(2)}) collective-permute-start(f32[4096,128]{1,0:T(8,128)S(1)} %get-tuple-element.26), channel_id=1, source_target_pairs={{0,16},{16,0},{1,17},{17,1},{2,18},{18,2},{3,19},{19,3},{4,20},{20... | collective-permute-start | bytes 6291464 | tf_op jit(solution)/shard_map/cross/ppermute | solution.py:96
  15.5 5.7 %collective-permute-done.1 = f32[4096,128]{1,0:T(8,128)S(1)} collective-permute-done((f32[4096,128]{1,0:T(8,128)S(1)}, f32[4096,128]{1,0:T(8,128)S(1)}, u32[]{:S(2)}, u32[]{:S(2)}) %collective-permute-start.1) | collective-permute-done | bytes 2097184 | tf_op jit(solution)/shard_map/cross/ppermute | solution.py:96
  21.2 1.6 add.27
  23.3 3.5 %add.26 = f32[16,320,128]{2,1,0:T(8,128)} add(f32[16,320,128]{2,1,0:T(8,128)S(1)} %get-tuple-element.21, f32[16,320,128]{2,1,0:T(8,128)} %collective-permute-done) | non-fusion elementwise | flops 655360 | bytes 7864320 | tf_op jit(solution)/shard_map/gram/add | solution.py:249
  26.8 5.0 %all-to-all-start = ((f32[16,320,128]{2,1,0:T(8,128)}), f32[16,320,128]{2,1,0:T(8,128)S(1)}, u32[]{:S(2)}, u32[]{:S(2)}) async-start(f32[16,320,128]{2,1,0:T(8,128)} %add.26), calls=%async_computation | async-start | bytes 5242880 | tf_op jit(solution)/shard_map/gram/all_to_all | solution.py:88
  31.9 50.7 %reduce-scatter.3.cloned.1.call-done = f32[1024,128]{1,0:T(8,128)} async-done(((f32[4096,128]{1,0:T(8,128)}), f32[1024,128]{1,0:T(8,128)}) %reduce-scatter.3.cloned.1.call-update) | async-done | bytes 524304 | tf_op jit(solution)/shard_map/cross/reduce_scatter | solution.py:256
  82.8 16.1 %all_to_all.35 = f32[8,40,128]{2,1,0:T(8,128)S(1)} all-to-all(f32[8,40,128]{2,1,0:T(8,128)S(1)} %bitcast.14), channel_id=1, replica_groups=mesh['z_hi'=2,'x'=4,'core'=2,'y'=4,'z_lo'=4] {'z_hi','z_lo'}, dimensions={0} | all-to-all | bytes 327680 | tf_op jit(solution)/shard_map/gram/all_to_all | solution.py:88
  98.9 8.4 %reduce-scatter.5.cloned.1.call-done = f32[256,128]{1,0:T(8,128)} async-done(((f32[1024,128]{1,0:T(8,128)}), f32[256,128]{1,0:T(8,128)}) %reduce-scatter.5.cloned.1.call-update) | async-done | bytes 131088 | tf_op jit(solution)/shard_map/cross/reduce_scatter | solution.py:256
  108.2 16.2 %all_to_all.36 = f32[8,72,128]{2,1,0:T(8,128)S(1)} all-to-all(f32[8,72,128]{2,1,0:T(8,128)S(1)} %pad_maximum_fusion), channel_id=1, replica_groups=mesh['z_hi'=2,'x'=4,'core'=2,'y'=4,'z_lo'=4] {'z_hi','z_lo'}, dimensions={0} | all-to-all | bytes 589824 | tf_op jit(solution)/shard_map/both/all_to_all | solution.py:88
  125.4 5.3 %all-to-all-start.3 = ((f32[16,80,128]{2,1,0:T(8,128)}), f32[16,80,128]{2,1,0:T(8,128)S(1)}, u32[]{:S(2)}, u32[]{:S(2)}) async-start(f32[16,80,128]{2,1,0:T(8,128)} %broadcast_in_dim.16), calls=%async_computation.5 | async-start | bytes 1310720 | tf_op jit(solution)/shard_map/both/all_to_all | solution.py:88
  130.7 9.7 %all-to-all-done.3 = f32[16,80,128]{2,1,0:T(8,128)S(1)} async-done(((f32[16,80,128]{2,1,0:T(8,128)}), f32[16,80,128]{2,1,0:T(8,128)S(1)}, u32[]{:S(2)}, u32[]{:S(2)}) %all-to-all-start.3) | async-done | bytes 655392 | tf_op jit(solution)/shard_map/both/all_to_all | solution.py:88
  140.4 1.4 broadcast_in_dim.18
  141.9 3.7 %all-to-all-start.4 = ((f32[16,240,128]{2,1,0:T(8,128)}), f32[16,240,128]{2,1,0:T(8,128)S(1)}, u32[]{:S(2)}, u32[]{:S(2)}) async-start(f32[16,240,128]{2,1,0:T(8,128)} %broadcast_in_dim.18), calls=%async_computation.6 | async-start | bytes 3932160 | tf_op jit(solution)/shard_map/both/all_to_all | solution.py:88
  145.6 19.5 %shard_map.28 = (f32[512,512]{1,0:T(8,128)S(1)}, f32[512,128]{1,0:T(8,128)S(1)}) custom-call(f32[1280,128]{1,0:T(8,128)S(1)} %bitcast.13), custom_call_target="tpu_custom_call" | custom-call | flops 30000001024 | tf_op jit(solution)/shard_map/pallas_call | solution.py:269
  165.1 1.0 copy-done.6
  166.1 1.7 all-to-all-done.4
  168.5 3.5 %all-to-all-start.5 = ((f32[8,32,128]{2,1,0:T(8,128)}), f32[8,32,128]{2,1,0:T(8,128)S(1)}, u32[]{:S(2)}, u32[]{:S(2)}) async-start(f32[8,32,128]{2,1,0:T(8,128)} %broadcast_in_dim.19), calls=%async_computation.7 | async-start | bytes 262144 | tf_op jit(solution)/shard_map/cross_back/all_to_all | solution.py:88
  172.0 1.2 copy-done.7
  173.3 8.6 %shard_map.29 = (f32[1024,1024]{1,0:T(8,128)S(1)}, f32[1024,128]{1,0:T(8,128)S(1)}) custom-call(f32[3840,128]{1,0:T(8,128)S(1)} %bitcast.12, f32[512,512]{1,0:T(8,128)S(1)} %copy-done.7, f32[512,128]{1,0:T(8,128)S(1)} %get-tuple-element.29.head_inverse), custom_call_target="tpu_custom_call" | custom-call | flops 10000000000 | tf_op jit(solution)/shard_map/pallas_call | solution.py:275
  181.8 1.9 copy-done
  183.8 1.6 broadcast_in_dim.40
  185.3 7.6 %all-to-all-start.6 = ((f32[16,256,128]{2,1,0:T(8,128)}), f32[16,256,128]{2,1,0:T(8,128)S(1)}, u32[]{:S(2)}, u32[]{:S(2)}) async-start(f32[16,256,128]{2,1,0:T(8,128)} %broadcast_in_dim.40), calls=%async_computation.8 | async-start | bytes 4194304 | tf_op jit(solution)/shard_map/cross_back/all_to_all | solution.py:88
  193.0 2.2 copy-done.1
  195.2 20.2 %shard_map.30 = (f32[1024,1024]{1,0:T(8,128)S(1)}, f32[1024,128]{1,0:T(8,128)S(1)}, f32[8,1024]{1,0:T(8,128)S(1)}) custom-call(s32[2]{0:T(128)S(1)} %pad_add_fusion.rows, f32[1024,1024]{1,0:T(8,128)S(1)} %copy-done.1, f32[1024,128]{1,0:T(8,128)S(1)} %get-tuple-element.31.inverse_in), custom_call_target="tpu_custom_call", output_to_operand_aliasing={{0}: (1, {}), {1}: (2, {})} | custom-call | flops 30000001024 | tf_op jit(solution)/shard_map/pallas_call | solution.py:280
  215.3 2.0 copy-done.2
  217.3 3.2 %collective-permute-start.2 = (f32[8,1024]{1,0:T(8,128)S(1)}, f32[8,1024]{1,0:T(8,128)S(1)}, u32[]{:S(2)}, u32[]{:S(2)}) collective-permute-start(f32[8,1024]{1,0:T(8,128)S(1)} %get-tuple-element.32.z_own), channel_id=1, source_target_pairs={{0,16},{16,0},{1,17},{17,1},{2,18},{18,2},{3,19},{19,3},{4,20},{20... | collective-permute-start | bytes 98312 | tf_op jit(solution)/shard_map/ppermute | solution.py:96
  222.3 2.5 %collective-permute-start.3 = (f32[8,1024]{1,0:T(8,128)S(1)}, f32[8,1024]{1,0:T(8,128)S(1)}, u32[]{:S(2)}, u32[]{:S(2)}) collective-permute-start(f32[8,1024]{1,0:T(8,128)S(1)} %shard_map.31.w_own), channel_id=1, source_target_pairs={{0,16},{16,0},{1,17},{17,1},{2,18},{18,2},{3,19},{19,3},{4,20},{20... | collective-permute-start | bytes 98312 | tf_op jit(solution)/shard_map/ppermute | solution.py:96
  225.7 2.2 copy-done.3
  227.8 3.6 %shard_map.32 = f32[8,1024]{1,0:T(8,128)S(1)} custom-call(f32[8,1024]{1,0:T(8,128)S(1)} %shard_map.31.w_own, f32[8,1024]{1,0:T(8,128)S(1)} %collective-permute-done.3.w_sent, f32[1024,1024]{1,0:T(8,128)S(1)} %copy-done.3, f32[1024,128]{1,0:T(8,128)S(1)} %get-tuple-element.36.inverse), custom_call_target="tpu_custom_call" | custom-call | tf_op jit(solution)/shard_map/pallas_call | solution.py:291
  (35 shorter events, 8.7 us)
Async XLA Ops:
  6.5 76.1 %reduce-scatter.3.cloned.1.call-start = ((), (), s32[]{:S(2)}) async-start(), calls=%async_computation.9 | async-start | bytes 2621440 | tf_op jit(solution)/shard_map/cross/reduce_scatter | solution.py:256
  6.5 1.0 copy-start.4
  7.6 1.0 copy-start.5
  12.0 9.1 %collective-permute-start.1 = (f32[4096,128]{1,0:T(8,128)S(1)}, f32[4096,128]{1,0:T(8,128)S(1)}, u32[]{:S(2)}, u32[]{:S(2)}) collective-permute-start(f32[4096,128]{1,0:T(8,128)S(1)} %get-tuple-element.26), channel_id=1, source_target_pairs={{0,16},{16,0},{1,17},{17,1},{2,18},{18,2},{3,19},{19,3},{4,20},{20... | collective-permute-start | bytes 6291464 | tf_op jit(solution)/shard_map/cross/ppermute | solution.py:96
  15.4 7.9 %collective-permute-start = (f32[16,320,128]{2,1,0:T(8,128)}, f32[16,320,128]{2,1,0:T(8,128)}, u32[]{:S(2)}, u32[]{:S(2)}) collective-permute-start(f32[16,320,128]{2,1,0:T(8,128)} %get-tuple-element.22), channel_id=1, source_target_pairs={{0,16},{16,0},{1,17},{17,1},{2,18},{18,2},{3,19},{19,3},{4,20},{20... | collective-permute-start | bytes 7864328 | tf_op jit(solution)/shard_map/gram/ppermute | solution.py:96
  26.8 55.8 %all-to-all-start = ((f32[16,320,128]{2,1,0:T(8,128)}), f32[16,320,128]{2,1,0:T(8,128)S(1)}, u32[]{:S(2)}, u32[]{:S(2)}) async-start(f32[16,320,128]{2,1,0:T(8,128)} %add.26), calls=%async_computation | async-start | bytes 5242880 | tf_op jit(solution)/shard_map/gram/all_to_all | solution.py:88
  31.8 75.5 %reduce-scatter.5.cloned.1.call-start = ((), (), s32[]{:S(2)}) async-start(), calls=%async_computation.10 | async-start | bytes 655360 | tf_op jit(solution)/shard_map/cross/reduce_scatter | solution.py:256
  125.4 15.0 %all-to-all-start.3 = ((f32[16,80,128]{2,1,0:T(8,128)}), f32[16,80,128]{2,1,0:T(8,128)S(1)}, u32[]{:S(2)}, u32[]{:S(2)}) async-start(f32[16,80,128]{2,1,0:T(8,128)} %broadcast_in_dim.16), calls=%async_computation.5 | async-start | bytes 1310720 | tf_op jit(solution)/shard_map/both/all_to_all | solution.py:88
  141.9 26.0 %all-to-all-start.4 = ((f32[16,240,128]{2,1,0:T(8,128)}), f32[16,240,128]{2,1,0:T(8,128)S(1)}, u32[]{:S(2)}, u32[]{:S(2)}) async-start(f32[16,240,128]{2,1,0:T(8,128)} %broadcast_in_dim.18), calls=%async_computation.6 | async-start | bytes 3932160 | tf_op jit(solution)/shard_map/both/all_to_all | solution.py:88
  165.1 1.0 copy-start.6
  168.5 15.3 %all-to-all-start.5 = ((f32[8,32,128]{2,1,0:T(8,128)}), f32[8,32,128]{2,1,0:T(8,128)S(1)}, u32[]{:S(2)}, u32[]{:S(2)}) async-start(f32[8,32,128]{2,1,0:T(8,128)} %broadcast_in_dim.19), calls=%async_computation.7 | async-start | bytes 262144 | tf_op jit(solution)/shard_map/cross_back/all_to_all | solution.py:88
  172.0 1.2 copy-start.7
  181.8 2.0 copy-start
  185.3 36.0 %all-to-all-start.6 = ((f32[16,256,128]{2,1,0:T(8,128)}), f32[16,256,128]{2,1,0:T(8,128)S(1)}, u32[]{:S(2)}, u32[]{:S(2)}) async-start(f32[16,256,128]{2,1,0:T(8,128)} %broadcast_in_dim.40), calls=%async_computation.8 | async-start | bytes 4194304 | tf_op jit(solution)/shard_map/cross_back/all_to_all | solution.py:88
  193.0 2.2 copy-start.1
  215.3 2.0 copy-start.2
  217.3 4.0 %collective-permute-start.2 = (f32[8,1024]{1,0:T(8,128)S(1)}, f32[8,1024]{1,0:T(8,128)S(1)}, u32[]{:S(2)}, u32[]{:S(2)}) collective-permute-start(f32[8,1024]{1,0:T(8,128)S(1)} %get-tuple-element.32.z_own), channel_id=1, source_target_pairs={{0,16},{16,0},{1,17},{17,1},{2,18},{18,2},{3,19},{19,3},{4,20},{20... | collective-permute-start | bytes 98312 | tf_op jit(solution)/shard_map/ppermute | solution.py:96
  222.3 3.4 %collective-permute-start.3 = (f32[8,1024]{1,0:T(8,128)S(1)}, f32[8,1024]{1,0:T(8,128)S(1)}, u32[]{:S(2)}, u32[]{:S(2)}) collective-permute-start(f32[8,1024]{1,0:T(8,128)S(1)} %shard_map.31.w_own), channel_id=1, source_target_pairs={{0,16},{16,0},{1,17},{17,1},{2,18},{18,2},{3,19},{19,3},{4,20},{20... | collective-permute-start | bytes 98312 | tf_op jit(solution)/shard_map/ppermute | solution.py:96
  225.7 2.2 copy-start.3
  231.5 1.2 collective-permute-start.4
Sparse Core Ops, SparseCore 0:
  22.9 59.6 reduce-scatter.2
  85.3 21.9 reduce-scatter.4

commit v3 on v2

--- a/solution.py
+++ b/solution.py
@@ -15,11 +15,14 @@
 N, NB, SB, G = 1024, 128, 32, 8
 KB = N // NB
 OWNED = 4
-HEAD = 4
+HEAD = 5
 EARLY = [(i, j) for i in range(HEAD) for j in range(i, HEAD)]
 LATE = [(i, j) for i in range(KB) for j in range(max(i, HEAD), KB)]
 LATE_SLOTS = 40 - len(EARLY)
-STEP = 16
+STEP = 8
+EARLY_ROWS = len(EARLY) * NB // 16
+GRAM = 40 * NB // 16
+PART = GRAM + N // 2 * N // NB // 16
 VMEM = pl.BlockSpec(memory_space=pltpu.VMEM)
 SMEM = pl.BlockSpec(memory_space=pltpu.SMEM)
 
@@ -43,7 +46,7 @@
 
 
 def gram_kernel(core, x, y, mine, other, pick):
-    early_rows, late_rows = len(EARLY) * NB // 16, LATE_SLOTS * NB // 16
+    early_rows, late_rows = EARLY_ROWS, GRAM - EARLY_ROWS
     for out, which in ((mine, 0), (other, 1)):
         @pl.when(core[0] == which)
         def _():
@@ -80,8 +83,7 @@
             )
             for i in range(half // NB):
                 for d in range(2):
-                    at = i * KB + 2 * j + d
-                    out[at * NB:(at + 1) * NB, :] = prod[i * NB:(i + 1) * NB, d * NB:(d + 1) * NB]
+                    out[i * KB // 2 + j, d * NB:(d + 1) * NB, :] = prod[i * NB:(i + 1) * NB, d * NB:(d + 1) * NB]
 
 
 def exchange(pieces, axes):
@@ -94,6 +96,59 @@
 
 def swap(a):
     return lax.ppermute(a, "core", [(0, 1), (1, 0)])
+
+
+def shift(pieces, axis, size):
+    return [
+        lax.ppermute(p, axis, [(i, (i + k) % size) for i in range(size)]) if k else p for k, p in enumerate(pieces)
+    ]
+
+
+def plane_first_kernel(at, gram, gram_got, cross, cross_got, *outs):
+    x, y, cut = at[0], at[1], PART // 2
+    for k in range(4):
+        for j in range(4):
+            p = ((x + k) & 3) * 4 + j
+            outs[k][j] = gram[p, :cut] + gram_got[p, :cut]
+            p = j * 4 + ((y + k) & 3)
+            outs[4 + k][j, :GRAM - cut] = gram[p, cut:] + gram_got[p, cut:]
+            outs[4 + k][j, GRAM - cut:] = cross[p] + cross_got[p]
+
+
+def plane_second_kernel(at, *refs):
+    ins, outs = refs[:8], refs[8:]
+    for k in range(4):
+        for base, me in ((0, at[1]), (4, at[0])):
+            p = (me + k) & 3
+            outs[base + k][...] = (ins[base][p] + ins[base + 1][p]) + (ins[base + 2][p] + ins[base + 3][p])
+
+
+def line_first_kernel(at, *refs):
+    ins, outs = refs[:8], refs[8:]
+    rows = PART // 8
+    for k in range(4):
+        lines = pl.ds(pl.multiple_of(((at[2] + k) & 3) * rows, 8), rows)
+        for h in range(2):
+            a, b, c, d = (r[lines, :] for r in ins[4 * h:4 * h + 4])
+            outs[k][h] = (a + b) + (c + d)
+
+
+def line_second_kernel(at, a, b, c, d, *outs):
+    for k in range(2):
+        h = (at[3] + k) & 1
+        outs[k][...] = (a[h] + b[h]) + (c[h] + d[h])
+
+
+def share_of_sum(at, gram, gram_got, cross, cross_got):
+    half, rows = PART // 2, PART // 8
+    pieces = call(plane_first_kernel, [(4, half, NB)] * 8, 1, 4)(at, gram, gram_got, cross, cross_got)
+    got = shift(pieces[:4], "x", 4) + shift(pieces[4:], "y", 4)
+    pieces = call(plane_second_kernel, [(half, NB)] * 8, 1, 8)(at, *got)
+    got = shift(pieces[:4], "y", 4) + shift(pieces[4:], "x", 4)
+    pieces = call(line_first_kernel, [(2, rows, NB)] * 4, 1, 8)(at, *got)
+    got = shift(pieces, "z_lo", 4)
+    mine, theirs = shift(call(line_second_kernel, [(rows, NB)] * 2, 1, 4)(at, *got), "z_hi", 2)
+    return mine + theirs
 
 
 def tile(v):
@@ -180,7 +235,7 @@
     eliminate(0, HEAD, HEAD, upper, inverse, work)
 
 
-def middle_kernel(last, blocks, head, head_inverse, upper, inverse, work):
+def tail_kernel(rows, blocks, head, head_inverse, upper, inverse, z, work):
     h = HEAD * NB
     upper[:h, :h] = head[...]
     inverse[:h, :] = head_inverse[...]
@@ -195,11 +250,7 @@
     for i in range(HEAD, KB):
         done = upper[:h, i * NB:]
         upper[i * NB:(i + 1) * NB, i * NB:] -= mm(done[:, :NB], done, ((0,), (0,)))
-    eliminate(HEAD, last, KB, upper, inverse, work)
-
-
-def tail_kernel(first, rows, upper_in, inverse_in, upper, inverse, z, work):
-    eliminate(first, KB, KB, upper, inverse, work)
+    eliminate(HEAD, KB, KB, upper, inverse, work)
     line = lax.broadcasted_iota(jnp.int32, (G, NB), 0)
     want = jnp.where(line < OWNED, rows[0] + line, rows[1] + line - OWNED)
     lane = lax.broadcasted_iota(jnp.int32, (G, NB), 1)
@@ -215,7 +266,7 @@
     z = jnp.where(core[0] == 0, z_own[:, :half], z_sent[:, half:])
     acc = jnp.zeros((G, N), jnp.float32)
     for i in range(half // NB):
-        row = jnp.concatenate([cross[(i * KB + j) * NB:(i * KB + j + 1) * NB, :] for j in range(KB)], axis=1)
+        row = jnp.concatenate([cross[(i * KB + j) // 2, j % 2 * NB:(j % 2 + 1) * NB, :] for j in range(KB)], axis=1)
         acc = acc + mm(z[:, i * NB:(i + 1) * NB], row, ((1,), (0,)))
     out[...] = acc
 
@@ -236,61 +287,39 @@
 def on_device(view_x, view_y):
     core = lax.axis_index("core")
     core_ref = core.astype(jnp.int32).reshape(1)
-    chip = ((lax.axis_index("z_hi") * 4 + lax.axis_index("x")) * 2) * 16 + lax.axis_index("y") * 4 + lax.axis_index("z_lo")
-    rows = jnp.stack([chip * OWNED, (chip + 16) * OWNED]).astype(jnp.int32)
+    x, y, z_lo, z_hi = (lax.axis_index(a).astype(jnp.int32) for a in ("x", "y", "z_lo", "z_hi"))
+    at = jnp.stack([x, y, z_lo, z_hi])
+    chip = (z_hi * 4 + x) * 32 + y * 4 + z_lo
+    rows = jnp.stack([chip * OWNED, (chip + 16) * OWNED])
     work = pltpu.VMEM((NB, 2 * NB), jnp.float32)
-    early_rows, late_rows = len(EARLY) * NB // 16, LATE_SLOTS * NB // 16
-    part = early_rows + late_rows
-
-    with jax.named_scope("gram"):
-        mine, other = call(
-            gram_kernel, [(16, part, NB)] * 2, 1, 2, [pltpu.VMEM(view_x.shape, view_x.dtype)], flops=2 * 10**9
+
+    with jax.named_scope("sums"):
+        gram, gram_other = call(
+            gram_kernel, [(16, GRAM, NB)] * 2, 1, 2, [pltpu.VMEM(view_x.shape, view_x.dtype)], flops=2 * 10**9
         )(core_ref, view_x, view_y)
-        gram = mine + swap(other)
-    with jax.named_scope("cross"):
-        keep, give = call(cross_kernel, [(32 * NB, NB)] * 2, 1, 2, flops=10**9)(
-            core_ref, *after((view_x, view_y), mine)
+        cross, cross_other = call(cross_kernel, [(16, PART - GRAM, NB)] * 2, 1, 2, flops=10**9)(
+            core_ref, *after((view_x, view_y), gram)
         )
-        cross = keep + swap(give)
-        for axis in PLANE:
-            cross = lax.psum_scatter(cross, axis, scatter_dimension=0, tiled=True)
-    with jax.named_scope("gram"):
-        piece = jnp.sum(exchange(gram, PLANE), axis=0)
-        share = jnp.sum(exchange(piece.reshape(8, part // 8, NB), LINE), axis=0)
-    with jax.named_scope("both"):
-        both = exchange(jnp.concatenate([spread(share, 8), cross.reshape(8, -1, NB)], axis=1), LINE)
-        piece = both[:, :part // 8].reshape(part, NB)
-        early = exchange(spread(piece[:early_rows], 16), PLANE).reshape(16 * early_rows, NB)
-        both = after(both, early)
-        piece = both[:, :part // 8].reshape(part, NB)
-        late = exchange(spread(piece[early_rows:], 16), PLANE).reshape(16 * late_rows, NB)
-        cross = jnp.sum(both[:, part // 8:], axis=0)
+        share = share_of_sum(at, gram, swap(gram_other), cross, swap(cross_other))
+    with jax.named_scope("early"):
+        piece = exchange(spread(share, 8), LINE).reshape(PART, NB)
+        early = exchange(spread(piece[:EARLY_ROWS], 16), PLANE).reshape(-1, NB)
+    with jax.named_scope("late"):
+        piece = after(piece, early)
+        late = exchange(spread(piece[EARLY_ROWS:GRAM], 16), PLANE).reshape(-1, NB)
+    with jax.named_scope("cross_back"):
+        cross = exchange(spread(after(piece, late)[GRAM:], 16), PLANE)
 
     head, head_inverse = call(
         head_kernel, [(HEAD * NB, HEAD * NB), (HEAD * NB, NB)], 0, 1, [work], flops=3 * 10**10
     )(early)
-    with jax.named_scope("cross_back"):
-        cross = after(cross, head)
-        cross = exchange(spread(cross, 8), LINE).reshape(256, NB)
-    upper, inverse = call(
-        functools.partial(middle_kernel, 5), [(N, N), (N, NB)], 0, 3, [work], flops=10**10
-    )(late, head, head_inverse)
-    with jax.named_scope("cross_back"):
-        cross = exchange(spread(after(cross, upper), 16), PLANE).reshape(32 * NB, NB)
-    upper, inverse, z = pl.pallas_call(
-        functools.partial(tail_kernel, 5),
-        out_shape=[jax.ShapeDtypeStruct(s, jnp.float32) for s in ((N, N), (N, NB), (G, N))],
-        in_specs=[SMEM, VMEM, VMEM],
-        out_specs=[VMEM] * 3,
-        scratch_shapes=[work],
-        input_output_aliases={1: 0, 2: 1},
-        compiler_params=pltpu.CompilerParams(vmem_limit_bytes=16 << 20),
-        cost_estimate=pl.CostEstimate(flops=3 * 10**10, bytes_accessed=0, transcendentals=0),
-    )(rows, upper, inverse)
+    upper, inverse, z = call(tail_kernel, [(N, N), (N, NB), (G, N)], 1, 3, [work], flops=4 * 10**10)(
+        rows, late, head, head_inverse
+    )
     (w,) = call(apply_kernel, [(G, N)], 1, 3)(core_ref, z, swap(z), cross)
-    (y,) = call(solve_kernel, [(G, N)], 0, 4)(w, swap(w), upper, inverse)
-    y_sent = swap(y[:OWNED])
-    return jnp.where(core == 0, y_sent, y[OWNED:])
+    (y_rows,) = call(solve_kernel, [(G, N)], 0, 4)(w, swap(w), upper, inverse)
+    y_sent = swap(y_rows[:OWNED])
+    return jnp.where(core == 0, y_sent, y_rows[OWNED:])
 
 
 def solution(mesh):

time: 241 us -> 207 us (0.86)
  waiting for transfers between devices: 79.3 us -> 52.9 us
  starting transfers between devices: 34.7 us -> 56.3 us
  blocking collectives: 32.3 us -> 15.5 us
  between operations: 13.6 us -> 0.15 us
  Pallas kernels: 56.3 us -> 63.7 us
  other arithmetic: 6.87 us -> 0.77 us
    reduce_scatter x2 -> x0, waiting for transfers between devices: 59.1 us -> none  [on_device(): cross = lax.psum_scatter(cross, axis, scatter_dimension=0, tiled=True)]
    ppermute x0 -> x16, waiting for transfers between devices: none -> 34.5 us  [shift(): lax.ppermute(p, axis, [(i, (i + k) % size) for i in range(size)])]
    ppermute x0 -> x16, starting transfers between devices: none -> 27.5 us  [shift(): lax.ppermute(p, axis, [(i, (i + k) % size) for i in range(size)])]
    all_to_all x2 -> x1, blocking collectives: 32.3 us -> 15.5 us  [exchange(): return lax.all_to_all(pieces, axes, 0, 0, tiled=True)]
    all_to_all x5 -> x3, starting transfers between devices: 25.2 us -> 18.5 us  [exchange(): return lax.all_to_all(pieces, axes, 0, 0, tiled=True)]
    pallas_call x1, Pallas kernels: 19.5 us -> 25 us  [on_device(): call(head_kernel, [(HEAD * NB, HEAD * NB), (HEAD * NB, NB)], 0, 1, [work]...]
    add x2 -> x1, other arithmetic: 5.1 us -> 0.01 us  [share_of_sum(): return mine + theirs]
    pallas_call x5 -> x8, Pallas kernels: 35.8 us -> 37.7 us  [the longest x1 24.6 us: on_device(): call(tail_kernel, [(N, N), (N, NB), (G, N)], 1, 3, [work], flops=4 * 10 *...]
  transfers between devices with their start and end apart: 12 -> 24, of which waited for: 9 -> 17; matrix products, arithmetic and copies ran while one was open for 2% -> 0% of each run, Pallas kernels for 20% -> 25%
where the time goes in v3:
time: 207 us
  Pallas kernels  63.7 us (31%)
  starting transfers between devices  56.3 us (27%)
  waiting for transfers between devices  52.9 us (26%)
  local copies, waits for them, and re-layouts  17.5 us (8%)
  blocking collectives  15.5 us (7%)
    ppermute x16, waiting for transfers between devices, shift(): lax.ppermute(p, axis, [(i, (i + k) % size) for i in range(size)])  34.5 us
    ppermute x16, starting transfers between devices, shift(): lax.ppermute(p, axis, [(i, (i + k) % size) for i in range(size)])  27.5 us
    pallas_call x1, Pallas kernels, on_device(): call(head_kernel, [(HEAD * NB, HEAD * NB), (HEAD * NB, NB)], 0, 1, [work]...  25 us
    pallas_call x1, Pallas kernels, on_device(): call(tail_kernel, [(N, N), (N, NB), (G, N)], 1, 3, [work], flops=4 * 10 *...  24.6 us
    all_to_all x3, starting transfers between devices, exchange(): return lax.all_to_all(pieces, axes, 0, 0, tiled=True)  18.5 us
    all_to_all x1, blocking collectives, exchange(): return lax.all_to_all(pieces, axes, 0, 0, tiled=True)  15.5 us
    unnamed x20, local copies, waits for them, and re-layouts  13.4 us
    all_to_all x3, waiting for transfers between devices, exchange(): return lax.all_to_all(pieces, axes, 0, 0, tiled=True)  11.5 us
  transfers between devices with their start and end apart: 24, of which 17 were waited for; matrix products, arithmetic and copies ran while one was open for 0% of the time, Pallas kernels for 25%

profile of v3, /device:TPU:1, one launch (start us, length us, event | category | flops | bytes accessed | tf_op | source)
XLA Modules:
  0.0 206.8 jit_solution(18068404973074856643)
XLA Ops:
  2.1 2.7 %sums.6 = (f32[16,320,128]{2,1,0:T(8,128)S(1)}, f32[16,320,128]{2,1,0:T(8,128)}) custom-call(s32[1]{0:T(128)} %bitcast.core, bf16[256,1024]{1,0:T(8,128)(2,1)S(1)} %copy-done.6, bf16[256,1024]{1,0:T(8,128)(2,1)S(1)} %copy-done.7), custom_call_target="tpu_custom_call" | custom-call | flops 2000000000 | tf_op jit(solution)/shard_map/sums/pallas_call | solution.py:297
  4.7 3.3 %collective-permute-start = (f32[16,320,128]{2,1,0:T(8,128)}, f32[16,320,128]{2,1,0:T(8,128)}, u32[]{:S(2)}, u32[]{:S(2)}) collective-permute-start(f32[16,320,128]{2,1,0:T(8,128)} %get-tuple-element.41), channel_id=1, source_target_pairs={{0,16},{16,0},{1,17},{17,1},{2,18},{18,2},{3,19},{19,3},{4,20},{20... | collective-permute-start | bytes 7864328 | tf_op jit(solution)/shard_map/sums/ppermute | solution.py:98
  8.0 2.1 %sums.7 = (f32[16,256,128]{2,1,0:T(8,128)S(1)}, f32[16,256,128]{2,1,0:T(8,128)}) custom-call(s32[1]{0:T(128)} %bitcast.core, bf16[256,1024]{1,0:T(8,128)(2,1)S(1)} %copy-done.6, bf16[256,1024]{1,0:T(8,128)(2,1)S(1)} %copy-done.7), custom_call_target="tpu_custom_call" | custom-call | flops 1000000000 | tf_op jit(solution)/shard_map/sums/pallas_call | solution.py:300
  11.5 4.4 %collective-permute-done.1.cross_got = f32[16,256,128]{2,1,0:T(8,128)} collective-permute-done((f32[16,256,128]{2,1,0:T(8,128)}, f32[16,256,128]{2,1,0:T(8,128)}, u32[]{:S(2)}, u32[]{:S(2)}) %collective-permute-start.1) | collective-permute-done | bytes 2097184 | tf_op jit(solution)/shard_map/sums/ppermute | solution.py:98
  16.0 1.6 copy-done.3
  17.5 2.9 %sums.8 = (f32[4,288,128]{2,1,0:T(8,128)S(1)}, f32[4,288,128]{2,1,0:T(8,128)S(1)}, f32[4,288,128]{2,1,0:T(8,128)S(1)}, f32[4,288,128]{2,1,0:T(8,128)S(1)}, f32[4...) custom-call(s32[4]{0:T(128)S(1)} %pad_add_fusion.1.at, ...), custom_call_target="tpu_custom_call" | custom-call | tf_op jit(solution)/shard_map/sums/pallas_call | solution.py:144
  20.5 1.9 collective-permute-start.3
  24.9 2.6 %collective-permute-start.6 = (f32[4,288,128]{2,1,0:T(8,128)S(1)}, f32[4,288,128]{2,1,0:T(8,128)S(1)}, u32[]{:S(2)}, u32[]{:S(2)}) collective-permute-start(f32[4,288,128]{2,1,0:T(8,128)S(1)} %get-tuple-element.52), channel_id=1, source_target_pairs={{0,8},{4,12},{8,0},{12,4},{1,9},{5,13},{9,1},{13,5},{2,10},{6,14},... | collective-permute-start | bytes 1769480 | tf_op jit(solution)/shard_map/sums/ppermute | solution.py:103
  27.5 9.6 %collective-permute-done.2.refs_1_ = f32[4,288,128]{2,1,0:T(8,128)S(1)} collective-permute-done((f32[4,288,128]{2,1,0:T(8,128)S(1)}, f32[4,288,128]{2,1,0:T(8,128)S(1)}, u32[]{:S(2)}, u32[]{:S(2)}) %collective-permute-start.2) | collective-permute-done | bytes 589856 | tf_op jit(solution)/shard_map/sums/ppermute | solution.py:103
  37.3 10.9 %collective-permute-done.3.refs_2_ = f32[4,288,128]{2,1,0:T(8,128)S(1)} collective-permute-done((f32[4,288,128]{2,1,0:T(8,128)S(1)}, f32[4,288,128]{2,1,0:T(8,128)S(1)}, u32[]{:S(2)}, u32[]{:S(2)}) %collective-permute-start.3) | collective-permute-done | bytes 589856 | tf_op jit(solution)/shard_map/sums/ppermute | solution.py:103
  49.3 3.1 %collective-permute-done.6.refs_6_ = f32[4,288,128]{2,1,0:T(8,128)S(1)} collective-permute-done((f32[4,288,128]{2,1,0:T(8,128)S(1)}, f32[4,288,128]{2,1,0:T(8,128)S(1)}, u32[]{:S(2)}, u32[]{:S(2)}) %collective-permute-start.6) | collective-permute-done | bytes 589856 | tf_op jit(solution)/shard_map/sums/ppermute | solution.py:103
  53.1 3.3 %collective-permute-start.8 = (f32[288,128]{1,0:T(8,128)S(1)}, f32[288,128]{1,0:T(8,128)S(1)}, u32[]{:S(2)}, u32[]{:S(2)}) collective-permute-start(f32[288,128]{1,0:T(8,128)S(1)} %get-tuple-element.55), channel_id=1, source_target_pairs={{0,4},{4,8},{8,12},{12,0},{1,5},{5,9},{9,13},{13,1},{2,6},{6,10},{... | collective-permute-start | bytes 442376 | tf_op jit(solution)/shard_map/sums/ppermute | solution.py:103
  56.4 2.5 %collective-permute-start.10 = (f32[288,128]{1,0:T(8,128)S(1)}, f32[288,128]{1,0:T(8,128)S(1)}, u32[]{:S(2)}, u32[]{:S(2)}) collective-permute-start(f32[288,128]{1,0:T(8,128)S(1)} %get-tuple-element.57), channel_id=1, source_target_pairs={{0,12},{4,0},{8,4},{12,8},{1,13},{5,1},{9,5},{13,9},{2,14},{6,2},{... | collective-permute-start | bytes 442376 | tf_op jit(solution)/shard_map/sums/ppermute | solution.py:103
  59.7 1.9 collective-permute-start.13
  62.5 3.3 %collective-permute-done.11.refs_5_ = f32[288,128]{1,0:T(8,128)S(1)} collective-permute-done((f32[288,128]{1,0:T(8,128)S(1)}, f32[288,128]{1,0:T(8,128)S(1)}, u32[]{:S(2)}, u32[]{:S(2)}) %collective-permute-start.11) | collective-permute-done | bytes 147488 | tf_op jit(solution)/shard_map/sums/ppermute | solution.py:103
  66.9 2.9 %collective-permute-start.14 = (f32[2,72,128]{2,1,0:T(8,128)S(1)}, f32[2,72,128]{2,1,0:T(8,128)S(1)}, u32[]{:S(2)}, u32[]{:S(2)}) collective-permute-start(f32[2,72,128]{2,1,0:T(8,128)S(1)} %get-tuple-element.63), channel_id=1, source_target_pairs={{0,1},{1,2},{2,3},{3,0},{4,5},{5,6},{6,7},{7,4},{8,9},{9,10},{10,1... | collective-permute-start | bytes 221192 | tf_op jit(solution)/shard_map/sums/ppermute | solution.py:103
  69.8 3.0 %collective-permute-start.15 = (f32[2,72,128]{2,1,0:T(8,128)S(1)}, f32[2,72,128]{2,1,0:T(8,128)S(1)}, u32[]{:S(2)}, u32[]{:S(2)}) collective-permute-start(f32[2,72,128]{2,1,0:T(8,128)S(1)} %get-tuple-element.64), channel_id=1, source_target_pairs={{0,2},{1,3},{2,0},{3,1},{4,6},{5,7},{6,4},{7,5},{8,10},{9,11},{10,... | collective-permute-start | bytes 221192 | tf_op jit(solution)/shard_map/sums/ppermute | solution.py:103
  74.4 1.6 collective-permute-done.15.c
  77.2 5.0 %collective-permute-start.17 = (f32[72,128]{1,0:T(8,128)S(1)}, f32[72,128]{1,0:T(8,128)S(1)}, u32[]{:S(2)}, u32[]{:S(2)}) collective-permute-start(f32[72,128]{1,0:T(8,128)S(1)} %get-tuple-element.67), channel_id=1, source_target_pairs={{0,128},{128,0},{1,129},{129,1},{2,130},{130,2},{3,131},{131,3},{4... | collective-permute-start | bytes 110600 | tf_op jit(solution)/shard_map/sums/ppermute | solution.py:103
  82.2 2.2 %collective-permute-done.17 = f32[72,128]{1,0:T(8,128)S(1)} collective-permute-done((f32[72,128]{1,0:T(8,128)S(1)}, f32[72,128]{1,0:T(8,128)S(1)}, u32[]{:S(2)}, u32[]{:S(2)}) %collective-permute-start.17) | collective-permute-done | bytes 36896 | tf_op jit(solution)/shard_map/sums/ppermute | solution.py:103
  84.4 15.5 %all_to_all.20 = f32[8,72,128]{2,1,0:T(8,128)S(1)} all-to-all(f32[8,72,128]{2,1,0:T(8,128)S(1)} %broadcast_in_dim.8), channel_id=1, replica_groups=mesh['z_hi'=2,'x'=4,'core'=2,'y'=4,'z_lo'=4] {'z_hi','z_lo'}, dimensions={0} | all-to-all | bytes 589824 | tf_op jit(solution)/shard_map/early/all_to_all | solution.py:90
  100.9 8.1 %all-to-all-start.1 = ((f32[16,120,128]{2,1,0:T(8,128)}), f32[16,120,128]{2,1,0:T(8,128)S(1)}, u32[]{:S(2)}, u32[]{:S(2)}) async-start(f32[16,120,128]{2,1,0:T(8,128)} %broadcast_in_dim.9), calls=%async_computation.1 | async-start | bytes 1966080 | tf_op jit(solution)/shard_map/early/all_to_all | solution.py:90
  109.1 11.5 %all-to-all-done.1 = f32[16,120,128]{2,1,0:T(8,128)S(1)} async-done(((f32[16,120,128]{2,1,0:T(8,128)}), f32[16,120,128]{2,1,0:T(8,128)S(1)}, u32[]{:S(2)}, u32[]{:S(2)}) %all-to-all-start.1) | async-done | bytes 983072 | tf_op jit(solution)/shard_map/early/all_to_all | solution.py:90
  121.9 3.7 %all-to-all-start.2 = ((f32[16,200,128]{2,1,0:T(8,128)}), f32[16,200,128]{2,1,0:T(8,128)S(1)}, u32[]{:S(2)}, u32[]{:S(2)}) async-start(f32[16,200,128]{2,1,0:T(8,128)} %broadcast_in_dim.10), calls=%async_computation.2 | async-start | bytes 3276800 | tf_op jit(solution)/shard_map/late/all_to_all | solution.py:90
  125.6 25.0 %shard_map.28 = (f32[640,640]{1,0:T(8,128)S(1)}, f32[640,128]{1,0:T(8,128)S(1)}) custom-call(f32[1920,128]{1,0:T(8,128)S(1)} %bitcast.11), custom_call_target="tpu_custom_call" | custom-call | flops 30000001024 | tf_op jit(solution)/shard_map/pallas_call | solution.py:313
  151.8 1.7 broadcast_in_dim.11
  153.7 6.7 %all-to-all-start.3 = ((f32[16,256,128]{2,1,0:T(8,128)}), f32[16,256,128]{2,1,0:T(8,128)S(1)}, u32[]{:S(2)}, u32[]{:S(2)}) async-start(f32[16,256,128]{2,1,0:T(8,128)} %broadcast_in_dim.11), calls=%async_computation.3 | async-start | bytes 4194304 | tf_op jit(solution)/shard_map/cross_back/all_to_all | solution.py:90
  163.2 24.6 %shard_map.29 = (f32[1024,1024]{1,0:T(8,128)S(1)}, f32[1024,128]{1,0:T(8,128)S(1)}, f32[8,1024]{1,0:T(8,128)S(1)}) custom-call(s32[2]{0:T(128)S(1)} %pad_add_fusion.rows, f32[3200,128]{1,0:T(8,128)S(1)} %bitcast.10, f32[640,640]{1,0:T(8,128)S(1)} %copy-done.9, f32[640,128]{1,0:T(8,128)S(1)} %get-tuple-element.70.head_inverse), custom_call_target="tpu_custom_call" | custom-call | flops 40000000000 | tf_op jit(solution)/shard_map/pallas_call | solution.py:316
  187.8 2.0 copy-done
  189.8 6.3 %collective-permute-start.18 = (f32[8,1024]{1,0:T(8,128)S(1)}, f32[8,1024]{1,0:T(8,128)S(1)}, u32[]{:S(2)}, u32[]{:S(2)}) collective-permute-start(f32[8,1024]{1,0:T(8,128)S(1)} %get-tuple-element.71.z_own), channel_id=1, source_target_pairs={{0,16},{16,0},{1,17},{17,1},{2,18},{18,2},{3,19},{19,3},{4,20},{20... | collective-permute-start | bytes 98312 | tf_op jit(solution)/shard_map/ppermute | solution.py:98
  199.2 2.2 %copy-done.1 = f32[1024,1024]{1,0:T(8,128)S(1)} copy-done((f32[1024,1024]{1,0:T(8,128)S(1)}, f32[1024,1024]{1,0:T(8,128)}, u32[]{:S(2)}) %copy-start.1) | copy-done | bytes 4194328
  201.3 3.6 %shard_map.31 = f32[8,1024]{1,0:T(8,128)S(1)} custom-call(f32[8,1024]{1,0:T(8,128)S(1)} %shard_map.30.w_own, f32[8,1024]{1,0:T(8,128)S(1)} %collective-permute-done.19.w_sent, f32[1024,1024]{1,0:T(8,128)S(1)} %copy-done.1, f32[1024,128]{1,0:T(8,128)S(1)} %get-tuple-element.74.inverse), custom_call_target="tpu_custom_call" | custom-call | tf_op jit(solution)/shard_map/pallas_call | solution.py:320
  (59 shorter events, 25.1 us)
Async XLA Ops:
  4.7 11.2 %collective-permute-start = (f32[16,320,128]{2,1,0:T(8,128)}, f32[16,320,128]{2,1,0:T(8,128)}, u32[]{:S(2)}, u32[]{:S(2)}) collective-permute-start(f32[16,320,128]{2,1,0:T(8,128)} %get-tuple-element.41), channel_id=1, source_target_pairs={{0,16},{16,0},{1,17},{17,1},{2,18},{18,2},{3,19},{19,3},{4,20},{20... | collective-permute-start | bytes 7864328 | tf_op jit(solution)/shard_map/sums/ppermute | solution.py:98
  10.1 1.4 copy-start.2
  11.4 4.5 %collective-permute-start.1 = (f32[16,256,128]{2,1,0:T(8,128)}, f32[16,256,128]{2,1,0:T(8,128)}, u32[]{:S(2)}, u32[]{:S(2)}) collective-permute-start(f32[16,256,128]{2,1,0:T(8,128)} %get-tuple-element.45), channel_id=1, source_target_pairs={{0,16},{16,0},{1,17},{17,1},{2,18},{18,2},{3,19},{19,3},{4,20},{20... | collective-permute-start | bytes 6291464 | tf_op jit(solution)/shard_map/sums/ppermute | solution.py:98
  16.0 1.6 copy-start.3
  20.4 16.6 %collective-permute-start.2 = (f32[4,288,128]{2,1,0:T(8,128)S(1)}, f32[4,288,128]{2,1,0:T(8,128)S(1)}, u32[]{:S(2)}, u32[]{:S(2)}) collective-permute-start(f32[4,288,128]{2,1,0:T(8,128)S(1)} %get-tuple-element.47), channel_id=1, source_target_pairs={{0,32},{32,64},{64,96},{96,0},{1,33},{33,65},{65,97},{97,1},{2,34}... | collective-permute-start | bytes 1769480 | tf_op jit(solution)/shard_map/sums/ppermute | solution.py:103
  20.5 27.7 %collective-permute-start.3 = (f32[4,288,128]{2,1,0:T(8,128)S(1)}, f32[4,288,128]{2,1,0:T(8,128)S(1)}, u32[]{:S(2)}, u32[]{:S(2)}) collective-permute-start(f32[4,288,128]{2,1,0:T(8,128)S(1)} %get-tuple-element.48), channel_id=1, source_target_pairs={{0,64},{32,96},{64,0},{96,32},{1,65},{33,97},{65,1},{97,33},{2,66}... | collective-permute-start | bytes 1769480 | tf_op jit(solution)/shard_map/sums/ppermute | solution.py:103
  22.4 26.8 %collective-permute-start.4 = (f32[4,288,128]{2,1,0:T(8,128)S(1)}, f32[4,288,128]{2,1,0:T(8,128)S(1)}, u32[]{:S(2)}, u32[]{:S(2)}) collective-permute-start(f32[4,288,128]{2,1,0:T(8,128)S(1)} %get-tuple-element.49), channel_id=1, source_target_pairs={{0,96},{32,0},{64,32},{96,64},{1,97},{33,1},{65,33},{97,65},{2,98}... | collective-permute-start | bytes 1769480 | tf_op jit(solution)/shard_map/sums/ppermute | solution.py:103
  23.6 25.7 %collective-permute-start.5 = (f32[4,288,128]{2,1,0:T(8,128)S(1)}, f32[4,288,128]{2,1,0:T(8,128)S(1)}, u32[]{:S(2)}, u32[]{:S(2)}) collective-permute-start(f32[4,288,128]{2,1,0:T(8,128)S(1)} %get-tuple-element.51), channel_id=1, source_target_pairs={{0,4},{4,8},{8,12},{12,0},{1,5},{5,9},{9,13},{13,1},{2,6},{6,10},{... | collective-permute-start | bytes 1769480 | tf_op jit(solution)/shard_map/sums/ppermute | solution.py:103
  24.9 27.5 %collective-permute-start.6 = (f32[4,288,128]{2,1,0:T(8,128)S(1)}, f32[4,288,128]{2,1,0:T(8,128)S(1)}, u32[]{:S(2)}, u32[]{:S(2)}) collective-permute-start(f32[4,288,128]{2,1,0:T(8,128)S(1)} %get-tuple-element.52), channel_id=1, source_target_pairs={{0,8},{4,12},{8,0},{12,4},{1,9},{5,13},{9,1},{13,5},{2,10},{6,14},... | collective-permute-start | bytes 1769480 | tf_op jit(solution)/shard_map/sums/ppermute | solution.py:103
  37.1 15.3 %collective-permute-start.7 = (f32[4,288,128]{2,1,0:T(8,128)S(1)}, f32[4,288,128]{2,1,0:T(8,128)S(1)}, u32[]{:S(2)}, u32[]{:S(2)}) collective-permute-start(f32[4,288,128]{2,1,0:T(8,128)S(1)} %get-tuple-element.53), channel_id=1, source_target_pairs={{0,12},{4,0},{8,4},{12,8},{1,13},{5,1},{9,5},{13,9},{2,14},{6,2},{... | collective-permute-start | bytes 1769480 | tf_op jit(solution)/shard_map/sums/ppermute | solution.py:103
  53.1 6.6 %collective-permute-start.8 = (f32[288,128]{1,0:T(8,128)S(1)}, f32[288,128]{1,0:T(8,128)S(1)}, u32[]{:S(2)}, u32[]{:S(2)}) collective-permute-start(f32[288,128]{1,0:T(8,128)S(1)} %get-tuple-element.55), channel_id=1, source_target_pairs={{0,4},{4,8},{8,12},{12,0},{1,5},{5,9},{9,13},{13,1},{2,6},{6,10},{... | collective-permute-start | bytes 442376 | tf_op jit(solution)/shard_map/sums/ppermute | solution.py:103
  56.4 5.5 %collective-permute-start.9 = (f32[288,128]{1,0:T(8,128)S(1)}, f32[288,128]{1,0:T(8,128)S(1)}, u32[]{:S(2)}, u32[]{:S(2)}) collective-permute-start(f32[288,128]{1,0:T(8,128)S(1)} %get-tuple-element.56), channel_id=1, source_target_pairs={{0,8},{4,12},{8,0},{12,4},{1,9},{5,13},{9,1},{13,5},{2,10},{6,14},... | collective-permute-start | bytes 442376 | tf_op jit(solution)/shard_map/sums/ppermute | solution.py:103
  56.4 6.0 %collective-permute-start.10 = (f32[288,128]{1,0:T(8,128)S(1)}, f32[288,128]{1,0:T(8,128)S(1)}, u32[]{:S(2)}, u32[]{:S(2)}) collective-permute-start(f32[288,128]{1,0:T(8,128)S(1)} %get-tuple-element.57), channel_id=1, source_target_pairs={{0,12},{4,0},{8,4},{12,8},{1,13},{5,1},{9,5},{13,9},{2,14},{6,2},{... | collective-permute-start | bytes 442376 | tf_op jit(solution)/shard_map/sums/ppermute | solution.py:103
  58.9 6.8 %collective-permute-start.11 = (f32[288,128]{1,0:T(8,128)S(1)}, f32[288,128]{1,0:T(8,128)S(1)}, u32[]{:S(2)}, u32[]{:S(2)}) collective-permute-start(f32[288,128]{1,0:T(8,128)S(1)} %get-tuple-element.59), channel_id=1, source_target_pairs={{0,32},{32,64},{64,96},{96,0},{1,33},{33,65},{65,97},{97,1},{2,34}... | collective-permute-start | bytes 442376 | tf_op jit(solution)/shard_map/sums/ppermute | solution.py:103
  59.2 6.5 %collective-permute-start.12 = (f32[288,128]{1,0:T(8,128)S(1)}, f32[288,128]{1,0:T(8,128)S(1)}, u32[]{:S(2)}, u32[]{:S(2)}) collective-permute-start(f32[288,128]{1,0:T(8,128)S(1)} %get-tuple-element.60), channel_id=1, source_target_pairs={{0,64},{32,96},{64,0},{96,32},{1,65},{33,97},{65,1},{97,33},{2,66}... | collective-permute-start | bytes 442376 | tf_op jit(solution)/shard_map/sums/ppermute | solution.py:103
  59.7 6.6 %collective-permute-start.13 = (f32[288,128]{1,0:T(8,128)S(1)}, f32[288,128]{1,0:T(8,128)S(1)}, u32[]{:S(2)}, u32[]{:S(2)}) collective-permute-start(f32[288,128]{1,0:T(8,128)S(1)} %get-tuple-element.61), channel_id=1, source_target_pairs={{0,96},{32,0},{64,32},{96,64},{1,97},{33,1},{65,33},{97,65},{2,98}... | collective-permute-start | bytes 442376 | tf_op jit(solution)/shard_map/sums/ppermute | solution.py:103
  66.9 7.4 %collective-permute-start.14 = (f32[2,72,128]{2,1,0:T(8,128)S(1)}, f32[2,72,128]{2,1,0:T(8,128)S(1)}, u32[]{:S(2)}, u32[]{:S(2)}) collective-permute-start(f32[2,72,128]{2,1,0:T(8,128)S(1)} %get-tuple-element.63), channel_id=1, source_target_pairs={{0,1},{1,2},{2,3},{3,0},{4,5},{5,6},{6,7},{7,4},{8,9},{9,10},{10,1... | collective-permute-start | bytes 221192 | tf_op jit(solution)/shard_map/sums/ppermute | solution.py:103
  69.8 6.1 %collective-permute-start.15 = (f32[2,72,128]{2,1,0:T(8,128)S(1)}, f32[2,72,128]{2,1,0:T(8,128)S(1)}, u32[]{:S(2)}, u32[]{:S(2)}) collective-permute-start(f32[2,72,128]{2,1,0:T(8,128)S(1)} %get-tuple-element.64), channel_id=1, source_target_pairs={{0,2},{1,3},{2,0},{3,1},{4,6},{5,7},{6,4},{7,5},{8,10},{9,11},{10,... | collective-permute-start | bytes 221192 | tf_op jit(solution)/shard_map/sums/ppermute | solution.py:103
  72.8 3.8 %collective-permute-start.16 = (f32[2,72,128]{2,1,0:T(8,128)S(1)}, f32[2,72,128]{2,1,0:T(8,128)S(1)}, u32[]{:S(2)}, u32[]{:S(2)}) collective-permute-start(f32[2,72,128]{2,1,0:T(8,128)S(1)} %get-tuple-element.65), channel_id=1, source_target_pairs={{0,3},{1,0},{2,1},{3,2},{4,7},{5,4},{6,5},{7,6},{8,11},{9,8},{10,9... | collective-permute-start | bytes 221192 | tf_op jit(solution)/shard_map/sums/ppermute | solution.py:103
  77.2 7.2 %collective-permute-start.17 = (f32[72,128]{1,0:T(8,128)S(1)}, f32[72,128]{1,0:T(8,128)S(1)}, u32[]{:S(2)}, u32[]{:S(2)}) collective-permute-start(f32[72,128]{1,0:T(8,128)S(1)} %get-tuple-element.67), channel_id=1, source_target_pairs={{0,128},{128,0},{1,129},{129,1},{2,130},{130,2},{3,131},{131,3},{4... | collective-permute-start | bytes 110600 | tf_op jit(solution)/shard_map/sums/ppermute | solution.py:103
  100.9 19.7 %all-to-all-start.1 = ((f32[16,120,128]{2,1,0:T(8,128)}), f32[16,120,128]{2,1,0:T(8,128)S(1)}, u32[]{:S(2)}, u32[]{:S(2)}) async-start(f32[16,120,128]{2,1,0:T(8,128)} %broadcast_in_dim.9), calls=%async_computation.1 | async-start | bytes 1966080 | tf_op jit(solution)/shard_map/early/all_to_all | solution.py:90
  121.9 29.9 %all-to-all-start.2 = ((f32[16,200,128]{2,1,0:T(8,128)}), f32[16,200,128]{2,1,0:T(8,128)S(1)}, u32[]{:S(2)}, u32[]{:S(2)}) async-start(f32[16,200,128]{2,1,0:T(8,128)} %broadcast_in_dim.10), calls=%async_computation.2 | async-start | bytes 3276800 | tf_op jit(solution)/shard_map/late/all_to_all | solution.py:90
  150.6 1.2 copy-start.8
  151.8 1.9 copy-start.4
  153.7 43.3 %all-to-all-start.3 = ((f32[16,256,128]{2,1,0:T(8,128)}), f32[16,256,128]{2,1,0:T(8,128)S(1)}, u32[]{:S(2)}, u32[]{:S(2)}) async-start(f32[16,256,128]{2,1,0:T(8,128)} %broadcast_in_dim.11), calls=%async_computation.3 | async-start | bytes 4194304 | tf_op jit(solution)/shard_map/cross_back/all_to_all | solution.py:90
  160.4 1.4 copy-start.5
  161.8 1.4 copy-start.9
  187.8 2.0 copy-start
  189.8 7.2 %collective-permute-start.18 = (f32[8,1024]{1,0:T(8,128)S(1)}, f32[8,1024]{1,0:T(8,128)S(1)}, u32[]{:S(2)}, u32[]{:S(2)}) collective-permute-start(f32[8,1024]{1,0:T(8,128)S(1)} %get-tuple-element.71.z_own), channel_id=1, source_target_pairs={{0,16},{16,0},{1,17},{17,1},{2,18},{18,2},{3,19},{19,3},{4,20},{20... | collective-permute-start | bytes 98312 | tf_op jit(solution)/shard_map/ppermute | solution.py:98
  197.9 1.2 collective-permute-start.19
  199.2 2.2 %copy-start.1 = (f32[1024,1024]{1,0:T(8,128)S(1)}, f32[1024,1024]{1,0:T(8,128)}, u32[]{:S(2)}) copy-start(f32[1024,1024]{1,0:T(8,128)} %copy-done) | copy-start | bytes 12582916
  205.0 1.2 collective-permute-start.20
  (2 other events, 2.1 us)

commit v4 on v3

--- a/solution.py
+++ b/solution.py
@@ -98,56 +98,64 @@
     return lax.ppermute(a, "core", [(0, 1), (1, 0)])
 
 
-def shift(pieces, axis, size):
+def plane_route(k, step):
     return [
-        lax.ppermute(p, axis, [(i, (i + k) % size) for i in range(size)]) if k else p for k, p in enumerate(pieces)
+        ((x * 2 + c) * 4 + y, ((x + k) % 4 * 2 + c) * 4 + y if c == step else (x * 2 + c) * 4 + (y + k) % 4)
+        for x in range(4) for c in range(2) for y in range(4)
     ]
 
 
+def shift(pieces, axes, route):
+    return [lax.ppermute(p, axes, route(k)) if k else p for k, p in enumerate(pieces)]
+
+
+def along_plane(pieces, step):
+    return shift(pieces, ("x", "core", "y"), lambda k: plane_route(k, step))
+
+
+def along_line(pieces, axis):
+    size = len(pieces)
+    return shift(pieces, axis, lambda k: [(i, (i + k) % size) for i in range(size)])
+
+
 def plane_first_kernel(at, gram, gram_got, cross, cross_got, *outs):
-    x, y, cut = at[0], at[1], PART // 2
     for k in range(4):
         for j in range(4):
-            p = ((x + k) & 3) * 4 + j
-            outs[k][j] = gram[p, :cut] + gram_got[p, :cut]
-            p = j * 4 + ((y + k) & 3)
-            outs[4 + k][j, :GRAM - cut] = gram[p, cut:] + gram_got[p, cut:]
-            outs[4 + k][j, GRAM - cut:] = cross[p] + cross_got[p]
-
-
-def plane_second_kernel(at, *refs):
-    ins, outs = refs[:8], refs[8:]
+            p = ((at[0] + k) & 3) * at[2] + j * at[3]
+            outs[k][j, :GRAM] = gram[p] + gram_got[p]
+            outs[k][j, GRAM:] = cross[p] + cross_got[p]
+
+
+def plane_second_kernel(at, a, b, c, d, *outs):
     for k in range(4):
-        for base, me in ((0, at[1]), (4, at[0])):
-            p = (me + k) & 3
-            outs[base + k][...] = (ins[base][p] + ins[base + 1][p]) + (ins[base + 2][p] + ins[base + 3][p])
+        p = (at[1] + k) & 3
+        outs[k][...] = (a[p] + b[p]) + (c[p] + d[p])
 
 
 def line_first_kernel(at, *refs):
-    ins, outs = refs[:8], refs[8:]
+    ins, outs = refs[:4], refs[4:]
     rows = PART // 8
     for k in range(4):
-        lines = pl.ds(pl.multiple_of(((at[2] + k) & 3) * rows, 8), rows)
         for h in range(2):
-            a, b, c, d = (r[lines, :] for r in ins[4 * h:4 * h + 4])
+            start = (h * 4 + ((at[4] + k) & 3)) * rows
+            lines = pl.ds(pl.multiple_of(start, 8), rows)
+            a, b, c, d = (r[lines, :] for r in ins)
             outs[k][h] = (a + b) + (c + d)
 
 
 def line_second_kernel(at, a, b, c, d, *outs):
     for k in range(2):
-        h = (at[3] + k) & 1
+        h = (at[5] + k) & 1
         outs[k][...] = (a[h] + b[h]) + (c[h] + d[h])
 
 
 def share_of_sum(at, gram, gram_got, cross, cross_got):
-    half, rows = PART // 2, PART // 8
-    pieces = call(plane_first_kernel, [(4, half, NB)] * 8, 1, 4)(at, gram, gram_got, cross, cross_got)
-    got = shift(pieces[:4], "x", 4) + shift(pieces[4:], "y", 4)
-    pieces = call(plane_second_kernel, [(half, NB)] * 8, 1, 8)(at, *got)
-    got = shift(pieces[:4], "y", 4) + shift(pieces[4:], "x", 4)
-    pieces = call(line_first_kernel, [(2, rows, NB)] * 4, 1, 8)(at, *got)
-    got = shift(pieces, "z_lo", 4)
-    mine, theirs = shift(call(line_second_kernel, [(rows, NB)] * 2, 1, 4)(at, *got), "z_hi", 2)
+    rows = PART // 8
+    pieces = call(plane_first_kernel, [(4, PART, NB)] * 4, 1, 4)(at, gram, gram_got, cross, cross_got)
+    pieces = call(plane_second_kernel, [(PART, NB)] * 4, 1, 4)(at, *along_plane(pieces, 0))
+    pieces = call(line_first_kernel, [(2, rows, NB)] * 4, 1, 4)(at, *along_plane(pieces, 1))
+    pieces = call(line_second_kernel, [(rows, NB)] * 2, 1, 4)(at, *along_line(pieces, "z_lo"))
+    mine, theirs = along_line(pieces, "z_hi")
     return mine + theirs
 
 
@@ -288,7 +296,7 @@
     core = lax.axis_index("core")
     core_ref = core.astype(jnp.int32).reshape(1)
     x, y, z_lo, z_hi = (lax.axis_index(a).astype(jnp.int32) for a in ("x", "y", "z_lo", "z_hi"))
-    at = jnp.stack([x, y, z_lo, z_hi])
+    at = jnp.stack([*jnp.where(core == 0, jnp.array([x, y, 4, 1]), jnp.array([y, x, 1, 4])), z_lo, z_hi]).astype(jnp.int32)
     chip = (z_hi * 4 + x) * 32 + y * 4 + z_lo
     rows = jnp.stack([chip * OWNED, (chip + 16) * OWNED])
     work = pltpu.VMEM((NB, 2 * NB), jnp.float32)
@@ -301,14 +309,15 @@
             core_ref, *after((view_x, view_y), gram)
         )
         share = share_of_sum(at, gram, swap(gram_other), cross, swap(cross_other))
-    with jax.named_scope("early"):
+    with jax.named_scope("back"):
         piece = exchange(spread(share, 8), LINE).reshape(PART, NB)
-        early = exchange(spread(piece[:EARLY_ROWS], 16), PLANE).reshape(-1, NB)
-    with jax.named_scope("late"):
-        piece = after(piece, early)
-        late = exchange(spread(piece[EARLY_ROWS:GRAM], 16), PLANE).reshape(-1, NB)
-    with jax.named_scope("cross_back"):
-        cross = exchange(spread(after(piece, late)[GRAM:], 16), PLANE)
+        early, late, cross = (
+            spread(piece[lo:hi], 16) for lo, hi in ((0, EARLY_ROWS), (EARLY_ROWS, GRAM), (GRAM, PART))
+        )
+        early = after(exchange(early, PLANE), late, cross)
+        late = exchange(after(late, early), PLANE)
+        cross = exchange(after(cross, late), PLANE)
+        early, late = early.reshape(-1, NB), late.reshape(-1, NB)
 
     head, head_inverse = call(
         head_kernel, [(HEAD * NB, HEAD * NB), (HEAD * NB, NB)], 0, 1, [work], flops=3 * 10**10

time: 207 us -> 201 us (0.971)
  starting transfers between devices: 56.3 us -> 42.4 us
  waiting for transfers between devices: 52.9 us -> 58.2 us
    ppermute x16 -> x10, starting transfers between devices: 27.5 us -> 15.7 us  [shift(): lax.ppermute(p, axes, route(k))]
    ppermute x16 -> x10, waiting for transfers between devices: 34.5 us -> 39.9 us  [shift(): lax.ppermute(p, axes, route(k))]
    all_to_all x3, starting transfers between devices: 18.5 us -> 15.7 us  [exchange(): return lax.all_to_all(pieces, axes, 0, 0, tiled=True)]
  transfers between devices with their start and end apart: 24 -> 18, of which waited for: 17 -> 13; matrix products, arithmetic and copies ran while one was open for 0% -> 0% of each run, Pallas kernels for 25% -> 26%
where the time goes in v4:
time: 201 us
  Pallas kernels  63.7 us (32%)
  waiting for transfers between devices  58.2 us (29%)
  starting transfers between devices  42.4 us (21%)
  local copies, waits for them, and re-layouts  18.4 us (9%)
  blocking collectives  17.1 us (9%)
    ppermute x10, waiting for transfers between devices, shift(): lax.ppermute(p, axes, route(k))  39.9 us
    pallas_call x1, Pallas kernels, on_device(): call(head_kernel, [(HEAD * NB, HEAD * NB), (HEAD * NB, NB)], 0, 1, [work]...  25 us
    pallas_call x1, Pallas kernels, on_device(): call(tail_kernel, [(N, N), (N, NB), (G, N)], 1, 3, [work], flops=4 * 10 *...  24.6 us
    all_to_all x1, blocking collectives, exchange(): return lax.all_to_all(pieces, axes, 0, 0, tiled=True)  17.1 us
    ppermute x10, starting transfers between devices, shift(): lax.ppermute(p, axes, route(k))  15.7 us
    all_to_all x3, starting transfers between devices, exchange(): return lax.all_to_all(pieces, axes, 0, 0, tiled=True)  15.7 us
    unnamed x20, local copies, waits for them, and re-layouts  14.5 us
    all_to_all x3, waiting for transfers between devices, exchange(): return lax.all_to_all(pieces, axes, 0, 0, tiled=True)  11.4 us
  transfers between devices with their start and end apart: 18, of which 13 were waited for; matrix products, arithmetic and copies ran while one was open for 0% of the time, Pallas kernels for 26%

profile of v4, /device:TPU:1, one launch (start us, length us, event | category | flops | bytes accessed | tf_op | source)
XLA Modules:
  0.0 200.9 jit_solution(10990261718536961750)
XLA Ops:
  2.1 2.7 %sums.6 = (f32[16,320,128]{2,1,0:T(8,128)S(1)}, f32[16,320,128]{2,1,0:T(8,128)}) custom-call(s32[1]{0:T(128)} %bitcast.core, bf16[256,1024]{1,0:T(8,128)(2,1)S(1)} %copy-done.6, bf16[256,1024]{1,0:T(8,128)(2,1)S(1)} %copy-done.7), custom_call_target="tpu_custom_call" | custom-call | flops 2000000000 | tf_op jit(solution)/shard_map/sums/pallas_call | solution.py:305
  4.8 3.3 %collective-permute-start = (f32[16,320,128]{2,1,0:T(8,128)}, f32[16,320,128]{2,1,0:T(8,128)}, u32[]{:S(2)}, u32[]{:S(2)}) collective-permute-start(f32[16,320,128]{2,1,0:T(8,128)} %get-tuple-element.34), channel_id=1, source_target_pairs={{0,16},{16,0},{1,17},{17,1},{2,18},{18,2},{3,19},{19,3},{4,20},{20... | collective-permute-start | bytes 7864328 | tf_op jit(solution)/shard_map/sums/ppermute | solution.py:98
  8.0 2.1 %sums.7 = (f32[16,256,128]{2,1,0:T(8,128)S(1)}, f32[16,256,128]{2,1,0:T(8,128)}) custom-call(s32[1]{0:T(128)} %bitcast.core, bf16[256,1024]{1,0:T(8,128)(2,1)S(1)} %copy-done.6, bf16[256,1024]{1,0:T(8,128)(2,1)S(1)} %copy-done.7), custom_call_target="tpu_custom_call" | custom-call | flops 1000000000 | tf_op jit(solution)/shard_map/sums/pallas_call | solution.py:308
  10.1 1.4 copy-done.2
  11.7 4.3 %collective-permute-done.1.cross_got = f32[16,256,128]{2,1,0:T(8,128)} collective-permute-done((f32[16,256,128]{2,1,0:T(8,128)}, f32[16,256,128]{2,1,0:T(8,128)}, u32[]{:S(2)}, u32[]{:S(2)}) %collective-permute-start.1) | collective-permute-done | bytes 2097184 | tf_op jit(solution)/shard_map/sums/ppermute | solution.py:98
  16.0 1.6 copy-done.3
  17.6 2.9 %sums.8 = (f32[4,576,128]{2,1,0:T(8,128)S(1)}, f32[4,576,128]{2,1,0:T(8,128)S(1)}, f32[4,576,128]{2,1,0:T(8,128)S(1)}, f32[4,576,128]{2,1,0:T(8,128)S(1)}) custom-call(s32[6]{0:T(128)S(1)} %pad_add_fusion.1.at, f32[16,320,128]{2,1,0:T(8,128)S(1)} %get-tuple-element.33.gram, f32[16,320,128]{2,1,0:T(8,128)} %collective-permute-done.gram_got, ...), custom_call_target="tpu_custom_call" | custom-call | tf_op jit(solution)/shard_map/sums/pallas_call | solution.py:154
  20.6 2.2 %collective-permute-start.3 = (f32[4,576,128]{2,1,0:T(8,128)S(1)}, f32[4,576,128]{2,1,0:T(8,128)S(1)}, u32[]{:S(2)}, u32[]{:S(2)}) collective-permute-start(f32[4,576,128]{2,1,0:T(8,128)S(1)} %get-tuple-element.41), channel_id=1, source_target_pairs={{0,64},{4,68},{8,72},{12,76},{16,24},{20,28},{24,16},{28,20},{32,9... | collective-permute-start | bytes 3538952 | tf_op jit(solution)/shard_map/sums/ppermute | solution.py:109
  23.8 25.9 %collective-permute-done.2.b = f32[4,576,128]{2,1,0:T(8,128)S(1)} collective-permute-done((f32[4,576,128]{2,1,0:T(8,128)S(1)}, f32[4,576,128]{2,1,0:T(8,128)S(1)}, u32[]{:S(2)}, u32[]{:S(2)}) %collective-permute-start.2) | collective-permute-done | bytes 1179680 | tf_op jit(solution)/shard_map/sums/ppermute | solution.py:109
  51.2 2.2 %collective-permute-start.6 = (f32[576,128]{1,0:T(8,128)S(1)}, f32[576,128]{1,0:T(8,128)S(1)}, u32[]{:S(2)}, u32[]{:S(2)}) collective-permute-start(f32[576,128]{1,0:T(8,128)S(1)} %get-tuple-element.45), channel_id=1, source_target_pairs={{0,8},{4,12},{8,0},{12,4},{16,80},{20,84},{24,88},{28,92},{32,40},... | collective-permute-start | bytes 884744 | tf_op jit(solution)/shard_map/sums/ppermute | solution.py:109
  54.6 6.8 %collective-permute-done.5.refs_1_ = f32[576,128]{1,0:T(8,128)S(1)} collective-permute-done((f32[576,128]{1,0:T(8,128)S(1)}, f32[576,128]{1,0:T(8,128)S(1)}, u32[]{:S(2)}, u32[]{:S(2)}) %collective-permute-start.5) | collective-permute-done | bytes 294944 | tf_op jit(solution)/shard_map/sums/ppermute | solution.py:109
  63.4 3.0 %collective-permute-start.9 = (f32[2,72,128]{2,1,0:T(8,128)S(1)}, f32[2,72,128]{2,1,0:T(8,128)S(1)}, u32[]{:S(2)}, u32[]{:S(2)}) collective-permute-start(f32[2,72,128]{2,1,0:T(8,128)S(1)} %get-tuple-element.49), channel_id=1, source_target_pairs={{0,2},{1,3},{2,0},{3,1},{4,6},{5,7},{6,4},{7,5},{8,10},{9,11},{10,... | collective-permute-start | bytes 221192 | tf_op jit(solution)/shard_map/sums/ppermute | solution.py:109
  67.9 1.6 collective-permute-done.9.c
  71.3 4.5 %collective-permute-start.11 = (f32[72,128]{1,0:T(8,128)S(1)}, f32[72,128]{1,0:T(8,128)S(1)}, u32[]{:S(2)}, u32[]{:S(2)}) collective-permute-start(f32[72,128]{1,0:T(8,128)S(1)} %get-tuple-element.52), channel_id=1, source_target_pairs={{0,128},{128,0},{1,129},{129,1},{2,130},{130,2},{3,131},{131,3},{4... | collective-permute-start | bytes 110600 | tf_op jit(solution)/shard_map/sums/ppermute | solution.py:109
  75.7 2.3 %collective-permute-done.11 = f32[72,128]{1,0:T(8,128)S(1)} collective-permute-done((f32[72,128]{1,0:T(8,128)S(1)}, f32[72,128]{1,0:T(8,128)S(1)}, u32[]{:S(2)}, u32[]{:S(2)}) %collective-permute-start.11) | collective-permute-done | bytes 36896 | tf_op jit(solution)/shard_map/sums/ppermute | solution.py:109
  78.1 17.1 %all_to_all.20 = f32[8,72,128]{2,1,0:T(8,128)S(1)} all-to-all(f32[8,72,128]{2,1,0:T(8,128)S(1)} %broadcast_in_dim.14), channel_id=1, replica_groups=mesh['z_hi'=2,'x'=4,'core'=2,'y'=4,'z_lo'=4] {'z_hi','z_lo'}, dimensions={0} | all-to-all | bytes 589824 | tf_op jit(solution)/shard_map/back/all_to_all | solution.py:90
  96.3 5.4 %all-to-all-start.1 = ((f32[16,120,128]{2,1,0:T(8,128)}), f32[16,120,128]{2,1,0:T(8,128)S(1)}, u32[]{:S(2)}, u32[]{:S(2)}) async-start(f32[16,120,128]{2,1,0:T(8,128)} %broadcast_in_dim.16), calls=%async_computation.1 | async-start | bytes 1966080 | tf_op jit(solution)/shard_map/back/all_to_all | solution.py:90
  101.8 11.4 %all-to-all-done.1 = f32[16,120,128]{2,1,0:T(8,128)S(1)} async-done(((f32[16,120,128]{2,1,0:T(8,128)}), f32[16,120,128]{2,1,0:T(8,128)S(1)}, u32[]{:S(2)}, u32[]{:S(2)}) %all-to-all-start.1) | async-done | bytes 983072 | tf_op jit(solution)/shard_map/back/all_to_all | solution.py:90
  113.1 1.3 broadcast_in_dim.15
  114.4 1.6 broadcast_in_dim.17
  116.0 3.9 %all-to-all-start.2 = ((f32[16,200,128]{2,1,0:T(8,128)}), f32[16,200,128]{2,1,0:T(8,128)S(1)}, u32[]{:S(2)}, u32[]{:S(2)}) async-start(f32[16,200,128]{2,1,0:T(8,128)} %broadcast_in_dim.15), calls=%async_computation.2 | async-start | bytes 3276800 | tf_op jit(solution)/shard_map/back/all_to_all | solution.py:90
  119.9 25.0 %shard_map.28 = (f32[640,640]{1,0:T(8,128)S(1)}, f32[640,128]{1,0:T(8,128)S(1)}) custom-call(f32[1920,128]{1,0:T(8,128)S(1)} %bitcast.11), custom_call_target="tpu_custom_call" | custom-call | flops 30000001024 | tf_op jit(solution)/shard_map/pallas_call | solution.py:322
  144.9 1.2 copy-done.8
  146.1 1.2 copy-done.4
  147.3 6.4 %all-to-all-start.3 = ((f32[16,256,128]{2,1,0:T(8,128)}), f32[16,256,128]{2,1,0:T(8,128)S(1)}, u32[]{:S(2)}, u32[]{:S(2)}) async-start(f32[16,256,128]{2,1,0:T(8,128)} %broadcast_in_dim.17), calls=%async_computation.3 | async-start | bytes 4194304 | tf_op jit(solution)/shard_map/back/all_to_all | solution.py:90
  153.7 1.4 copy-done.5
  155.2 1.4 copy-done.9
  156.6 24.6 %shard_map.29 = (f32[1024,1024]{1,0:T(8,128)S(1)}, f32[1024,128]{1,0:T(8,128)S(1)}, f32[8,1024]{1,0:T(8,128)S(1)}) custom-call(s32[2]{0:T(128)S(1)} %pad_add_fusion.rows, f32[3200,128]{1,0:T(8,128)S(1)} %bitcast.10, f32[640,640]{1,0:T(8,128)S(1)} %copy-done.9, f32[640,128]{1,0:T(8,128)S(1)} %get-tuple-element.56.head_inverse), custom_call_target="tpu_custom_call" | custom-call | flops 40000000000 | tf_op jit(solution)/shard_map/pallas_call | solution.py:325
  181.2 2.0 copy-done
  183.1 7.0 %collective-permute-start.12 = (f32[8,1024]{1,0:T(8,128)S(1)}, f32[8,1024]{1,0:T(8,128)S(1)}, u32[]{:S(2)}, u32[]{:S(2)}) collective-permute-start(f32[8,1024]{1,0:T(8,128)S(1)} %get-tuple-element.57.z_own), channel_id=1, source_target_pairs={{0,16},{16,0},{1,17},{17,1},{2,18},{18,2},{3,19},{19,3},{4,20},{20... | collective-permute-start | bytes 98312 | tf_op jit(solution)/shard_map/ppermute | solution.py:98
  193.2 2.2 %copy-done.1 = f32[1024,1024]{1,0:T(8,128)S(1)} copy-done((f32[1024,1024]{1,0:T(8,128)S(1)}, f32[1024,1024]{1,0:T(8,128)}, u32[]{:S(2)}) %copy-start.1) | copy-done | bytes 4194328
  195.4 3.6 %shard_map.31 = f32[8,1024]{1,0:T(8,128)S(1)} custom-call(f32[8,1024]{1,0:T(8,128)S(1)} %shard_map.30.w_own, f32[8,1024]{1,0:T(8,128)S(1)} %collective-permute-done.13.w_sent, f32[1024,1024]{1,0:T(8,128)S(1)} %copy-done.1, f32[1024,128]{1,0:T(8,128)S(1)} %get-tuple-element.60.inverse), custom_call_target="tpu_custom_call" | custom-call | tf_op jit(solution)/shard_map/pallas_call | solution.py:329
  (48 shorter events, 17.2 us)
Async XLA Ops:
  0.0 1.0 copy-start.6
  1.0 1.0 copy-start.7
  4.8 11.2 %collective-permute-start = (f32[16,320,128]{2,1,0:T(8,128)}, f32[16,320,128]{2,1,0:T(8,128)}, u32[]{:S(2)}, u32[]{:S(2)}) collective-permute-start(f32[16,320,128]{2,1,0:T(8,128)} %get-tuple-element.34), channel_id=1, source_target_pairs={{0,16},{16,0},{1,17},{17,1},{2,18},{18,2},{3,19},{19,3},{4,20},{20... | collective-permute-start | bytes 7864328 | tf_op jit(solution)/shard_map/sums/ppermute | solution.py:98
  10.1 1.4 copy-start.2
  11.5 4.5 %collective-permute-start.1 = (f32[16,256,128]{2,1,0:T(8,128)}, f32[16,256,128]{2,1,0:T(8,128)}, u32[]{:S(2)}, u32[]{:S(2)}) collective-permute-start(f32[16,256,128]{2,1,0:T(8,128)} %get-tuple-element.38), channel_id=1, source_target_pairs={{0,16},{16,0},{1,17},{17,1},{2,18},{18,2},{3,19},{19,3},{4,20},{20... | collective-permute-start | bytes 6291464 | tf_op jit(solution)/shard_map/sums/ppermute | solution.py:98
  16.0 1.6 copy-start.3
  20.5 29.3 %collective-permute-start.2 = (f32[4,576,128]{2,1,0:T(8,128)S(1)}, f32[4,576,128]{2,1,0:T(8,128)S(1)}, u32[]{:S(2)}, u32[]{:S(2)}) collective-permute-start(f32[4,576,128]{2,1,0:T(8,128)S(1)} %get-tuple-element.40), channel_id=1, source_target_pairs={{0,32},{4,36},{8,40},{12,44},{16,20},{20,24},{24,28},{28,16},{32,6... | collective-permute-start | bytes 3538952 | tf_op jit(solution)/shard_map/sums/ppermute | solution.py:109
  20.6 29.2 %collective-permute-start.3 = (f32[4,576,128]{2,1,0:T(8,128)S(1)}, f32[4,576,128]{2,1,0:T(8,128)S(1)}, u32[]{:S(2)}, u32[]{:S(2)}) collective-permute-start(f32[4,576,128]{2,1,0:T(8,128)S(1)} %get-tuple-element.41), channel_id=1, source_target_pairs={{0,64},{4,68},{8,72},{12,76},{16,24},{20,28},{24,16},{28,20},{32,9... | collective-permute-start | bytes 3538952 | tf_op jit(solution)/shard_map/sums/ppermute | solution.py:109
  22.7 27.6 %collective-permute-start.4 = (f32[4,576,128]{2,1,0:T(8,128)S(1)}, f32[4,576,128]{2,1,0:T(8,128)S(1)}, u32[]{:S(2)}, u32[]{:S(2)}) collective-permute-start(f32[4,576,128]{2,1,0:T(8,128)S(1)} %get-tuple-element.42), channel_id=1, source_target_pairs={{0,96},{4,100},{8,104},{12,108},{16,28},{20,16},{24,20},{28,24},{3... | collective-permute-start | bytes 3538952 | tf_op jit(solution)/shard_map/sums/ppermute | solution.py:109
  51.2 10.3 %collective-permute-start.5 = (f32[576,128]{1,0:T(8,128)S(1)}, f32[576,128]{1,0:T(8,128)S(1)}, u32[]{:S(2)}, u32[]{:S(2)}) collective-permute-start(f32[576,128]{1,0:T(8,128)S(1)} %get-tuple-element.44), channel_id=1, source_target_pairs={{0,4},{4,8},{8,12},{12,0},{16,48},{20,52},{24,56},{28,60},{32,36},... | collective-permute-start | bytes 884744 | tf_op jit(solution)/shard_map/sums/ppermute | solution.py:109
  51.2 10.2 %collective-permute-start.6 = (f32[576,128]{1,0:T(8,128)S(1)}, f32[576,128]{1,0:T(8,128)S(1)}, u32[]{:S(2)}, u32[]{:S(2)}) collective-permute-start(f32[576,128]{1,0:T(8,128)S(1)} %get-tuple-element.45), channel_id=1, source_target_pairs={{0,8},{4,12},{8,0},{12,4},{16,80},{20,84},{24,88},{28,92},{32,40},... | collective-permute-start | bytes 884744 | tf_op jit(solution)/shard_map/sums/ppermute | solution.py:109
  53.5 8.6 %collective-permute-start.7 = (f32[576,128]{1,0:T(8,128)S(1)}, f32[576,128]{1,0:T(8,128)S(1)}, u32[]{:S(2)}, u32[]{:S(2)}) collective-permute-start(f32[576,128]{1,0:T(8,128)S(1)} %get-tuple-element.46), channel_id=1, source_target_pairs={{0,12},{4,0},{8,4},{12,8},{16,112},{20,116},{24,120},{28,124},{32,... | collective-permute-start | bytes 884744 | tf_op jit(solution)/shard_map/sums/ppermute | solution.py:109
  62.7 5.2 %collective-permute-start.8 = (f32[2,72,128]{2,1,0:T(8,128)S(1)}, f32[2,72,128]{2,1,0:T(8,128)S(1)}, u32[]{:S(2)}, u32[]{:S(2)}) collective-permute-start(f32[2,72,128]{2,1,0:T(8,128)S(1)} %get-tuple-element.48), channel_id=1, source_target_pairs={{0,1},{1,2},{2,3},{3,0},{4,5},{5,6},{6,7},{7,4},{8,9},{9,10},{10,1... | collective-permute-start | bytes 221192 | tf_op jit(solution)/shard_map/sums/ppermute | solution.py:109
  63.4 6.1 %collective-permute-start.9 = (f32[2,72,128]{2,1,0:T(8,128)S(1)}, f32[2,72,128]{2,1,0:T(8,128)S(1)}, u32[]{:S(2)}, u32[]{:S(2)}) collective-permute-start(f32[2,72,128]{2,1,0:T(8,128)S(1)} %get-tuple-element.49), channel_id=1, source_target_pairs={{0,2},{1,3},{2,0},{3,1},{4,6},{5,7},{6,4},{7,5},{8,10},{9,11},{10,... | collective-permute-start | bytes 221192 | tf_op jit(solution)/shard_map/sums/ppermute | solution.py:109
  66.4 4.3 %collective-permute-start.10 = (f32[2,72,128]{2,1,0:T(8,128)S(1)}, f32[2,72,128]{2,1,0:T(8,128)S(1)}, u32[]{:S(2)}, u32[]{:S(2)}) collective-permute-start(f32[2,72,128]{2,1,0:T(8,128)S(1)} %get-tuple-element.50), channel_id=1, source_target_pairs={{0,3},{1,0},{2,1},{3,2},{4,7},{5,4},{6,5},{7,6},{8,11},{9,8},{10,9... | collective-permute-start | bytes 221192 | tf_op jit(solution)/shard_map/sums/ppermute | solution.py:109
  71.3 6.8 %collective-permute-start.11 = (f32[72,128]{1,0:T(8,128)S(1)}, f32[72,128]{1,0:T(8,128)S(1)}, u32[]{:S(2)}, u32[]{:S(2)}) collective-permute-start(f32[72,128]{1,0:T(8,128)S(1)} %get-tuple-element.52), channel_id=1, source_target_pairs={{0,128},{128,0},{1,129},{129,1},{2,130},{130,2},{3,131},{131,3},{4... | collective-permute-start | bytes 110600 | tf_op jit(solution)/shard_map/sums/ppermute | solution.py:109
  96.3 16.9 %all-to-all-start.1 = ((f32[16,120,128]{2,1,0:T(8,128)}), f32[16,120,128]{2,1,0:T(8,128)S(1)}, u32[]{:S(2)}, u32[]{:S(2)}) async-start(f32[16,120,128]{2,1,0:T(8,128)} %broadcast_in_dim.16), calls=%async_computation.1 | async-start | bytes 1966080 | tf_op jit(solution)/shard_map/back/all_to_all | solution.py:90
  116.0 30.1 %all-to-all-start.2 = ((f32[16,200,128]{2,1,0:T(8,128)}), f32[16,200,128]{2,1,0:T(8,128)S(1)}, u32[]{:S(2)}, u32[]{:S(2)}) async-start(f32[16,200,128]{2,1,0:T(8,128)} %broadcast_in_dim.15), calls=%async_computation.2 | async-start | bytes 3276800 | tf_op jit(solution)/shard_map/back/all_to_all | solution.py:90
  144.9 1.2 copy-start.8
  146.1 1.2 copy-start.4
  147.3 43.8 %all-to-all-start.3 = ((f32[16,256,128]{2,1,0:T(8,128)}), f32[16,256,128]{2,1,0:T(8,128)S(1)}, u32[]{:S(2)}, u32[]{:S(2)}) async-start(f32[16,256,128]{2,1,0:T(8,128)} %broadcast_in_dim.17), calls=%async_computation.3 | async-start | bytes 4194304 | tf_op jit(solution)/shard_map/back/all_to_all | solution.py:90
  153.7 1.4 copy-start.5
  155.2 1.4 copy-start.9
  181.2 2.0 copy-start
  183.1 7.9 %collective-permute-start.12 = (f32[8,1024]{1,0:T(8,128)S(1)}, f32[8,1024]{1,0:T(8,128)S(1)}, u32[]{:S(2)}, u32[]{:S(2)}) collective-permute-start(f32[8,1024]{1,0:T(8,128)S(1)} %get-tuple-element.57.z_own), channel_id=1, source_target_pairs={{0,16},{16,0},{1,17},{17,1},{2,18},{18,2},{3,19},{19,3},{4,20},{20... | collective-permute-start | bytes 98312 | tf_op jit(solution)/shard_map/ppermute | solution.py:98
  192.0 1.2 collective-permute-start.13
  193.2 2.2 %copy-start.1 = (f32[1024,1024]{1,0:T(8,128)S(1)}, f32[1024,1024]{1,0:T(8,128)}, u32[]{:S(2)}) copy-start(f32[1024,1024]{1,0:T(8,128)} %copy-done) | copy-start | bytes 12582916
  199.1 1.2 collective-permute-start.14

commit v5 on v4

--- a/solution.py
+++ b/solution.py
@@ -11,7 +11,6 @@
 AXES = ("z_hi", "x", "core", "y", "z_lo")
 SIZES = (2, 4, 2, 4, 4)
 PLANE = ("x", "y")
-LINE = ("z_hi", "z_lo")
 N, NB, SB, G = 1024, 128, 32, 8
 KB = N // NB
 OWNED = 4
@@ -90,10 +89,6 @@
     return lax.all_to_all(pieces, axes, 0, 0, tiled=True)
 
 
-def spread(piece, n):
-    return jnp.broadcast_to(piece[None], (n, *piece.shape))
-
-
 def swap(a):
     return lax.ppermute(a, "core", [(0, 1), (1, 0)])
 
@@ -143,20 +138,33 @@
             outs[k][h] = (a + b) + (c + d)
 
 
-def line_second_kernel(at, a, b, c, d, *outs):
-    for k in range(2):
-        h = (at[5] + k) & 1
-        outs[k][...] = (a[h] + b[h]) + (c[h] + d[h])
-
-
-def share_of_sum(at, gram, gram_got, cross, cross_got):
+def line_second_kernel(a, b, c, d, out):
+    out[...] = (a[...] + b[...]) + (c[...] + d[...])
+
+
+def line_third_kernel(a, b, out):
+    out[...] = a[...] + b[...]
+
+
+def gather_kernel(at, a, b, c, d, early, late, cross, piece):
     rows = PART // 8
+    for k, got in enumerate((a, b, c, d)):
+        for h in range(2):
+            start = (h * 4 + ((at[4] - k) & 3)) * rows
+            piece[pl.ds(pl.multiple_of(start, 8), rows), :] = got[h]
+    for out, lo, hi in ((early, 0, EARLY_ROWS), (late, EARLY_ROWS, GRAM), (cross, GRAM, PART)):
+        out[...] = jnp.broadcast_to(piece[lo:hi, :][None], out.shape)
+
+
+def sum_of_chips(at, gram, gram_got, cross, cross_got):
+    share = (2, PART // 8, NB)
     pieces = call(plane_first_kernel, [(4, PART, NB)] * 4, 1, 4)(at, gram, gram_got, cross, cross_got)
     pieces = call(plane_second_kernel, [(PART, NB)] * 4, 1, 4)(at, *along_plane(pieces, 0))
-    pieces = call(line_first_kernel, [(2, rows, NB)] * 4, 1, 4)(at, *along_plane(pieces, 1))
-    pieces = call(line_second_kernel, [(rows, NB)] * 2, 1, 4)(at, *along_line(pieces, "z_lo"))
-    mine, theirs = along_line(pieces, "z_hi")
-    return mine + theirs
+    pieces = call(line_first_kernel, [share] * 4, 1, 4)(at, *along_plane(pieces, 1))
+    (mine,) = call(line_second_kernel, [share], 0, 4)(*along_line(pieces, "z_lo"))
+    (mine,) = call(line_third_kernel, [share], 0, 2)(*along_line([mine] * 2, "z_hi"))
+    wide = [(16, n, NB) for n in (EARLY_ROWS, GRAM - EARLY_ROWS, PART - GRAM)]
+    return call(gather_kernel, wide, 1, 4, [pltpu.VMEM((PART, NB), jnp.float32)])(at, *along_line([mine] * 4, "z_lo"))
 
 
 def tile(v):
@@ -296,7 +304,7 @@
     core = lax.axis_index("core")
     core_ref = core.astype(jnp.int32).reshape(1)
     x, y, z_lo, z_hi = (lax.axis_index(a).astype(jnp.int32) for a in ("x", "y", "z_lo", "z_hi"))
-    at = jnp.stack([*jnp.where(core == 0, jnp.array([x, y, 4, 1]), jnp.array([y, x, 1, 4])), z_lo, z_hi]).astype(jnp.int32)
+    at = jnp.stack([*jnp.where(core == 0, jnp.array([x, y, 4, 1]), jnp.array([y, x, 1, 4])), z_lo]).astype(jnp.int32)
     chip = (z_hi * 4 + x) * 32 + y * 4 + z_lo
     rows = jnp.stack([chip * OWNED, (chip + 16) * OWNED])
     work = pltpu.VMEM((NB, 2 * NB), jnp.float32)
@@ -308,13 +316,9 @@
         cross, cross_other = call(cross_kernel, [(16, PART - GRAM, NB)] * 2, 1, 2, flops=10**9)(
             core_ref, *after((view_x, view_y), gram)
         )
-        share = share_of_sum(at, gram, swap(gram_other), cross, swap(cross_other))
+        early, late, cross = sum_of_chips(at, gram, swap(gram_other), cross, swap(cross_other))
     with jax.named_scope("back"):
-        piece = exchange(spread(share, 8), LINE).reshape(PART, NB)
-        early, late, cross = (
-            spread(piece[lo:hi], 16) for lo, hi in ((0, EARLY_ROWS), (EARLY_ROWS, GRAM), (GRAM, PART))
-        )
-        early = after(exchange(early, PLANE), late, cross)
+        early = exchange(early, PLANE)
         late = exchange(after(late, early), PLANE)
         cross = exchange(after(cross, late), PLANE)
         early, late = early.reshape(-1, NB), late.reshape(-1, NB)

time: 201 us -> 193 us (0.960)
  blocking collectives: 17.1 us -> 0 us
  waiting for transfers between devices: 58.2 us -> 64.1 us
  starting transfers between devices: 42.4 us -> 46.1 us
  local copies, waits for them, and re-layouts: 18.4 us -> 15.8 us
    all_to_all x1 -> x0, blocking collectives: 17.1 us -> none  [exchange(): return lax.all_to_all(pieces, axes, 0, 0, tiled=True)]
    ppermute x10 -> x13, waiting for transfers between devices: 39.9 us -> 45.7 us  [shift(): lax.ppermute(p, axes, route(k))]
    ppermute x10 -> x13, starting transfers between devices: 15.7 us -> 19.8 us  [shift(): lax.ppermute(p, axes, route(k))]
    broadcast_in_dim x4 -> x0, local copies, waits for them, and re-layouts: 3.92 us -> none  [spread(): return jnp.broadcast_to(piece[None], (n, *piece.shape))]
    pallas_call x4 -> x6, Pallas kernels: 4.82 us -> 6.39 us  [the longest x1 2.87 us: sum_of_chips(): call(plane_first_kernel, [(4, PART, NB)] * 4, 1, 4)]
    unnamed x20 -> x26, local copies, waits for them, and re-layouts: 14.5 us -> 15.8 us
  transfers between devices with their start and end apart: 18 -> 21, of which waited for: 13 -> 16; matrix products, arithmetic and copies ran while one was open for 0% -> 0% of each run, Pallas kernels for 26% -> 27%
where the time goes in v5:
time: 193 us; the launch traced here: 192 us
  Pallas kernels  65.3 us (34%)
  waiting for transfers between devices  64.1 us (33%)
  starting transfers between devices  46.1 us (24%)
  local copies, waits for them, and re-layouts  15.8 us (8%)
    ppermute x13, waiting for transfers between devices, shift(): lax.ppermute(p, axes, route(k))  45.7 us
    pallas_call x1, Pallas kernels, on_device(): call(head_kernel, [(HEAD * NB, HEAD * NB), (HEAD * NB, NB)], 0, 1, [work]...  25 us
    pallas_call x1, Pallas kernels, on_device(): call(tail_kernel, [(N, N), (N, NB), (G, N)], 1, 3, [work], flops=4 * 10 *...  24.6 us
    ppermute x13, starting transfers between devices, shift(): lax.ppermute(p, axes, route(k))  19.8 us
    unnamed x26, local copies, waits for them, and re-layouts  15.8 us
    all_to_all x3, starting transfers between devices, exchange(): return lax.all_to_all(pieces, axes, 0, 0, tiled=True)  15.6 us
    all_to_all x3, waiting for transfers between devices, exchange(): return lax.all_to_all(pieces, axes, 0, 0, tiled=True)  11.4 us
    ppermute x5, starting transfers between devices, swap(): return lax.ppermute(a, 'core', [(0, 1), (1, 0)])  10.7 us
  transfers between devices with their start and end apart: 21, of which 16 were waited for; matrix products, arithmetic and copies ran while one was open for 0% of the time, Pallas kernels for 27%

profile of v5, /device:TPU:1, one launch (start us, length us, event | category | flops | bytes accessed | tf_op | source)
XLA Modules:
  0.0 192.2 jit_solution(15891708712114403734)
XLA Ops:
  2.1 2.7 %sums.8 = (f32[16,320,128]{2,1,0:T(8,128)S(1)}, f32[16,320,128]{2,1,0:T(8,128)}) custom-call(s32[1]{0:T(128)} %bitcast.core, bf16[256,1024]{1,0:T(8,128)(2,1)S(1)} %copy-done.7, bf16[256,1024]{1,0:T(8,128)(2,1)S(1)} %copy-done.9), custom_call_target="tpu_custom_call" | custom-call | flops 2000000000 | tf_op jit(solution)/shard_map/sums/pallas_call | solution.py:313
  4.8 3.3 %collective-permute-start = (f32[16,320,128]{2,1,0:T(8,128)}, f32[16,320,128]{2,1,0:T(8,128)}, u32[]{:S(2)}, u32[]{:S(2)}) collective-permute-start(f32[16,320,128]{2,1,0:T(8,128)} %get-tuple-element.34), channel_id=1, source_target_pairs={{0,16},{16,0},{1,17},{17,1},{2,18},{18,2},{3,19},{19,3},{4,20},{20... | collective-permute-start | bytes 7864328 | tf_op jit(solution)/shard_map/sums/ppermute | solution.py:93
  8.0 2.1 %sums.9 = (f32[16,256,128]{2,1,0:T(8,128)S(1)}, f32[16,256,128]{2,1,0:T(8,128)}) custom-call(s32[1]{0:T(128)} %bitcast.core, bf16[256,1024]{1,0:T(8,128)(2,1)S(1)} %copy-done.8, bf16[256,1024]{1,0:T(8,128)(2,1)S(1)} %copy-done.10), custom_call_target="tpu_custom_call" | custom-call | flops 1000000000 | tf_op jit(solution)/shard_map/sums/pallas_call | solution.py:316
  11.6 4.3 %collective-permute-done.1.cross_got = f32[16,256,128]{2,1,0:T(8,128)} collective-permute-done((f32[16,256,128]{2,1,0:T(8,128)}, f32[16,256,128]{2,1,0:T(8,128)}, u32[]{:S(2)}, u32[]{:S(2)}) %collective-permute-start.1) | collective-permute-done | bytes 2097184 | tf_op jit(solution)/shard_map/sums/ppermute | solution.py:93
  16.0 1.6 copy-done.3
  17.6 2.9 %sums.10 = (f32[4,576,128]{2,1,0:T(8,128)S(1)}, f32[4,576,128]{2,1,0:T(8,128)S(1)}, f32[4,576,128]{2,1,0:T(8,128)S(1)}, f32[4,576,128]{2,1,0:T(8,128)S(1)}) custom-call(s32[5]{0:T(128)S(1)} %pad_add_fusion.1.at, f32[16,320,128]{2,1,0:T(8,128)S(1)} %get-tuple-element.33.gram, f32[16,320,128]{2,1,0:T(8,128)} %collective-permute-done.gram_got, ...), custom_call_target="tpu_custom_call" | custom-call | tf_op jit(solution)/shard_map/sums/pallas_call | solution.py:161
  20.5 2.2 %collective-permute-start.3 = (f32[4,576,128]{2,1,0:T(8,128)S(1)}, f32[4,576,128]{2,1,0:T(8,128)S(1)}, u32[]{:S(2)}, u32[]{:S(2)}) collective-permute-start(f32[4,576,128]{2,1,0:T(8,128)S(1)} %get-tuple-element.41), channel_id=1, source_target_pairs={{0,64},{4,68},{8,72},{12,76},{16,24},{20,28},{24,16},{28,20},{32,9... | collective-permute-start | bytes 3538952 | tf_op jit(solution)/shard_map/sums/ppermute | solution.py:104
  23.8 25.9 %collective-permute-done.2.b = f32[4,576,128]{2,1,0:T(8,128)S(1)} collective-permute-done((f32[4,576,128]{2,1,0:T(8,128)S(1)}, f32[4,576,128]{2,1,0:T(8,128)S(1)}, u32[]{:S(2)}, u32[]{:S(2)}) %collective-permute-start.2) | collective-permute-done | bytes 1179680 | tf_op jit(solution)/shard_map/sums/ppermute | solution.py:104
  51.2 2.2 %collective-permute-start.6 = (f32[576,128]{1,0:T(8,128)S(1)}, f32[576,128]{1,0:T(8,128)S(1)}, u32[]{:S(2)}, u32[]{:S(2)}) collective-permute-start(f32[576,128]{1,0:T(8,128)S(1)} %get-tuple-element.45), channel_id=1, source_target_pairs={{0,8},{4,12},{8,0},{12,4},{16,80},{20,84},{24,88},{28,92},{32,40},... | collective-permute-start | bytes 884744 | tf_op jit(solution)/shard_map/sums/ppermute | solution.py:104
  54.6 6.8 %collective-permute-done.5.refs_1_ = f32[576,128]{1,0:T(8,128)S(1)} collective-permute-done((f32[576,128]{1,0:T(8,128)S(1)}, f32[576,128]{1,0:T(8,128)S(1)}, u32[]{:S(2)}, u32[]{:S(2)}) %collective-permute-start.5) | collective-permute-done | bytes 294944 | tf_op jit(solution)/shard_map/sums/ppermute | solution.py:104
  63.3 3.0 %collective-permute-start.9 = (f32[2,72,128]{2,1,0:T(8,128)S(1)}, f32[2,72,128]{2,1,0:T(8,128)S(1)}, u32[]{:S(2)}, u32[]{:S(2)}) collective-permute-start(f32[2,72,128]{2,1,0:T(8,128)S(1)} %get-tuple-element.49), channel_id=1, source_target_pairs={{0,2},{1,3},{2,0},{3,1},{4,6},{5,7},{6,4},{7,5},{8,10},{9,11},{10,... | collective-permute-start | bytes 221192 | tf_op jit(solution)/shard_map/sums/ppermute | solution.py:104
  67.8 1.6 collective-permute-done.9.c
  70.7 4.4 %collective-permute-start.11 = (f32[2,72,128]{2,1,0:T(8,128)S(1)}, f32[2,72,128]{2,1,0:T(8,128)S(1)}, u32[]{:S(2)}, u32[]{:S(2)}) collective-permute-start(f32[2,72,128]{2,1,0:T(8,128)S(1)} %sums.13.a), channel_id=1, source_target_pairs={{0,128},{128,0},{1,129},{129,1},{2,130},{130,2},{3,131},{131,3},{4... | collective-permute-start | bytes 221192 | tf_op jit(solution)/shard_map/sums/ppermute | solution.py:104
  75.1 2.9 %collective-permute-done.11.b = f32[2,72,128]{2,1,0:T(8,128)S(1)} collective-permute-done((f32[2,72,128]{2,1,0:T(8,128)S(1)}, f32[2,72,128]{2,1,0:T(8,128)S(1)}, u32[]{:S(2)}, u32[]{:S(2)}) %collective-permute-start.11) | collective-permute-done | bytes 73760 | tf_op jit(solution)/shard_map/sums/ppermute | solution.py:104
  78.0 2.2 %collective-permute-start.14 = (f32[2,72,128]{2,1,0:T(8,128)S(1)}, f32[2,72,128]{2,1,0:T(8,128)S(1)}, u32[]{:S(2)}, u32[]{:S(2)}) collective-permute-start(f32[2,72,128]{2,1,0:T(8,128)S(1)} %sums.14.a), channel_id=1, source_target_pairs={{0,3},{1,0},{2,1},{3,2},{4,7},{5,4},{6,5},{7,6},{8,11},{9,8},{10,9... | collective-permute-start | bytes 221192 | tf_op jit(solution)/shard_map/sums/ppermute | solution.py:104
  80.2 1.5 collective-permute-start.13
  83.3 2.6 %collective-permute-done.13.c = f32[2,72,128]{2,1,0:T(8,128)S(1)} collective-permute-done((f32[2,72,128]{2,1,0:T(8,128)S(1)}, f32[2,72,128]{2,1,0:T(8,128)S(1)}, u32[]{:S(2)}, u32[]{:S(2)}) %collective-permute-start.13) | collective-permute-done | bytes 73760 | tf_op jit(solution)/shard_map/sums/ppermute | solution.py:104
  85.9 1.5 collective-permute-done.12.b
  87.4 2.1 %sums.15 = (f32[16,120,128]{2,1,0:T(8,128)}, f32[16,200,128]{2,1,0:T(8,128)}, f32[16,256,128]{2,1,0:T(8,128)S(1)}) custom-call(s32[5]{0:T(128)S(1)} %pad_add_fusion.1.at, f32[2,72,128]{2,1,0:T(8,128)S(1)} %sums.14.a, f32[2,72,128]{2,1,0:T(8,128)S(1)} %collective-permute-done.12.b, f32[2,72,128]{2,1,0:T(8,128)S(1)} %collective-permute-done.13.c, ...), custom_call_target="tpu_custom_call" | custom-call | tf_op jit(solution)/shard_map/sums/pallas_call | solution.py:167
  89.5 1.4 copy-done.4
  90.9 5.3 %all-to-all-start = ((f32[16,120,128]{2,1,0:T(8,128)}), f32[16,120,128]{2,1,0:T(8,128)S(1)}, u32[]{:S(2)}, u32[]{:S(2)}) async-start(f32[16,120,128]{2,1,0:T(8,128)} %get-tuple-element.52), calls=%async_computation | async-start | bytes 1966080 | tf_op jit(solution)/shard_map/back/all_to_all | solution.py:89
  96.3 11.4 %all-to-all-done = f32[16,120,128]{2,1,0:T(8,128)S(1)} async-done(((f32[16,120,128]{2,1,0:T(8,128)}), f32[16,120,128]{2,1,0:T(8,128)S(1)}, u32[]{:S(2)}, u32[]{:S(2)}) %all-to-all-start) | async-done | bytes 983072 | tf_op jit(solution)/shard_map/back/all_to_all | solution.py:89
  107.7 3.7 %all-to-all-start.1 = ((f32[16,200,128]{2,1,0:T(8,128)}), f32[16,200,128]{2,1,0:T(8,128)S(1)}, u32[]{:S(2)}, u32[]{:S(2)}) async-start(f32[16,200,128]{2,1,0:T(8,128)} %get-tuple-element.53), calls=%async_computation.1 | async-start | bytes 3276800 | tf_op jit(solution)/shard_map/back/all_to_all | solution.py:89
  111.5 25.0 %shard_map.28 = (f32[640,640]{1,0:T(8,128)S(1)}, f32[640,128]{1,0:T(8,128)S(1)}) custom-call(f32[1920,128]{1,0:T(8,128)S(1)} %bitcast.9), custom_call_target="tpu_custom_call" | custom-call | flops 30000001024 | tf_op jit(solution)/shard_map/pallas_call | solution.py:326
  138.8 6.6 %all-to-all-start.2 = ((f32[16,256,128]{2,1,0:T(8,128)}), f32[16,256,128]{2,1,0:T(8,128)S(1)}, u32[]{:S(2)}, u32[]{:S(2)}) async-start(f32[16,256,128]{2,1,0:T(8,128)} %copy-done.4), calls=%async_computation.2 | async-start | bytes 4194304 | tf_op jit(solution)/shard_map/back/all_to_all | solution.py:89
  145.4 1.4 copy-done.6
  146.8 1.4 copy-done.12
  148.3 24.6 %shard_map.29 = (f32[1024,1024]{1,0:T(8,128)S(1)}, f32[1024,128]{1,0:T(8,128)S(1)}, f32[8,1024]{1,0:T(8,128)S(1)}) custom-call(s32[2]{0:T(128)S(1)} %pad_add_fusion.rows, f32[3200,128]{1,0:T(8,128)S(1)} %bitcast.8, f32[640,640]{1,0:T(8,128)S(1)} %copy-done.12, f32[640,128]{1,0:T(8,128)S(1)} %get-tuple-element.55.head_inverse), custom_call_target="tpu_custom_call" | custom-call | flops 40000000000 | tf_op jit(solution)/shard_map/pallas_call | solution.py:329
  172.9 2.0 %copy-done = f32[1024,1024]{1,0:T(8,128)} copy-done((f32[1024,1024]{1,0:T(8,128)}, f32[1024,1024]{1,0:T(8,128)S(1)}, u32[]{:S(2)}) %copy-start) | copy-done | bytes 4194328
  174.8 6.7 %collective-permute-start.15 = (f32[8,1024]{1,0:T(8,128)S(1)}, f32[8,1024]{1,0:T(8,128)S(1)}, u32[]{:S(2)}, u32[]{:S(2)}) collective-permute-start(f32[8,1024]{1,0:T(8,128)S(1)} %get-tuple-element.56.z_own), channel_id=1, source_target_pairs={{0,16},{16,0},{1,17},{17,1},{2,18},{18,2},{3,19},{19,3},{4,20},{20... | collective-permute-start | bytes 98312 | tf_op jit(solution)/shard_map/ppermute | solution.py:93
  184.5 2.2 %copy-done.1 = f32[1024,1024]{1,0:T(8,128)S(1)} copy-done((f32[1024,1024]{1,0:T(8,128)S(1)}, f32[1024,1024]{1,0:T(8,128)}, u32[]{:S(2)}) %copy-start.1) | copy-done | bytes 4194328
  186.7 3.6 %shard_map.31 = f32[8,1024]{1,0:T(8,128)S(1)} custom-call(f32[8,1024]{1,0:T(8,128)S(1)} %shard_map.30.w_own, f32[8,1024]{1,0:T(8,128)S(1)} %collective-permute-done.16.w_sent, f32[1024,1024]{1,0:T(8,128)S(1)} %copy-done.1, f32[1024,128]{1,0:T(8,128)S(1)} %get-tuple-element.60.inverse), custom_call_target="tpu_custom_call" | custom-call | tf_op jit(solution)/shard_map/pallas_call | solution.py:333
  (53 shorter events, 21.0 us)
Async XLA Ops:
  2.1 5.9 %copy-start.8 = (bf16[256,1024]{1,0:T(8,128)(2,1)S(1)}, bf16[256,1024]{1,0:T(8,128)(2,1)}, u32[]{:S(2)}) copy-start(bf16[256,1024]{1,0:T(8,128)(2,1)} %x.2) | copy-start | bytes 1572868
  2.1 5.9 %copy-start.10 = (bf16[256,1024]{1,0:T(8,128)(2,1)S(1)}, bf16[256,1024]{1,0:T(8,128)(2,1)}, u32[]{:S(2)}) copy-start(bf16[256,1024]{1,0:T(8,128)(2,1)} %y.2) | copy-start | bytes 1572868
  4.8 11.2 %collective-permute-start = (f32[16,320,128]{2,1,0:T(8,128)}, f32[16,320,128]{2,1,0:T(8,128)}, u32[]{:S(2)}, u32[]{:S(2)}) collective-permute-start(f32[16,320,128]{2,1,0:T(8,128)} %get-tuple-element.34), channel_id=1, source_target_pairs={{0,16},{16,0},{1,17},{17,1},{2,18},{18,2},{3,19},{19,3},{4,20},{20... | collective-permute-start | bytes 7864328 | tf_op jit(solution)/shard_map/sums/ppermute | solution.py:93
  10.1 1.4 copy-start.2
  11.5 4.5 %collective-permute-start.1 = (f32[16,256,128]{2,1,0:T(8,128)}, f32[16,256,128]{2,1,0:T(8,128)}, u32[]{:S(2)}, u32[]{:S(2)}) collective-permute-start(f32[16,256,128]{2,1,0:T(8,128)} %get-tuple-element.38), channel_id=1, source_target_pairs={{0,16},{16,0},{1,17},{17,1},{2,18},{18,2},{3,19},{19,3},{4,20},{20... | collective-permute-start | bytes 6291464 | tf_op jit(solution)/shard_map/sums/ppermute | solution.py:93
  16.0 1.6 copy-start.3
  20.4 29.3 %collective-permute-start.2 = (f32[4,576,128]{2,1,0:T(8,128)S(1)}, f32[4,576,128]{2,1,0:T(8,128)S(1)}, u32[]{:S(2)}, u32[]{:S(2)}) collective-permute-start(f32[4,576,128]{2,1,0:T(8,128)S(1)} %get-tuple-element.40), channel_id=1, source_target_pairs={{0,32},{4,36},{8,40},{12,44},{16,20},{20,24},{24,28},{28,16},{32,6... | collective-permute-start | bytes 3538952 | tf_op jit(solution)/shard_map/sums/ppermute | solution.py:104
  20.5 29.2 %collective-permute-start.3 = (f32[4,576,128]{2,1,0:T(8,128)S(1)}, f32[4,576,128]{2,1,0:T(8,128)S(1)}, u32[]{:S(2)}, u32[]{:S(2)}) collective-permute-start(f32[4,576,128]{2,1,0:T(8,128)S(1)} %get-tuple-element.41), channel_id=1, source_target_pairs={{0,64},{4,68},{8,72},{12,76},{16,24},{20,28},{24,16},{28,20},{32,9... | collective-permute-start | bytes 3538952 | tf_op jit(solution)/shard_map/sums/ppermute | solution.py:104
  22.7 27.6 %collective-permute-start.4 = (f32[4,576,128]{2,1,0:T(8,128)S(1)}, f32[4,576,128]{2,1,0:T(8,128)S(1)}, u32[]{:S(2)}, u32[]{:S(2)}) collective-permute-start(f32[4,576,128]{2,1,0:T(8,128)S(1)} %get-tuple-element.42), channel_id=1, source_target_pairs={{0,96},{4,100},{8,104},{12,108},{16,28},{20,16},{24,20},{28,24},{3... | collective-permute-start | bytes 3538952 | tf_op jit(solution)/shard_map/sums/ppermute | solution.py:104
  51.1 10.3 %collective-permute-start.5 = (f32[576,128]{1,0:T(8,128)S(1)}, f32[576,128]{1,0:T(8,128)S(1)}, u32[]{:S(2)}, u32[]{:S(2)}) collective-permute-start(f32[576,128]{1,0:T(8,128)S(1)} %get-tuple-element.44), channel_id=1, source_target_pairs={{0,4},{4,8},{8,12},{12,0},{16,48},{20,52},{24,56},{28,60},{32,36},... | collective-permute-start | bytes 884744 | tf_op jit(solution)/shard_map/sums/ppermute | solution.py:104
  51.2 10.2 %collective-permute-start.6 = (f32[576,128]{1,0:T(8,128)S(1)}, f32[576,128]{1,0:T(8,128)S(1)}, u32[]{:S(2)}, u32[]{:S(2)}) collective-permute-start(f32[576,128]{1,0:T(8,128)S(1)} %get-tuple-element.45), channel_id=1, source_target_pairs={{0,8},{4,12},{8,0},{12,4},{16,80},{20,84},{24,88},{28,92},{32,40},... | collective-permute-start | bytes 884744 | tf_op jit(solution)/shard_map/sums/ppermute | solution.py:104
  53.4 8.6 %collective-permute-start.7 = (f32[576,128]{1,0:T(8,128)S(1)}, f32[576,128]{1,0:T(8,128)S(1)}, u32[]{:S(2)}, u32[]{:S(2)}) collective-permute-start(f32[576,128]{1,0:T(8,128)S(1)} %get-tuple-element.46), channel_id=1, source_target_pairs={{0,12},{4,0},{8,4},{12,8},{16,112},{20,116},{24,120},{28,124},{32,... | collective-permute-start | bytes 884744 | tf_op jit(solution)/shard_map/sums/ppermute | solution.py:104
  62.7 5.2 %collective-permute-start.8 = (f32[2,72,128]{2,1,0:T(8,128)S(1)}, f32[2,72,128]{2,1,0:T(8,128)S(1)}, u32[]{:S(2)}, u32[]{:S(2)}) collective-permute-start(f32[2,72,128]{2,1,0:T(8,128)S(1)} %get-tuple-element.48), channel_id=1, source_target_pairs={{0,1},{1,2},{2,3},{3,0},{4,5},{5,6},{6,7},{7,4},{8,9},{9,10},{10,1... | collective-permute-start | bytes 221192 | tf_op jit(solution)/shard_map/sums/ppermute | solution.py:104
  63.3 6.1 %collective-permute-start.9 = (f32[2,72,128]{2,1,0:T(8,128)S(1)}, f32[2,72,128]{2,1,0:T(8,128)S(1)}, u32[]{:S(2)}, u32[]{:S(2)}) collective-permute-start(f32[2,72,128]{2,1,0:T(8,128)S(1)} %get-tuple-element.49), channel_id=1, source_target_pairs={{0,2},{1,3},{2,0},{3,1},{4,6},{5,7},{6,4},{7,5},{8,10},{9,11},{10,... | collective-permute-start | bytes 221192 | tf_op jit(solution)/shard_map/sums/ppermute | solution.py:104
  66.3 4.4 %collective-permute-start.10 = (f32[2,72,128]{2,1,0:T(8,128)S(1)}, f32[2,72,128]{2,1,0:T(8,128)S(1)}, u32[]{:S(2)}, u32[]{:S(2)}) collective-permute-start(f32[2,72,128]{2,1,0:T(8,128)S(1)} %get-tuple-element.50), channel_id=1, source_target_pairs={{0,3},{1,0},{2,1},{3,2},{4,7},{5,4},{6,5},{7,6},{8,11},{9,8},{10,9... | collective-permute-start | bytes 221192 | tf_op jit(solution)/shard_map/sums/ppermute | solution.py:104
  70.7 7.3 %collective-permute-start.11 = (f32[2,72,128]{2,1,0:T(8,128)S(1)}, f32[2,72,128]{2,1,0:T(8,128)S(1)}, u32[]{:S(2)}, u32[]{:S(2)}) collective-permute-start(f32[2,72,128]{2,1,0:T(8,128)S(1)} %sums.13.a), channel_id=1, source_target_pairs={{0,128},{128,0},{1,129},{129,1},{2,130},{130,2},{3,131},{131,3},{4... | collective-permute-start | bytes 221192 | tf_op jit(solution)/shard_map/sums/ppermute | solution.py:104
  78.0 5.3 %collective-permute-start.14 = (f32[2,72,128]{2,1,0:T(8,128)S(1)}, f32[2,72,128]{2,1,0:T(8,128)S(1)}, u32[]{:S(2)}, u32[]{:S(2)}) collective-permute-start(f32[2,72,128]{2,1,0:T(8,128)S(1)} %sums.14.a), channel_id=1, source_target_pairs={{0,3},{1,0},{2,1},{3,2},{4,7},{5,4},{6,5},{7,6},{8,11},{9,8},{10,9... | collective-permute-start | bytes 221192 | tf_op jit(solution)/shard_map/sums/ppermute | solution.py:104
  80.2 5.7 %collective-permute-start.13 = (f32[2,72,128]{2,1,0:T(8,128)S(1)}, f32[2,72,128]{2,1,0:T(8,128)S(1)}, u32[]{:S(2)}, u32[]{:S(2)}) collective-permute-start(f32[2,72,128]{2,1,0:T(8,128)S(1)} %sums.14.a), channel_id=1, source_target_pairs={{0,2},{1,3},{2,0},{3,1},{4,6},{5,7},{6,4},{7,5},{8,10},{9,11},{10,... | collective-permute-start | bytes 221192 | tf_op jit(solution)/shard_map/sums/ppermute | solution.py:104
  81.7 5.7 %collective-permute-start.12 = (f32[2,72,128]{2,1,0:T(8,128)S(1)}, f32[2,72,128]{2,1,0:T(8,128)S(1)}, u32[]{:S(2)}, u32[]{:S(2)}) collective-permute-start(f32[2,72,128]{2,1,0:T(8,128)S(1)} %sums.14.a), channel_id=1, source_target_pairs={{0,1},{1,2},{2,3},{3,0},{4,5},{5,6},{6,7},{7,4},{8,9},{9,10},{10,1... | collective-permute-start | bytes 221192 | tf_op jit(solution)/shard_map/sums/ppermute | solution.py:104
  89.5 1.4 copy-start.4
  90.9 16.9 %all-to-all-start = ((f32[16,120,128]{2,1,0:T(8,128)}), f32[16,120,128]{2,1,0:T(8,128)S(1)}, u32[]{:S(2)}, u32[]{:S(2)}) async-start(f32[16,120,128]{2,1,0:T(8,128)} %get-tuple-element.52), calls=%async_computation | async-start | bytes 1966080 | tf_op jit(solution)/shard_map/back/all_to_all | solution.py:89
  107.7 29.9 %all-to-all-start.1 = ((f32[16,200,128]{2,1,0:T(8,128)}), f32[16,200,128]{2,1,0:T(8,128)S(1)}, u32[]{:S(2)}, u32[]{:S(2)}) async-start(f32[16,200,128]{2,1,0:T(8,128)} %get-tuple-element.53), calls=%async_computation.1 | async-start | bytes 3276800 | tf_op jit(solution)/shard_map/back/all_to_all | solution.py:89
  136.5 1.2 copy-start.11
  137.6 1.2 copy-start.5
  138.8 43.5 %all-to-all-start.2 = ((f32[16,256,128]{2,1,0:T(8,128)}), f32[16,256,128]{2,1,0:T(8,128)S(1)}, u32[]{:S(2)}, u32[]{:S(2)}) async-start(f32[16,256,128]{2,1,0:T(8,128)} %copy-done.4), calls=%async_computation.2 | async-start | bytes 4194304 | tf_op jit(solution)/shard_map/back/all_to_all | solution.py:89
  145.4 1.4 copy-start.6
  146.8 1.4 copy-start.12
  172.8 2.0 %copy-start = (f32[1024,1024]{1,0:T(8,128)}, f32[1024,1024]{1,0:T(8,128)S(1)}, u32[]{:S(2)}) copy-start(f32[1024,1024]{1,0:T(8,128)S(1)} %get-tuple-element.59.upper) | copy-start | bytes 12582916
  174.8 7.5 %collective-permute-start.15 = (f32[8,1024]{1,0:T(8,128)S(1)}, f32[8,1024]{1,0:T(8,128)S(1)}, u32[]{:S(2)}, u32[]{:S(2)}) collective-permute-start(f32[8,1024]{1,0:T(8,128)S(1)} %get-tuple-element.56.z_own), channel_id=1, source_target_pairs={{0,16},{16,0},{1,17},{17,1},{2,18},{18,2},{3,19},{19,3},{4,20},{20... | collective-permute-start | bytes 98312 | tf_op jit(solution)/shard_map/ppermute | solution.py:93
  183.3 1.2 collective-permute-start.16
  184.5 2.2 %copy-start.1 = (f32[1024,1024]{1,0:T(8,128)S(1)}, f32[1024,1024]{1,0:T(8,128)}, u32[]{:S(2)}) copy-start(f32[1024,1024]{1,0:T(8,128)} %copy-done) | copy-start | bytes 12582916
  190.3 1.2 collective-permute-start.17
  (2 other events, 2.1 us)

commit v6 on v5

--- a/solution.py
+++ b/solution.py
@@ -11,7 +11,7 @@
 AXES = ("z_hi", "x", "core", "y", "z_lo")
 SIZES = (2, 4, 2, 4, 4)
 PLANE = ("x", "y")
-N, NB, SB, G = 1024, 128, 32, 8
+N, NB, SB, G = 1024, 128, 64, 8
 KB = N // NB
 OWNED = 4
 HEAD = 5
@@ -24,6 +24,7 @@
 PART = GRAM + N // 2 * N // NB // 16
 VMEM = pl.BlockSpec(memory_space=pltpu.VMEM)
 SMEM = pl.BlockSpec(memory_space=pltpu.SMEM)
+HBM = pl.BlockSpec(memory_space=pltpu.HBM)
 
 
 def mm(a, b, dims):
@@ -32,15 +33,15 @@
     )
 
 
-def call(kernel, outs, n_smem, n_vmem, scratch=(), flops=0, bytes_accessed=0):
+def call(kernel, outs, n_smem, n_vmem, scratch=(), flops=0, n_hbm=0, hbm_outs=0):
     return pl.pallas_call(
         kernel,
         out_shape=[jax.ShapeDtypeStruct(s, jnp.float32) for s in outs],
-        in_specs=[SMEM] * n_smem + [VMEM] * n_vmem,
-        out_specs=[VMEM] * len(outs),
+        in_specs=[SMEM] * n_smem + [HBM] * n_hbm + [VMEM] * n_vmem,
+        out_specs=[HBM] * hbm_outs + [VMEM] * (len(outs) - hbm_outs),
         scratch_shapes=list(scratch),
-        compiler_params=pltpu.CompilerParams(vmem_limit_bytes=16 << 20),
-        cost_estimate=pl.CostEstimate(flops=flops, bytes_accessed=bytes_accessed, transcendentals=0),
+        compiler_params=pltpu.CompilerParams(vmem_limit_bytes=(60 if n_hbm + hbm_outs else 16) << 20),
+        cost_estimate=pl.CostEstimate(flops=flops, bytes_accessed=0, transcendentals=0),
     )
 
 
@@ -245,18 +246,42 @@
     lax.fori_loop(first, last, step, 0)
 
 
-def head_kernel(blocks, upper, inverse, work):
+def right_of(ref, i, end):
+    return ref.at[pl.ds(i * NB, NB), pl.ds((i + 1) * NB, end - (i + 1) * NB)]
+
+
+def block(ref, i, j):
+    return ref.at[pl.ds(i * NB, NB), pl.ds(j * NB, NB)]
+
+
+def head_kernel(blocks, head, inverse, upper, work, sems):
     for at, (i, j) in enumerate(EARLY):
         upper[i * NB:(i + 1) * NB, j * NB:(j + 1) * NB] = blocks[at * NB:(at + 1) * NB, :]
     eliminate(0, HEAD, HEAD, upper, inverse, work)
-
-
-def tail_kernel(rows, blocks, head, head_inverse, upper, inverse, z, work):
+    copies = [
+        pltpu.make_async_copy(right_of(upper, i, HEAD * NB), right_of(head, i, HEAD * NB), sems.at[i])
+        for i in range(HEAD - 1)
+    ]
+    for c in copies:
+        c.start()
+    for c in copies:
+        c.wait()
+
+
+def tail_kernel(rows, late, head, head_inverse, factor, inverse, z, upper, work, in_sems, out_sems):
     h = HEAD * NB
-    upper[:h, :h] = head[...]
+    copies = [
+        pltpu.make_async_copy(late.at[pl.ds(at * NB, NB), :], block(upper, i, j), in_sems.at[at])
+        for at, (i, j) in enumerate(LATE)
+    ] + [
+        pltpu.make_async_copy(right_of(head, i, h), right_of(upper, i, h), in_sems.at[len(LATE) + i])
+        for i in range(HEAD - 1)
+    ]
+    for c in copies:
+        c.start()
     inverse[:h, :] = head_inverse[...]
-    for at, (i, j) in enumerate(LATE):
-        upper[i * NB:(i + 1) * NB, j * NB:(j + 1) * NB] = blocks[at * NB:(at + 1) * NB, :]
+    for c in copies:
+        c.wait()
     for k in range(HEAD):
         lo, nxt = k * NB, (k + 1) * NB
         v = upper[lo:nxt, h:]
@@ -266,7 +291,14 @@
     for i in range(HEAD, KB):
         done = upper[:h, i * NB:]
         upper[i * NB:(i + 1) * NB, i * NB:] -= mm(done[:, :NB], done, ((0,), (0,)))
+    copies = [
+        pltpu.make_async_copy(right_of(upper, i, N), right_of(factor, i, N), out_sems.at[i]) for i in range(KB - 1)
+    ]
+    for c in copies[:HEAD]:
+        c.start()
     eliminate(HEAD, KB, KB, upper, inverse, work)
+    for c in copies[HEAD:]:
+        c.start()
     line = lax.broadcasted_iota(jnp.int32, (G, NB), 0)
     want = jnp.where(line < OWNED, rows[0] + line, rows[1] + line - OWNED)
     lane = lax.broadcasted_iota(jnp.int32, (G, NB), 1)
@@ -275,6 +307,8 @@
         if k < KB - 1:
             v = v - mm(z[:, (k + 1) * NB:], upper[k * NB:(k + 1) * NB, (k + 1) * NB:], ((1,), (1,)))
         z[:, k * NB:(k + 1) * NB] = mm(v, inverse[k * NB:(k + 1) * NB, :], ((1,), (0,)))
+    for c in copies:
+        c.wait()
 
 
 def apply_kernel(core, z_own, z_sent, cross, out):
@@ -287,11 +321,20 @@
     out[...] = acc
 
 
-def solve_kernel(w_own, w_sent, upper, inverse, y):
+def solve_kernel(factor, w_own, w_sent, inverse, y, upper, sems):
+    copies = [
+        pltpu.make_async_copy(
+            factor.at[pl.ds(0, k * NB), pl.ds(k * NB, NB)], upper.at[pl.ds(0, k * NB), pl.ds(k * NB, NB)], sems.at[k - 1]
+        )
+        for k in range(1, KB)
+    ]
+    for c in copies:
+        c.start()
     w = w_own[...] + w_sent[...]
     for k in range(KB):
         v = w[:, k * NB:(k + 1) * NB]
         if k:
+            copies[k - 1].wait()
             v = v - mm(y[:, :k * NB], upper[:k * NB, k * NB:(k + 1) * NB], ((1,), (0,)))
         y[:, k * NB:(k + 1) * NB] = mm(v, inverse[k * NB:(k + 1) * NB, :], ((1,), (1,)))
 
@@ -323,14 +366,19 @@
         cross = exchange(after(cross, late), PLANE)
         early, late = early.reshape(-1, NB), late.reshape(-1, NB)
 
+    size = HEAD * NB
+    dma = pltpu.SemaphoreType.DMA
+    square = pltpu.VMEM((N, N), jnp.float32)
     head, head_inverse = call(
-        head_kernel, [(HEAD * NB, HEAD * NB), (HEAD * NB, NB)], 0, 1, [work], flops=3 * 10**10
+        head_kernel, [(size, size), (size, NB)], 0, 1,
+        [pltpu.VMEM((size, size), jnp.float32), work, dma((HEAD - 1,))], flops=3 * 10**10, hbm_outs=1,
     )(early)
-    upper, inverse, z = call(tail_kernel, [(N, N), (N, NB), (G, N)], 1, 3, [work], flops=4 * 10**10)(
-        rows, late, head, head_inverse
-    )
+    factor, inverse, z = call(
+        tail_kernel, [(N, N), (N, NB), (G, N)], 1, 1,
+        [square, work, dma((len(LATE) + HEAD - 1,)), dma((KB - 1,))], flops=4 * 10**10, n_hbm=2, hbm_outs=1,
+    )(rows, late, head, head_inverse)
     (w,) = call(apply_kernel, [(G, N)], 1, 3)(core_ref, z, swap(z), cross)
-    (y_rows,) = call(solve_kernel, [(G, N)], 0, 4)(w, swap(w), upper, inverse)
+    (y_rows,) = call(solve_kernel, [(G, N)], 0, 3, [square, dma((KB - 1,))], n_hbm=1)(factor, w, swap(w), inverse)
     y_sent = swap(y_rows[:OWNED])
     return jnp.where(core == 0, y_sent, y_rows[OWNED:])
 

time: 193 us -> 196 us (1.016)
  Pallas kernels: 65.3 us -> 71.9 us
  local copies, waits for them, and re-layouts: 15.8 us -> 10.7 us
    pallas_call x3, Pallas kernels: 53.2 us -> 59.8 us  [the longest x1 26.7 us: on_device(): call(tail_kernel, [(N, N), (N, NB), (G, N)], 1, 1, [square, work, dma((le...]
    unnamed x26 -> x24, local copies, waits for them, and re-layouts: 15.8 us -> 9.99 us
  transfers between devices with their start and end apart: 21 -> 21, of which waited for: 16 -> 16; matrix products, arithmetic and copies ran while one was open for 0% -> 0% of each run, Pallas kernels for 27% -> 28%
where the time goes in v6:
time: 196 us; the launch traced here: 195 us
  Pallas kernels  71.9 us (37%)
  waiting for transfers between devices  63.7 us (32%)
  starting transfers between devices  46.4 us (24%)
  local copies, waits for them, and re-layouts  10.7 us (5%)
  other arithmetic  2.11 us (1%)
    ppermute x13, waiting for transfers between devices, shift(): lax.ppermute(p, axes, route(k))  45.7 us
    pallas_call x1, Pallas kernels, on_device(): call(tail_kernel, [(N, N), (N, NB), (G, N)], 1, 1, [square, work, dma((le...  26.7 us
    pallas_call x1, Pallas kernels, on_device(): call(head_kernel, [(size, size), (size, NB)], 0, 1, [pltpu.VMEM((size, si...  26.4 us
    ppermute x13, starting transfers between devices, shift(): lax.ppermute(p, axes, route(k))  19.8 us
    all_to_all x3, starting transfers between devices, exchange(): return lax.all_to_all(pieces, axes, 0, 0, tiled=True)  15.8 us
    all_to_all x3, waiting for transfers between devices, exchange(): return lax.all_to_all(pieces, axes, 0, 0, tiled=True)  10.9 us
    ppermute x5, starting transfers between devices, swap(): return lax.ppermute(a, 'core', [(0, 1), (1, 0)])  10.8 us
    unnamed x24, local copies, waits for them, and re-layouts  9.99 us
  transfers between devices with their start and end apart: 21, of which 16 were waited for; matrix products, arithmetic and copies ran while one was open for 0% of the time, Pallas kernels for 28%

profile of v6, /device:TPU:1, one launch (start us, length us, event | category | flops | bytes accessed | tf_op | source)
XLA Modules:
  0.0 195.0 jit_solution(9787638316602919106)
XLA Ops:
  2.1 2.7 %sums.8 = (f32[16,320,128]{2,1,0:T(8,128)S(1)}, f32[16,320,128]{2,1,0:T(8,128)}) custom-call(s32[1]{0:T(128)} %bitcast.5.core, bf16[256,1024]{1,0:T(8,128)(2,1)S(1)} %copy-done.5, bf16[256,1024]{1,0:T(8,128)(2,1)S(1)} %copy-done.7), custom_call_target="tpu_custom_call" | custom-call | flops 2000000000 | tf_op jit(solution)/shard_map/sums/pallas_call | solution.py:356
  4.8 3.3 %collective-permute-start = (f32[16,320,128]{2,1,0:T(8,128)}, f32[16,320,128]{2,1,0:T(8,128)}, u32[]{:S(2)}, u32[]{:S(2)}) collective-permute-start(f32[16,320,128]{2,1,0:T(8,128)} %get-tuple-element.34), channel_id=1, source_target_pairs={{0,16},{16,0},{1,17},{17,1},{2,18},{18,2},{3,19},{19,3},{4,20},{20... | collective-permute-start | bytes 7864328 | tf_op jit(solution)/shard_map/sums/ppermute | solution.py:94
  8.0 2.1 %sums.9 = (f32[16,256,128]{2,1,0:T(8,128)S(1)}, f32[16,256,128]{2,1,0:T(8,128)}) custom-call(s32[1]{0:T(128)} %bitcast.5.core, bf16[256,1024]{1,0:T(8,128)(2,1)S(1)} %copy-done.6, bf16[256,1024]{1,0:T(8,128)(2,1)S(1)} %copy-done.8), custom_call_target="tpu_custom_call" | custom-call | flops 1000000000 | tf_op jit(solution)/shard_map/sums/pallas_call | solution.py:359
  10.1 1.4 copy-done
  11.6 4.3 %collective-permute-done.1.cross_got = f32[16,256,128]{2,1,0:T(8,128)} collective-permute-done((f32[16,256,128]{2,1,0:T(8,128)}, f32[16,256,128]{2,1,0:T(8,128)}, u32[]{:S(2)}, u32[]{:S(2)}) %collective-permute-start.1) | collective-permute-done | bytes 2097184 | tf_op jit(solution)/shard_map/sums/ppermute | solution.py:94
  16.0 1.6 copy-done.1
  17.6 2.9 %sums.10 = (f32[4,576,128]{2,1,0:T(8,128)S(1)}, f32[4,576,128]{2,1,0:T(8,128)S(1)}, f32[4,576,128]{2,1,0:T(8,128)S(1)}, f32[4,576,128]{2,1,0:T(8,128)S(1)}) custom-call(s32[5]{0:T(128)S(1)} %pad_add_fusion.1.at, f32[16,320,128]{2,1,0:T(8,128)S(1)} %get-tuple-element.33.gram, f32[16,320,128]{2,1,0:T(8,128)} %collective-permute-done.gram_got, ...), custom_call_target="tpu_custom_call" | custom-call | tf_op jit(solution)/shard_map/sums/pallas_call | solution.py:162
  20.5 2.2 %collective-permute-start.3 = (f32[4,576,128]{2,1,0:T(8,128)S(1)}, f32[4,576,128]{2,1,0:T(8,128)S(1)}, u32[]{:S(2)}, u32[]{:S(2)}) collective-permute-start(f32[4,576,128]{2,1,0:T(8,128)S(1)} %get-tuple-element.41), channel_id=1, source_target_pairs={{0,64},{4,68},{8,72},{12,76},{16,24},{20,28},{24,16},{28,20},{32,9... | collective-permute-start | bytes 3538952 | tf_op jit(solution)/shard_map/sums/ppermute | solution.py:105
  23.8 25.9 %collective-permute-done.2.b = f32[4,576,128]{2,1,0:T(8,128)S(1)} collective-permute-done((f32[4,576,128]{2,1,0:T(8,128)S(1)}, f32[4,576,128]{2,1,0:T(8,128)S(1)}, u32[]{:S(2)}, u32[]{:S(2)}) %collective-permute-start.2) | collective-permute-done | bytes 1179680 | tf_op jit(solution)/shard_map/sums/ppermute | solution.py:105
  51.2 2.2 %collective-permute-start.6 = (f32[576,128]{1,0:T(8,128)S(1)}, f32[576,128]{1,0:T(8,128)S(1)}, u32[]{:S(2)}, u32[]{:S(2)}) collective-permute-start(f32[576,128]{1,0:T(8,128)S(1)} %get-tuple-element.45), channel_id=1, source_target_pairs={{0,8},{4,12},{8,0},{12,4},{16,80},{20,84},{24,88},{28,92},{32,40},... | collective-permute-start | bytes 884744 | tf_op jit(solution)/shard_map/sums/ppermute | solution.py:105
  54.6 6.8 %collective-permute-done.5.refs_1_ = f32[576,128]{1,0:T(8,128)S(1)} collective-permute-done((f32[576,128]{1,0:T(8,128)S(1)}, f32[576,128]{1,0:T(8,128)S(1)}, u32[]{:S(2)}, u32[]{:S(2)}) %collective-permute-start.5) | collective-permute-done | bytes 294944 | tf_op jit(solution)/shard_map/sums/ppermute | solution.py:105
  63.4 3.0 %collective-permute-start.9 = (f32[2,72,128]{2,1,0:T(8,128)S(1)}, f32[2,72,128]{2,1,0:T(8,128)S(1)}, u32[]{:S(2)}, u32[]{:S(2)}) collective-permute-start(f32[2,72,128]{2,1,0:T(8,128)S(1)} %get-tuple-element.49), channel_id=1, source_target_pairs={{0,2},{1,3},{2,0},{3,1},{4,6},{5,7},{6,4},{7,5},{8,10},{9,11},{10,... | collective-permute-start | bytes 221192 | tf_op jit(solution)/shard_map/sums/ppermute | solution.py:105
  67.9 1.6 collective-permute-done.9.c
  69.5 1.2 collective-permute-done.10.d
  70.7 4.5 %collective-permute-start.11 = (f32[2,72,128]{2,1,0:T(8,128)S(1)}, f32[2,72,128]{2,1,0:T(8,128)S(1)}, u32[]{:S(2)}, u32[]{:S(2)}) collective-permute-start(f32[2,72,128]{2,1,0:T(8,128)S(1)} %sums.13.a), channel_id=1, source_target_pairs={{0,128},{128,0},{1,129},{129,1},{2,130},{130,2},{3,131},{131,3},{4... | collective-permute-start | bytes 221192 | tf_op jit(solution)/shard_map/sums/ppermute | solution.py:105
  75.2 2.9 %collective-permute-done.11.b = f32[2,72,128]{2,1,0:T(8,128)S(1)} collective-permute-done((f32[2,72,128]{2,1,0:T(8,128)S(1)}, f32[2,72,128]{2,1,0:T(8,128)S(1)}, u32[]{:S(2)}, u32[]{:S(2)}) %collective-permute-start.11) | collective-permute-done | bytes 73760 | tf_op jit(solution)/shard_map/sums/ppermute | solution.py:105
  78.0 2.2 %collective-permute-start.14 = (f32[2,72,128]{2,1,0:T(8,128)S(1)}, f32[2,72,128]{2,1,0:T(8,128)S(1)}, u32[]{:S(2)}, u32[]{:S(2)}) collective-permute-start(f32[2,72,128]{2,1,0:T(8,128)S(1)} %sums.14.a), channel_id=1, source_target_pairs={{0,3},{1,0},{2,1},{3,2},{4,7},{5,4},{6,5},{7,6},{8,11},{9,8},{10,9... | collective-permute-start | bytes 221192 | tf_op jit(solution)/shard_map/sums/ppermute | solution.py:105
  80.2 1.5 collective-permute-start.13
  83.2 2.7 %collective-permute-done.13.c = f32[2,72,128]{2,1,0:T(8,128)S(1)} collective-permute-done((f32[2,72,128]{2,1,0:T(8,128)S(1)}, f32[2,72,128]{2,1,0:T(8,128)S(1)}, u32[]{:S(2)}, u32[]{:S(2)}) %collective-permute-start.13) | collective-permute-done | bytes 73760 | tf_op jit(solution)/shard_map/sums/ppermute | solution.py:105
  85.9 1.5 collective-permute-done.12.b
  87.4 2.1 %sums.15 = (f32[16,120,128]{2,1,0:T(8,128)}, f32[16,200,128]{2,1,0:T(8,128)}, f32[16,256,128]{2,1,0:T(8,128)S(1)}) custom-call(s32[5]{0:T(128)S(1)} %pad_add_fusion.1.at, f32[2,72,128]{2,1,0:T(8,128)S(1)} %sums.14.a, f32[2,72,128]{2,1,0:T(8,128)S(1)} %collective-permute-done.12.b, f32[2,72,128]{2,1,0:T(8,128)S(1)} %collective-permute-done.13.c, ...), custom_call_target="tpu_custom_call" | custom-call | tf_op jit(solution)/shard_map/sums/pallas_call | solution.py:168
  89.5 1.4 copy-done.2
  90.9 5.5 %all-to-all-start = ((f32[16,120,128]{2,1,0:T(8,128)}), f32[16,120,128]{2,1,0:T(8,128)S(1)}, u32[]{:S(2)}, u32[]{:S(2)}) async-start(f32[16,120,128]{2,1,0:T(8,128)} %get-tuple-element.52), calls=%async_computation | async-start | bytes 1966080 | tf_op jit(solution)/shard_map/back/all_to_all | solution.py:90
  97.0 10.9 %all-to-all-done = f32[16,120,128]{2,1,0:T(8,128)S(1)} async-done(((f32[16,120,128]{2,1,0:T(8,128)}), f32[16,120,128]{2,1,0:T(8,128)S(1)}, u32[]{:S(2)}, u32[]{:S(2)}) %all-to-all-start) | async-done | bytes 983072 | tf_op jit(solution)/shard_map/back/all_to_all | solution.py:90
  108.8 3.7 %all-to-all-start.1 = ((f32[16,200,128]{2,1,0:T(8,128)}), f32[16,200,128]{2,1,0:T(8,128)S(1)}, u32[]{:S(2)}, u32[]{:S(2)}) async-start(f32[16,200,128]{2,1,0:T(8,128)} %get-tuple-element.53), calls=%async_computation.1 | async-start | bytes 3276800 | tf_op jit(solution)/shard_map/back/all_to_all | solution.py:90
  112.6 26.4 %shard_map.28 = (f32[640,640]{1,0:T(8,128)}, f32[640,128]{1,0:T(8,128)}) custom-call(f32[1920,128]{1,0:T(8,128)} %bitcast.9), custom_call_target="tpu_custom_call" | custom-call | flops 30000001024 | tf_op jit(solution)/shard_map/pallas_call | solution.py:372
  139.0 1.2 copy-done.9
  140.2 6.6 %all-to-all-start.2 = ((f32[16,256,128]{2,1,0:T(8,128)}), f32[16,256,128]{2,1,0:T(8,128)S(1)}, u32[]{:S(2)}, u32[]{:S(2)}) async-start(f32[16,256,128]{2,1,0:T(8,128)} %copy-done.2), calls=%async_computation.2 | async-start | bytes 4194304 | tf_op jit(solution)/shard_map/back/all_to_all | solution.py:90
  146.8 26.7 %shard_map.29 = (f32[1024,1024]{1,0:T(8,128)}, f32[1024,128]{1,0:T(8,128)}, f32[8,1024]{1,0:T(8,128)}) custom-call(s32[2]{0:T(128)} %pad_add_fusion.rows, f32[3200,128]{1,0:T(8,128)} %bitcast.8, f32[640,640]{1,0:T(8,128)} %get-tuple-element.54.head, f32[640,128]{1,0:T(8,128)} %get-tuple-element.55.head_inverse), custom_call_target="tpu_custom_call" | custom-call | flops 40000000000 | tf_op jit(solution)/shard_map/pallas_call | solution.py:376
  173.5 6.6 %collective-permute-start.15 = (f32[8,1024]{1,0:T(8,128)}, f32[8,1024]{1,0:T(8,128)S(1)}, u32[]{:S(2)}, u32[]{:S(2)}) collective-permute-start(f32[8,1024]{1,0:T(8,128)} %get-tuple-element.57.z_own), channel_id=1, source_target_pairs={{0,16},{16,0},{1,17},{17,1},{2,18},{18,2},{3,19},{19,3},{4,20},{20... | collective-permute-start | bytes 98312 | tf_op jit(solution)/shard_map/ppermute | solution.py:94
  185.0 6.7 %shard_map.31 = f32[8,1024]{1,0:T(8,128)} custom-call(f32[1024,1024]{1,0:T(8,128)} %get-tuple-element.56.factor, f32[8,1024]{1,0:T(8,128)} %copy-done.3, f32[8,1024]{1,0:T(8,128)} %copy-done.11, f32[1024,128]{1,0:T(8,128)} %get-tuple-element.60.inverse), custom_call_target="tpu_custom_call" | custom-call | tf_op jit(solution)/shard_map/pallas_call | solution.py:381
  193.6 1.4 slice_select_fusion
  (51 shorter events, 19.3 us)
Async XLA Ops:
  0.0 1.0 copy-start.5
  1.0 1.0 copy-start.7
  2.1 5.9 %copy-start.6 = (bf16[256,1024]{1,0:T(8,128)(2,1)S(1)}, bf16[256,1024]{1,0:T(8,128)(2,1)}, u32[]{:S(2)}) copy-start(bf16[256,1024]{1,0:T(8,128)(2,1)} %x.2) | copy-start | bytes 1572868
  2.1 5.9 %copy-start.8 = (bf16[256,1024]{1,0:T(8,128)(2,1)S(1)}, bf16[256,1024]{1,0:T(8,128)(2,1)}, u32[]{:S(2)}) copy-start(bf16[256,1024]{1,0:T(8,128)(2,1)} %y.2) | copy-start | bytes 1572868
  4.8 11.2 %collective-permute-start = (f32[16,320,128]{2,1,0:T(8,128)}, f32[16,320,128]{2,1,0:T(8,128)}, u32[]{:S(2)}, u32[]{:S(2)}) collective-permute-start(f32[16,320,128]{2,1,0:T(8,128)} %get-tuple-element.34), channel_id=1, source_target_pairs={{0,16},{16,0},{1,17},{17,1},{2,18},{18,2},{3,19},{19,3},{4,20},{20... | collective-permute-start | bytes 7864328 | tf_op jit(solution)/shard_map/sums/ppermute | solution.py:94
  10.1 1.4 copy-start
  11.5 4.5 %collective-permute-start.1 = (f32[16,256,128]{2,1,0:T(8,128)}, f32[16,256,128]{2,1,0:T(8,128)}, u32[]{:S(2)}, u32[]{:S(2)}) collective-permute-start(f32[16,256,128]{2,1,0:T(8,128)} %get-tuple-element.38), channel_id=1, source_target_pairs={{0,16},{16,0},{1,17},{17,1},{2,18},{18,2},{3,19},{19,3},{4,20},{20... | collective-permute-start | bytes 6291464 | tf_op jit(solution)/shard_map/sums/ppermute | solution.py:94
  16.0 1.6 copy-start.1
  20.5 29.3 %collective-permute-start.2 = (f32[4,576,128]{2,1,0:T(8,128)S(1)}, f32[4,576,128]{2,1,0:T(8,128)S(1)}, u32[]{:S(2)}, u32[]{:S(2)}) collective-permute-start(f32[4,576,128]{2,1,0:T(8,128)S(1)} %get-tuple-element.40), channel_id=1, source_target_pairs={{0,32},{4,36},{8,40},{12,44},{16,20},{20,24},{24,28},{28,16},{32,6... | collective-permute-start | bytes 3538952 | tf_op jit(solution)/shard_map/sums/ppermute | solution.py:105
  20.5 29.2 %collective-permute-start.3 = (f32[4,576,128]{2,1,0:T(8,128)S(1)}, f32[4,576,128]{2,1,0:T(8,128)S(1)}, u32[]{:S(2)}, u32[]{:S(2)}) collective-permute-start(f32[4,576,128]{2,1,0:T(8,128)S(1)} %get-tuple-element.41), channel_id=1, source_target_pairs={{0,64},{4,68},{8,72},{12,76},{16,24},{20,28},{24,16},{28,20},{32,9... | collective-permute-start | bytes 3538952 | tf_op jit(solution)/shard_map/sums/ppermute | solution.py:105
  22.7 27.6 %collective-permute-start.4 = (f32[4,576,128]{2,1,0:T(8,128)S(1)}, f32[4,576,128]{2,1,0:T(8,128)S(1)}, u32[]{:S(2)}, u32[]{:S(2)}) collective-permute-start(f32[4,576,128]{2,1,0:T(8,128)S(1)} %get-tuple-element.42), channel_id=1, source_target_pairs={{0,96},{4,100},{8,104},{12,108},{16,28},{20,16},{24,20},{28,24},{3... | collective-permute-start | bytes 3538952 | tf_op jit(solution)/shard_map/sums/ppermute | solution.py:105
  51.1 10.3 %collective-permute-start.5 = (f32[576,128]{1,0:T(8,128)S(1)}, f32[576,128]{1,0:T(8,128)S(1)}, u32[]{:S(2)}, u32[]{:S(2)}) collective-permute-start(f32[576,128]{1,0:T(8,128)S(1)} %get-tuple-element.44), channel_id=1, source_target_pairs={{0,4},{4,8},{8,12},{12,0},{16,48},{20,52},{24,56},{28,60},{32,36},... | collective-permute-start | bytes 884744 | tf_op jit(solution)/shard_map/sums/ppermute | solution.py:105
  51.2 10.2 %collective-permute-start.6 = (f32[576,128]{1,0:T(8,128)S(1)}, f32[576,128]{1,0:T(8,128)S(1)}, u32[]{:S(2)}, u32[]{:S(2)}) collective-permute-start(f32[576,128]{1,0:T(8,128)S(1)} %get-tuple-element.45), channel_id=1, source_target_pairs={{0,8},{4,12},{8,0},{12,4},{16,80},{20,84},{24,88},{28,92},{32,40},... | collective-permute-start | bytes 884744 | tf_op jit(solution)/shard_map/sums/ppermute | solution.py:105
  53.5 8.6 %collective-permute-start.7 = (f32[576,128]{1,0:T(8,128)S(1)}, f32[576,128]{1,0:T(8,128)S(1)}, u32[]{:S(2)}, u32[]{:S(2)}) collective-permute-start(f32[576,128]{1,0:T(8,128)S(1)} %get-tuple-element.46), channel_id=1, source_target_pairs={{0,12},{4,0},{8,4},{12,8},{16,112},{20,116},{24,120},{28,124},{32,... | collective-permute-start | bytes 884744 | tf_op jit(solution)/shard_map/sums/ppermute | solution.py:105
  62.7 5.2 %collective-permute-start.8 = (f32[2,72,128]{2,1,0:T(8,128)S(1)}, f32[2,72,128]{2,1,0:T(8,128)S(1)}, u32[]{:S(2)}, u32[]{:S(2)}) collective-permute-start(f32[2,72,128]{2,1,0:T(8,128)S(1)} %get-tuple-element.48), channel_id=1, source_target_pairs={{0,1},{1,2},{2,3},{3,0},{4,5},{5,6},{6,7},{7,4},{8,9},{9,10},{10,1... | collective-permute-start | bytes 221192 | tf_op jit(solution)/shard_map/sums/ppermute | solution.py:105
  63.4 6.1 %collective-permute-start.9 = (f32[2,72,128]{2,1,0:T(8,128)S(1)}, f32[2,72,128]{2,1,0:T(8,128)S(1)}, u32[]{:S(2)}, u32[]{:S(2)}) collective-permute-start(f32[2,72,128]{2,1,0:T(8,128)S(1)} %get-tuple-element.49), channel_id=1, source_target_pairs={{0,2},{1,3},{2,0},{3,1},{4,6},{5,7},{6,4},{7,5},{8,10},{9,11},{10,... | collective-permute-start | bytes 221192 | tf_op jit(solution)/shard_map/sums/ppermute | solution.py:105
  66.3 4.3 %collective-permute-start.10 = (f32[2,72,128]{2,1,0:T(8,128)S(1)}, f32[2,72,128]{2,1,0:T(8,128)S(1)}, u32[]{:S(2)}, u32[]{:S(2)}) collective-permute-start(f32[2,72,128]{2,1,0:T(8,128)S(1)} %get-tuple-element.50), channel_id=1, source_target_pairs={{0,3},{1,0},{2,1},{3,2},{4,7},{5,4},{6,5},{7,6},{8,11},{9,8},{10,9... | collective-permute-start | bytes 221192 | tf_op jit(solution)/shard_map/sums/ppermute | solution.py:105
  70.7 7.3 %collective-permute-start.11 = (f32[2,72,128]{2,1,0:T(8,128)S(1)}, f32[2,72,128]{2,1,0:T(8,128)S(1)}, u32[]{:S(2)}, u32[]{:S(2)}) collective-permute-start(f32[2,72,128]{2,1,0:T(8,128)S(1)} %sums.13.a), channel_id=1, source_target_pairs={{0,128},{128,0},{1,129},{129,1},{2,130},{130,2},{3,131},{131,3},{4... | collective-permute-start | bytes 221192 | tf_op jit(solution)/shard_map/sums/ppermute | solution.py:105
  78.0 5.2 %collective-permute-start.14 = (f32[2,72,128]{2,1,0:T(8,128)S(1)}, f32[2,72,128]{2,1,0:T(8,128)S(1)}, u32[]{:S(2)}, u32[]{:S(2)}) collective-permute-start(f32[2,72,128]{2,1,0:T(8,128)S(1)} %sums.14.a), channel_id=1, source_target_pairs={{0,3},{1,0},{2,1},{3,2},{4,7},{5,4},{6,5},{7,6},{8,11},{9,8},{10,9... | collective-permute-start | bytes 221192 | tf_op jit(solution)/shard_map/sums/ppermute | solution.py:105
  80.2 5.7 %collective-permute-start.13 = (f32[2,72,128]{2,1,0:T(8,128)S(1)}, f32[2,72,128]{2,1,0:T(8,128)S(1)}, u32[]{:S(2)}, u32[]{:S(2)}) collective-permute-start(f32[2,72,128]{2,1,0:T(8,128)S(1)} %sums.14.a), channel_id=1, source_target_pairs={{0,2},{1,3},{2,0},{3,1},{4,6},{5,7},{6,4},{7,5},{8,10},{9,11},{10,... | collective-permute-start | bytes 221192 | tf_op jit(solution)/shard_map/sums/ppermute | solution.py:105
  81.7 5.7 %collective-permute-start.12 = (f32[2,72,128]{2,1,0:T(8,128)S(1)}, f32[2,72,128]{2,1,0:T(8,128)S(1)}, u32[]{:S(2)}, u32[]{:S(2)}) collective-permute-start(f32[2,72,128]{2,1,0:T(8,128)S(1)} %sums.14.a), channel_id=1, source_target_pairs={{0,1},{1,2},{2,3},{3,0},{4,5},{5,6},{6,7},{7,4},{8,9},{9,10},{10,1... | collective-permute-start | bytes 221192 | tf_op jit(solution)/shard_map/sums/ppermute | solution.py:105
  89.5 1.4 copy-start.2
  90.9 17.0 %all-to-all-start = ((f32[16,120,128]{2,1,0:T(8,128)}), f32[16,120,128]{2,1,0:T(8,128)S(1)}, u32[]{:S(2)}, u32[]{:S(2)}) async-start(f32[16,120,128]{2,1,0:T(8,128)} %get-tuple-element.52), calls=%async_computation | async-start | bytes 1966080 | tf_op jit(solution)/shard_map/back/all_to_all | solution.py:90
  107.9 1.0 copy-start.10
  108.8 30.1 %all-to-all-start.1 = ((f32[16,200,128]{2,1,0:T(8,128)}), f32[16,200,128]{2,1,0:T(8,128)S(1)}, u32[]{:S(2)}, u32[]{:S(2)}) async-start(f32[16,200,128]{2,1,0:T(8,128)} %get-tuple-element.53), calls=%async_computation.1 | async-start | bytes 3276800 | tf_op jit(solution)/shard_map/back/all_to_all | solution.py:90
  138.9 1.2 copy-start.9
  140.2 41.0 %all-to-all-start.2 = ((f32[16,256,128]{2,1,0:T(8,128)}), f32[16,256,128]{2,1,0:T(8,128)S(1)}, u32[]{:S(2)}, u32[]{:S(2)}) async-start(f32[16,256,128]{2,1,0:T(8,128)} %copy-done.2), calls=%async_computation.2 | async-start | bytes 4194304 | tf_op jit(solution)/shard_map/back/all_to_all | solution.py:90
  173.5 7.7 %collective-permute-start.15 = (f32[8,1024]{1,0:T(8,128)}, f32[8,1024]{1,0:T(8,128)S(1)}, u32[]{:S(2)}, u32[]{:S(2)}) collective-permute-start(f32[8,1024]{1,0:T(8,128)} %get-tuple-element.57.z_own), channel_id=1, source_target_pairs={{0,16},{16,0},{1,17},{17,1},{2,18},{18,2},{3,19},{19,3},{4,20},{20... | collective-permute-start | bytes 98312 | tf_op jit(solution)/shard_map/ppermute | solution.py:94
  181.2 0.8 copy-start.4
  182.9 1.5 copy-start.3
  182.9 1.5 collective-permute-start.16
  192.5 1.2 collective-permute-start.17
  (1 other events, 0.6 us)
